TPU v7x, 32 devices: a whole 2x2x4 slice. The times are simulated.
32 devices in a mesh: dp: 8 (over z, y), tp: 4 (over x, core).
Axes of the slice: x: 2, y: 2, z: 4, core: 2. Of those that a mesh axis runs over, the one named last changes fastest.
Arguments:
- frames: bfloat16 [24, 1024, 512], P('dp', 'tp'), may hold values from -6 to 6
- cotangent: bfloat16 [24, 1024, 512], P('dp', 'tp'), may hold values from -6 to 6
- lengths: int32 [24], P('dp'), may hold values from 64 to 1024, as said below
- conv_weight: float32 [512, 7], P(('dp', 'tp')), may hold values from -2 to 2
- conv_bias: float32 [512], P(('dp', 'tp')), may hold values from -0.6 to 0.6
- norm_gain: float32 [512], P(('dp', 'tp')), may hold values from 0.5 to 1.5
- norm_bias: float32 [512], P(('dp', 'tp')), may hold values from -0.6 to 0.6
- up_weight: float32 [512, 1536], P('dp', 'tp'), may hold values from -0.25 to 0.25
- up_bias: float32 [1536], P(('dp', 'tp')), may hold values from -0.6 to 0.6
- down_weight: float32 [512, 1536], P('dp', 'tp'), may hold values from -0.15625 to 0.15625
- down_bias: float32 [512], P(('dp', 'tp')), may hold values from -0.6 to 0.6
- layer_scale: float32 [512], P(('dp', 'tp')), may hold values from 0.25 to 1.75
- moment_conv_weight: float32 [512, 7], P(('dp', 'tp')), may hold values from -36 to 36
- moment_conv_bias: float32 [512], P(('dp', 'tp')), may hold values from -36 to 36
- moment_norm_gain: float32 [512], P(('dp', 'tp')), may hold values from -36 to 36
- moment_norm_bias: float32 [512], P(('dp', 'tp')), may hold values from -36 to 36
- moment_up_weight: float32 [512, 1536], P('dp', 'tp'), may hold values from -36 to 36
- moment_up_bias: float32 [1536], P(('dp', 'tp')), may hold values from -36 to 36
- moment_down_weight: float32 [512, 1536], P('dp', 'tp'), may hold values from -36 to 36
- moment_down_bias: float32 [512], P(('dp', 'tp')), may hold values from -36 to 36
- moment_layer_scale: float32 [512], P(('dp', 'tp')), may hold values from -36 to 36
- square_conv_weight: float32 [512, 7], P(('dp', 'tp')), may hold values from 1 to 9
- square_conv_bias: float32 [512], P(('dp', 'tp')), may hold values from 1 to 9
- square_norm_gain: float32 [512], P(('dp', 'tp')), may hold values from 1 to 9
- square_norm_bias: float32 [512], P(('dp', 'tp')), may hold values from 1 to 9
- square_up_weight: float32 [512, 1536], P('dp', 'tp'), may hold values from 1 to 9
- square_up_bias: float32 [1536], P(('dp', 'tp')), may hold values from 1 to 9
- square_down_weight: float32 [512, 1536], P('dp', 'tp'), may hold values from 1 to 9
- square_down_bias: float32 [512], P(('dp', 'tp')), may hold values from 1 to 9
- square_layer_scale: float32 [512], P(('dp', 'tp')), may hold values from 1 to 9
Outputs:
- output: float32 [24, 1024, 512], P('dp', 'tp')
- input_grad: float32 [24, 1024, 512], P('dp', 'tp')
- grad_conv_weight: float32 [512, 7], P(('dp', 'tp'))
- next_conv_weight: float32 [512, 7], P(('dp', 'tp'))
- next_moment_conv_weight: float32 [512, 7], P(('dp', 'tp'))
- next_square_conv_weight: float32 [512, 7], P(('dp', 'tp'))
- grad_conv_bias: float32 [512], P(('dp', 'tp'))
- next_conv_bias: float32 [512], P(('dp', 'tp'))
- next_moment_conv_bias: float32 [512], P(('dp', 'tp'))
- next_square_conv_bias: float32 [512], P(('dp', 'tp'))
- grad_norm_gain: float32 [512], P(('dp', 'tp'))
- update_norm_gain: float32 [512], P(('dp', 'tp'))
- next_moment_norm_gain: float32 [512], P(('dp', 'tp'))
- next_square_norm_gain: float32 [512], P(('dp', 'tp'))
- grad_norm_bias: float32 [512], P(('dp', 'tp'))
- next_norm_bias: float32 [512], P(('dp', 'tp'))
- next_moment_norm_bias: float32 [512], P(('dp', 'tp'))
- next_square_norm_bias: float32 [512], P(('dp', 'tp'))
- grad_up_weight: float32 [512, 1536], P('dp', 'tp')
- next_up_weight: float32 [512, 1536], P('dp', 'tp')
- next_moment_up_weight: float32 [512, 1536], P('dp', 'tp')
- next_square_up_weight: float32 [512, 1536], P('dp', 'tp')
- grad_up_bias: float32 [1536], P(('dp', 'tp'))
- next_up_bias: float32 [1536], P(('dp', 'tp'))
- next_moment_up_bias: float32 [1536], P(('dp', 'tp'))
- next_square_up_bias: float32 [1536], P(('dp', 'tp'))
- grad_down_weight: float32 [512, 1536], P('dp', 'tp')
- next_down_weight: float32 [512, 1536], P('dp', 'tp')
- next_moment_down_weight: float32 [512, 1536], P('dp', 'tp')
- next_square_down_weight: float32 [512, 1536], P('dp', 'tp')
- grad_down_bias: float32 [512], P(('dp', 'tp'))
- next_down_bias: float32 [512], P(('dp', 'tp'))
- next_moment_down_bias: float32 [512], P(('dp', 'tp'))
- next_square_down_bias: float32 [512], P(('dp', 'tp'))
- grad_layer_scale: float32 [512], P(('dp', 'tp'))
- update_layer_scale: float32 [512], P(('dp', 'tp'))
- next_moment_layer_scale: float32 [512], P(('dp', 'tp'))
- next_square_layer_scale: float32 [512], P(('dp', 'tp'))
Inputs may be any that keep to these rules, and one draw needn't show every extreme that they name: `lengths`: each slot's true frame count lies between 64 and 1024; in every draw at least one slot holds 1024 true frames.
All inputs are finite; a program needn't handle non-finite values.
Results may differ from a plain program's by a relative error of at most 0.0079.
Values may be sent and summed in bfloat16 or wider, within the bound.
No kernel may reach another device: no remote copies, remote signals or barrier semaphores. Data moves between devices by JAX's collectives and lax.ppermute only.
A program may use at most 128 MiB of HBM per device.

v0:
```python
import jax
import jax.numpy as jnp
from jax import lax
from jax.sharding import PartitionSpec as P

STEP = 4


norm_eps = 1e-06
learn_rate = 0.05
first_decay = 0.9
second_decay = 0.999
adam_eps = 1e-08
weight_decay = 0.1
update_flags = (False, False, True, False, False, False, False, False, True)


def conv_apply(padded, tap_weights, conv_shift, frames_out):
    result = conv_shift + padded[:, 0:frames_out, :] * tap_weights[:, 0]
    for offset in range(1, tap_weights.shape[1]):
        result = result + padded[:, offset : offset + frames_out, :] * tap_weights[:, offset]
    return result


def conv_back(grad_padded, tap_weights, frames_out):
    edge_start = tap_weights.shape[1] - 1
    result = grad_padded[:, edge_start : edge_start + frames_out, :] * tap_weights[:, 0]
    for offset in range(1, tap_weights.shape[1]):
        begin = edge_start - offset
        result = result + grad_padded[:, begin : begin + frames_out, :] * tap_weights[:, offset]
    return result


def tap_grads(conv_grad, padded):
    frames_out = conv_grad.shape[1]
    tap_total = padded.shape[1] - frames_out + 1
    columns = [
        jnp.sum(conv_grad * padded[:, offset : offset + frames_out, :], axis=(0, 1))
        for offset in range(tap_total)
    ]
    return jnp.stack(columns, axis=1)


def norm_forward(conv_out, gain_vector, shift_vector):
    centred = conv_out - jnp.mean(conv_out, axis=-1, keepdims=True)
    inverse = lax.rsqrt(jnp.mean(centred * centred, axis=-1, keepdims=True) + norm_eps)
    unit_norm = centred * inverse
    return (unit_norm * gain_vector + shift_vector, unit_norm, inverse)


def norm_backward(normed_grad, unit_norm, inverse, gain_vector):
    scaled = normed_grad * gain_vector
    centred_grad = scaled - jnp.mean(scaled, axis=-1, keepdims=True)
    return inverse * (
        centred_grad - unit_norm * jnp.mean(scaled * unit_norm, axis=-1, keepdims=True)
    )


def exact_gelu(values):
    return jax.nn.gelu(values, approximate=False)


def adam_step(weights_now, gradient, moment, square, step_number):
    next_moment = first_decay * moment + (1.0 - first_decay) * gradient
    next_square = second_decay * square + (1.0 - second_decay) * gradient * gradient
    first_fix = 1.0 - jnp.power(jnp.float32(first_decay), step_number)
    second_fix = 1.0 - jnp.power(jnp.float32(second_decay), step_number)
    step_ratio = next_moment / first_fix / (jnp.sqrt(next_square / second_fix) + adam_eps)
    update = -(learn_rate * (step_ratio + weight_decay * weights_now))
    return (weights_now + update, next_moment, next_square, update)


def per_device(
    frames,
    cotangent,
    lengths,
    conv_weight,
    conv_bias,
    norm_gain,
    norm_bias,
    up_weight,
    up_bias,
    down_weight,
    down_bias,
    layer_scale,
    moment_conv_weight,
    moment_conv_bias,
    moment_norm_gain,
    moment_norm_bias,
    moment_up_weight,
    moment_up_bias,
    moment_down_weight,
    moment_down_bias,
    moment_layer_scale,
    square_conv_weight,
    square_conv_bias,
    square_norm_gain,
    square_norm_bias,
    square_up_weight,
    square_up_bias,
    square_down_weight,
    square_down_bias,
    square_layer_scale,
):
    tp_count = lax.axis_size("tp")
    device_rank = lax.axis_index("tp")
    slot_count, quarter_len, feature_width = frames.shape
    slot_len = quarter_len * tp_count
    frame_start = device_rank * quarter_len
    up_rows, down_rows = (
        lax.all_gather(up_weight.astype(jnp.bfloat16), "dp", axis=0, tiled=True),
        lax.all_gather(down_weight.astype(jnp.bfloat16), "dp", axis=0, tiled=True),
    )
    tap_weights, conv_shift, gain_vector, shift_vector, up_shift, down_shift, scale_vector = (
        lax.all_gather(conv_weight, ("dp", "tp"), axis=0, tiled=True),
        lax.all_gather(conv_bias, ("dp", "tp"), axis=0, tiled=True),
        lax.all_gather(norm_gain, ("dp", "tp"), axis=0, tiled=True),
        lax.all_gather(norm_bias, ("dp", "tp"), axis=0, tiled=True),
        lax.all_gather(up_bias, ("dp", "tp"), axis=0, tiled=True),
        lax.all_gather(down_bias, ("dp", "tp"), axis=0, tiled=True),
        lax.all_gather(layer_scale, ("dp", "tp"), axis=0, tiled=True),
    )
    kernel_half = tap_weights.shape[1] // 2
    hidden_width = up_shift.shape[0]
    own_width = up_rows.shape[1]
    whole_frames, whole_cot = (
        lax.all_gather(frames, "tp", axis=1, tiled=True),
        lax.all_gather(cotangent, "tp", axis=1, tiled=True),
    )
    positions = lax.broadcasted_iota(jnp.int32, (slot_count, slot_len), 1)
    frame_mask = (positions < lengths[:, None]).astype(jnp.float32)[:, :, None]
    signal = whole_frames.astype(jnp.float32)
    shifted = signal * frame_mask
    padded = jnp.pad(shifted, ((0, 0), (kernel_half, kernel_half), (0, 0)))
    conv_out = conv_apply(padded, tap_weights, conv_shift, slot_len)
    normed, unit_norm, inverse = norm_forward(conv_out, gain_vector, shift_vector)
    normed_low = normed.astype(jnp.bfloat16)
    own_shift = lax.dynamic_slice_in_dim(up_shift, device_rank * own_width, own_width)
    hidden = (
        jnp.einsum("slc,ch->slh", normed_low, up_rows, preferred_element_type=jnp.float32)
        + own_shift
    )
    active, gelu_pull = jax.vjp(exact_gelu, hidden)
    active_low = active.astype(jnp.bfloat16)
    partial_out = jnp.einsum(
        "slh,ch->slc", active_low, down_rows, preferred_element_type=jnp.float32
    )
    branch = lax.psum(partial_out, "tp") + down_shift
    output_full = (signal + scale_vector * branch) * frame_mask
    back_grad = whole_cot.astype(jnp.float32) * frame_mask
    branch_grad = (back_grad * scale_vector).astype(jnp.bfloat16)
    active_grad = jnp.einsum(
        "slc,ch->slh", branch_grad, down_rows, preferred_element_type=jnp.float32
    )
    hidden_grad = gelu_pull(active_grad)[0].astype(jnp.bfloat16)
    normed_part = jnp.einsum(
        "slh,ch->slc", hidden_grad, up_rows, preferred_element_type=jnp.float32
    )
    normed_grad = lax.psum(normed_part, "tp")
    conv_grad = norm_backward(normed_grad, unit_norm, inverse, gain_vector)
    grad_padded = jnp.pad(conv_grad, ((0, 0), (kernel_half, kernel_half), (0, 0)))
    input_full = back_grad + frame_mask * conv_back(grad_padded, tap_weights, slot_len)
    grad_up = jnp.einsum("slc,slh->ch", normed_low, hidden_grad, preferred_element_type=jnp.float32)
    grad_down = jnp.einsum(
        "slc,slh->ch", branch_grad, active_low, preferred_element_type=jnp.float32
    )
    own_up_grad = jnp.sum(hidden_grad.astype(jnp.float32), axis=(0, 1))
    grad_up_shift = lax.dynamic_update_slice_in_dim(
        jnp.zeros((hidden_width,), jnp.float32), own_up_grad, device_rank * own_width, 0
    )

    def own_frames(values):
        return lax.dynamic_slice_in_dim(values, frame_start, quarter_len, 1)

    conv_grad_own = own_frames(conv_grad)
    normed_grad_own = own_frames(normed_grad)
    unit_own = own_frames(unit_norm)
    back_own = own_frames(back_grad)
    branch_own = own_frames(branch)
    branch_grad_own = own_frames(branch_grad)
    taps_grad = tap_grads(
        conv_grad_own,
        lax.dynamic_slice_in_dim(padded, frame_start, quarter_len + 2 * kernel_half, 1),
    )
    output_own = own_frames(output_full)
    input_own = own_frames(input_full)
    grad_scale = jnp.sum(back_own * branch_own, axis=(0, 1))
    grad_down_shift = jnp.sum(branch_grad_own.astype(jnp.float32), axis=(0, 1))
    grad_gain = jnp.sum(normed_grad_own * unit_own, axis=(0, 1))
    grad_shift = jnp.sum(normed_grad_own, axis=(0, 1))
    grad_conv_shift = jnp.sum(conv_grad_own, axis=(0, 1))
    up_share, down_share = (
        lax.psum_scatter(grad_up, "dp", scatter_dimension=0, tiled=True),
        lax.psum_scatter(grad_down, "dp", scatter_dimension=0, tiled=True),
    )
    share_taps, share_conv, share_gain, share_shift, share_up, share_down, share_scale = (
        lax.psum_scatter(taps_grad, ("dp", "tp"), scatter_dimension=0, tiled=True),
        lax.psum_scatter(grad_conv_shift, ("dp", "tp"), scatter_dimension=0, tiled=True),
        lax.psum_scatter(grad_gain, ("dp", "tp"), scatter_dimension=0, tiled=True),
        lax.psum_scatter(grad_shift, ("dp", "tp"), scatter_dimension=0, tiled=True),
        lax.psum_scatter(grad_up_shift, ("dp", "tp"), scatter_dimension=0, tiled=True),
        lax.psum_scatter(grad_down_shift, ("dp", "tp"), scatter_dimension=0, tiled=True),
        lax.psum_scatter(grad_scale, ("dp", "tp"), scatter_dimension=0, tiled=True),
    )
    step_number = jnp.float32(STEP)
    params = (
        conv_weight,
        conv_bias,
        norm_gain,
        norm_bias,
        up_weight,
        up_bias,
        down_weight,
        down_bias,
        layer_scale,
    )
    gradients = (
        share_taps,
        share_conv,
        share_gain,
        share_shift,
        up_share,
        share_up,
        down_share,
        share_down,
        share_scale,
    )
    moments = (
        moment_conv_weight,
        moment_conv_bias,
        moment_norm_gain,
        moment_norm_bias,
        moment_up_weight,
        moment_up_bias,
        moment_down_weight,
        moment_down_bias,
        moment_layer_scale,
    )
    squares = (
        square_conv_weight,
        square_conv_bias,
        square_norm_gain,
        square_norm_bias,
        square_up_weight,
        square_up_bias,
        square_down_weight,
        square_down_bias,
        square_layer_scale,
    )
    flat = [output_own, input_own]
    for weights_now, gradient, moment, square, use_update in zip(
        params, gradients, moments, squares, update_flags
    ):
        next_weights, next_moment, next_square, update = adam_step(
            weights_now, gradient, moment, square, step_number
        )
        shown = update if use_update else next_weights
        flat = flat + [gradient, shown, next_moment, next_square]
    return (
        flat[0],
        flat[1],
        flat[2],
        flat[3],
        flat[4],
        flat[5],
        flat[6],
        flat[7],
        flat[8],
        flat[9],
        flat[10],
        flat[11],
        flat[12],
        flat[13],
        flat[14],
        flat[15],
        flat[16],
        flat[17],
        flat[18],
        flat[19],
        flat[20],
        flat[21],
        flat[22],
        flat[23],
        flat[24],
        flat[25],
        flat[26],
        flat[27],
        flat[28],
        flat[29],
        flat[30],
        flat[31],
        flat[32],
        flat[33],
        flat[34],
        flat[35],
        flat[36],
        flat[37],
    )


def solution(mesh):
    return jax.shard_map(
        per_device,
        mesh=mesh,
        in_specs=(
            P("dp", "tp", None),
            P("dp", "tp", None),
            P("dp"),
            P(("dp", "tp"), None),
            P(("dp", "tp")),
            P(("dp", "tp")),
            P(("dp", "tp")),
            P("dp", "tp"),
            P(("dp", "tp")),
            P("dp", "tp"),
            P(("dp", "tp")),
            P(("dp", "tp")),
            P(("dp", "tp"), None),
            P(("dp", "tp")),
            P(("dp", "tp")),
            P(("dp", "tp")),
            P("dp", "tp"),
            P(("dp", "tp")),
            P("dp", "tp"),
            P(("dp", "tp")),
            P(("dp", "tp")),
            P(("dp", "tp"), None),
            P(("dp", "tp")),
            P(("dp", "tp")),
            P(("dp", "tp")),
            P("dp", "tp"),
            P(("dp", "tp")),
            P("dp", "tp"),
            P(("dp", "tp")),
            P(("dp", "tp")),
        ),
        out_specs=(
            P("dp", "tp", None),
            P("dp", "tp", None),
            P(("dp", "tp"), None),
            P(("dp", "tp"), None),
            P(("dp", "tp"), None),
            P(("dp", "tp"), None),
            P(("dp", "tp")),
            P(("dp", "tp")),
            P(("dp", "tp")),
            P(("dp", "tp")),
            P(("dp", "tp")),
            P(("dp", "tp")),
            P(("dp", "tp")),
            P(("dp", "tp")),
            P(("dp", "tp")),
            P(("dp", "tp")),
            P(("dp", "tp")),
            P(("dp", "tp")),
            P("dp", "tp"),
            P("dp", "tp"),
            P("dp", "tp"),
            P("dp", "tp"),
            P(("dp", "tp")),
            P(("dp", "tp")),
            P(("dp", "tp")),
            P(("dp", "tp")),
            P("dp", "tp"),
            P("dp", "tp"),
            P("dp", "tp"),
            P("dp", "tp"),
            P(("dp", "tp")),
            P(("dp", "tp")),
            P(("dp", "tp")),
            P(("dp", "tp")),
            P(("dp", "tp")),
            P(("dp", "tp")),
            P(("dp", "tp")),
            P(("dp", "tp")),
        ),
        check_vma=False,
    )
```

profile of v0, /device:TPU:0, one launch (start us, length us, event | category | flops | bytes accessed | tf_op | source)
XLA Modules:
  0.0 722.1 jit_solution(14380153058658341902)
XLA Ops:
  9.7 44.2 %all-gather = f32[32,16,7]{1,2,0:T(8,128)S(1)} all-gather(f32[1,16,7]{1,2,0:T(8,128)} %bitcast.62), channel_id=1, replica_groups=mesh['dp'=8,'tp'=4] {'dp','tp'}, dimensions={0}, use_global_device_ids=true | all-gather | bytes 14784 | tf_op jit(solution)/shard_map/all_gather | solution.py:115
  59.1 37.4 %all-reduce.15 = (f32[512]{0:T(512)S(1)}, f32[512]{0:T(512)S(1)}, f32[512]{0:T(512)S(1)}, f32[1536]{0:T(1024)S(1)}, f32[512]{0:T(512)S(1)}, /*index=5*/f32[512]{0:T(512)S(1)}) all-reduce(f32[512]{0:T(512)S(1)} %dynamic-update-slice.1, f32[512]{0:T(512)S(1)} %dynamic-update-slice.3, ...), channel_id=1, replica_groups=mesh['dp'=8,'tp'=4] {'dp','tp'}, use_global_device_ids=true, to_apply=%add.3 | all-reduce | flops 4096 | bytes 32768
  96.5 31.3 %all_gather.39 = bf16[512,384]{1,0:T(8,128)(2,1)S(1)} all-gather(bf16[64,384]{1,0:T(8,128)(2,1)S(1)} %convert_element_type.43), channel_id=1, replica_groups=mesh['dp'=8,'tp'=4] {'dp'}, dimensions={0}, use_global_device_ids=true | all-gather | bytes 442368 | tf_op jit(solution)/shard_map/all_gather | solution.py:111
  128.6 5.2 convert_multiply_fusion
  133.8 6.0 fusion.59
  139.9 1.1 multiply_reduce_fusion.1
  142.4 3.1 fusion.31
  145.6 11.7 %multiply_convert_fusion.1 = (bf16[3,1024,384]{2,1,0:T(8,128)(2,1)S(1)}, f32[3,1024,384]{2,1,0:T(8,128)}) fusion(f32[3,1024,384]{2,1,0:T(8,128)S(1)} %get-tuple-element.123, f32[384]{0:T(512)S(1)} %dynamic_slice.30, u8[1024,384]{1,0:T(8,128)(4,1)S(1)} %get-tuple-element.51, u8[1024,384]{1,0:T(8,128)(4,1)S(1)} %get-tuple-element.50), kind=kLoop, calls=%fused_computation.35 | loop fusion | flops 83755008 | bytes 12584448 | tf_op jit(solution)/shard_map/convert_element_type | solution.py:144
  157.4 2.7 convolution_bitcast_fusion
  160.3 63.0 %reduce-scatter.8.cloned.1.call-done = f32[64,384]{1,0:T(8,128)} async-done(((f32[512,384]{1,0:T(8,128)}), f32[64,384]{1,0:T(8,128)}) %reduce-scatter.8.cloned.1.call-update) | async-done | bytes 98320 | tf_op jit(solution)/shard_map/reduce_scatter | solution.py:194
  223.3 1.8 negate_add_fusion
  225.1 31.1 %all_gather.41 = bf16[512,384]{1,0:T(8,128)(2,1)S(1)} all-gather(bf16[64,384]{1,0:T(8,128)(2,1)S(1)} %get-tuple-element.114), channel_id=1, replica_groups=mesh['dp'=8,'tp'=4] {'dp'}, dimensions={0}, use_global_device_ids=true | all-gather | bytes 442368 | tf_op jit(solution)/shard_map/all_gather | solution.py:112
  256.2 8.1 %convert_reduce_fusion = (f32[384]{0:T(512)S(1)}, bf16[3,1024,384]{2,1,0:T(8,128)(2,1)S(1)}) fusion(f32[3,1024,384]{2,1,0:T(8,128)} %get-tuple-element.102, bf16[3,1024,512]{2,1,0:T(8,128)(2,1)} %copy-done.4, bf16[512,384]{1,0:T(8,128)(2,1)S(1)} %all_gather.41, f32[3,1024,384]{2,1,0:T(8,128)} %copy-done.7, f32[384]{0:T(512)S(1)} %dynamic_slice.30), kind=kOutput, calls=%fused_computation.33 | convolution fusion | flops 1228013184 | bytes 15338496 | tf_op jit(solution)/shard_map/slc,ch->slh/dot_general | solution.py:152
  264.3 1.4 copy-done.5
  265.7 2.7 convolution_bitcast_fusion.1
  268.5 6.1 fusion.36
  274.6 4.4 fusion.34
  279.4 1.6 copy-done.6
  280.9 3.6 convert_element_type.40
  284.5 1.3 convert_reduce_fusion.1
  286.1 44.5 %reduce-scatter.6.cloned.1.call-done = f32[64,384]{1,0:T(8,128)} async-done(((f32[512,384]{1,0:T(8,128)}), f32[64,384]{1,0:T(8,128)}) %reduce-scatter.6.cloned.1.call-update) | async-done | bytes 98320 | tf_op jit(solution)/shard_map/reduce_scatter | solution.py:193
  330.7 1.6 negate_add_fusion.1
  332.3 220.5 %all-reduce.19.cloned.1.call-done = (f32[3,1024,512]{2,1,0:T(8,128)}, f32[3,1024,512]{2,1,0:T(8,128)}) async-done(((f32[3,1024,512]{2,1,0:T(8,128)}, f32[3,1024,512]{2,1,0:T(8,128)}), (f32[3,1024,512]{2,1,0:T(8,128)}, f32[3,1024,512]{2,1,0:T(8,128)})) %all-reduce.19.cloned.1.call-update) | async-done | bytes 12582928 | tf_op jit(solution)/shard_map/psum | solution.py:148
  552.8 2.3 dynamic-slice_reduce_fusion
  555.2 6.1 multiply_reduce_fusion.2
  562.4 4.0 broadcast_multiply_fusion
  566.4 9.2 %multiply_add_fusion = (f32[3,1024,512]{2,1,0:T(8,128)}, f32[3,1024,512]{2,1,0:T(8,128)}, f32[3,1024,512]{2,1,0:T(8,128)}, f32[3,1024,512]{2,1,0:T(8,128)}) fusion(f32[3,1024,512]{2,1,0:T(8,128)S(1)} %get-tuple-element.100, f32[512]{0:T(512)S(1)} %bitcast.57, f32[512]{0:T(512)S(1)} %bitcast.59, f32[512]{0:T(512)S(1)} %bitcast.55), kind=kLoop, calls=%fused_computation.1 | loop fusion | flops 7864320 | bytes 31463424 | tf_op jit(solution)/shard_map/add | solution.py:30
  575.5 1.8 fusion.17
  578.2 3.6 broadcast_add_fusion
  582.1 6.8 multiply_reduce_fusion.3
  588.8 39.8 %all-reduce.14 = (f32[512]{0:T(512)S(1)}, f32[512]{0:T(512)S(1)}, f32[512]{0:T(512)S(1)}, f32[1536]{0:T(1024)S(1)}, f32[512]{0:T(512)S(1)}, /*index=5*/f32[512]{0:T(512)S(1)}) all-reduce(f32[512]{0:T(512)S(1)} %get-tuple-element.49, f32[512]{0:T(512)S(1)} %get-tuple-element.48, ...), channel_id=3, replica_groups=mesh['dp'=8,'tp'=4] {'dp','tp'}, use_global_device_ids=true, to_apply=%region_15.16.clone | all-reduce | flops 4096 | bytes 32768
  632.3 81.5 %reduce-scatter.10.cloned.1.call-done = f32[16,7]{1,0:T(8,128)} async-done(((f32[512,7]{1,0:T(8,128)}), f32[16,7]{1,0:T(8,128)}) %reduce-scatter.10.cloned.1.call-update) | async-done | bytes 464
  (134 shorter events, 18.0 us)
Async XLA Ops:
  7.2 121.4 %all-gather.4.cloned.1.call-start = ((), (), s32[]{:S(2)}) async-start(), calls=%async_computation.3 | async-start | bytes 3932160 | tf_op jit(solution)/shard_map/all_gather | solution.py:127
  7.9 120.7 %all-gather.6.cloned.1.call-start = ((), (), s32[]{:S(2)}) async-start(), calls=%async_computation.4 | async-start | bytes 3932160 | tf_op jit(solution)/shard_map/all_gather | solution.py:128
  8.7 214.6 %reduce-scatter.8.cloned.1.call-start = ((), (), s32[]{:S(2)}) async-start(), calls=%async_computation.6 | async-start | bytes 884736 | tf_op jit(solution)/shard_map/reduce_scatter | solution.py:194
  157.3 66.0 %copy-start.9 = (f32[64,384]{1,0:T(8,128)S(1)}, f32[64,384]{1,0:T(8,128)}, u32[]{:S(2)}) copy-start(f32[64,384]{1,0:T(8,128)} %param.39) | copy-start | bytes 294916
  157.3 66.0 %copy-start.10 = (f32[64,384]{1,0:T(8,128)S(1)}, f32[64,384]{1,0:T(8,128)}, u32[]{:S(2)}) copy-start(f32[64,384]{1,0:T(8,128)} %param.57) | copy-start | bytes 294916
  157.3 66.0 %copy-start.11 = (f32[64,384]{1,0:T(8,128)S(1)}, f32[64,384]{1,0:T(8,128)}, u32[]{:S(2)}) copy-start(f32[64,384]{1,0:T(8,128)} %param.48) | copy-start | bytes 294916
  160.1 170.5 %reduce-scatter.6.cloned.1.call-start = ((), (), s32[]{:S(2)}) async-start(), calls=%async_computation.5 | async-start | bytes 884736 | tf_op jit(solution)/shard_map/reduce_scatter | solution.py:193
  268.5 284.4 %all-reduce.19.cloned.1.call-start = ((), (), s32[]{:S(2)}) async-start(), calls=%async_computation.8 | async-start | bytes 25165824 | tf_op jit(solution)/shard_map/psum | solution.py:148
  279.1 434.8 %reduce-scatter.10.cloned.1.call-start = ((), (), s32[]{:S(2)}) async-start(), calls=%async_computation.7 | async-start | bytes 270336
  280.9 49.7 %copy-start.8 = (f32[64,384]{1,0:T(8,128)S(1)}, f32[64,384]{1,0:T(8,128)}, u32[]{:S(2)}) copy-start(f32[64,384]{1,0:T(8,128)} %param.37) | copy-start | bytes 294916
  280.9 49.7 %copy-start.12 = (f32[64,384]{1,0:T(8,128)S(1)}, f32[64,384]{1,0:T(8,128)}, u32[]{:S(2)}) copy-start(f32[64,384]{1,0:T(8,128)} %param.55) | copy-start | bytes 294916
  280.9 49.7 %copy-start.13 = (f32[64,384]{1,0:T(8,128)S(1)}, f32[64,384]{1,0:T(8,128)}, u32[]{:S(2)}) copy-start(f32[64,384]{1,0:T(8,128)} %param.46) | copy-start | bytes 294916
  581.8 46.8 %copy-start.18 = (f32[16]{0:T(128)S(1)}, f32[16]{0:T(128)}, u32[]{:S(2)}) copy-start(f32[16]{0:T(128)} %param.34) | copy-start | bytes 196
  581.8 46.8 %copy-start.19 = (f32[16]{0:T(128)S(1)}, f32[16]{0:T(128)}, u32[]{:S(2)}) copy-start(f32[16]{0:T(128)} %param.52) | copy-start | bytes 196
  581.8 47.4 %copy-start.21 = (f32[16]{0:T(128)S(1)}, f32[16]{0:T(128)}, u32[]{:S(2)}) copy-start(f32[16]{0:T(128)} %param.35) | copy-start | bytes 196
  581.8 47.4 %copy-start.22 = (f32[16]{0:T(128)S(1)}, f32[16]{0:T(128)}, u32[]{:S(2)}) copy-start(f32[16]{0:T(128)} %param.53) | copy-start | bytes 196
  581.9 47.4 %copy-start.23 = (f32[16]{0:T(128)S(1)}, f32[16]{0:T(128)}, u32[]{:S(2)}) copy-start(f32[16]{0:T(128)} %param.44) | copy-start | bytes 196
  581.9 48.0 %copy-start.24 = (f32[16]{0:T(128)S(1)}, f32[16]{0:T(128)}, u32[]{:S(2)}) copy-start(f32[16]{0:T(128)} %param.36) | copy-start | bytes 196
  581.9 48.0 %copy-start.25 = (f32[16]{0:T(128)S(1)}, f32[16]{0:T(128)}, u32[]{:S(2)}) copy-start(f32[16]{0:T(128)} %param.54) | copy-start | bytes 196
  581.9 48.0 %copy-start.26 = (f32[16]{0:T(128)S(1)}, f32[16]{0:T(128)}, u32[]{:S(2)}) copy-start(f32[16]{0:T(128)} %param.45) | copy-start | bytes 196
  581.9 48.6 %copy-start.27 = (f32[16]{0:T(128)S(1)}, f32[16]{0:T(128)}, u32[]{:S(2)}) copy-start(f32[16]{0:T(128)} %param.40) | copy-start | bytes 196
  581.9 48.6 %copy-start.28 = (f32[16]{0:T(128)S(1)}, f32[16]{0:T(128)}, u32[]{:S(2)}) copy-start(f32[16]{0:T(128)} %param.58) | copy-start | bytes 196
  581.9 48.5 %copy-start.29 = (f32[16]{0:T(128)S(1)}, f32[16]{0:T(128)}, u32[]{:S(2)}) copy-start(f32[16]{0:T(128)} %param.49) | copy-start | bytes 196
  581.9 49.2 %copy-start.30 = (f32[16]{0:T(128)S(1)}, f32[16]{0:T(128)}, u32[]{:S(2)}) copy-start(f32[16]{0:T(128)} %param.41) | copy-start | bytes 196
  582.0 49.1 %copy-start.31 = (f32[16]{0:T(128)S(1)}, f32[16]{0:T(128)}, u32[]{:S(2)}) copy-start(f32[16]{0:T(128)} %param.59) | copy-start | bytes 196
  582.0 49.1 %copy-start.32 = (f32[16]{0:T(128)S(1)}, f32[16]{0:T(128)}, u32[]{:S(2)}) copy-start(f32[16]{0:T(128)} %param.50) | copy-start | bytes 196
  582.0 49.7 %copy-start.33 = (f32[48]{0:T(128)S(1)}, f32[48]{0:T(128)}, u32[]{:S(2)}) copy-start(f32[48]{0:T(128)} %param.38) | copy-start | bytes 580
  582.0 49.7 %copy-start.34 = (f32[48]{0:T(128)S(1)}, f32[48]{0:T(128)}, u32[]{:S(2)}) copy-start(f32[48]{0:T(128)} %param.56) | copy-start | bytes 580
  582.0 49.7 %copy-start.35 = (f32[48]{0:T(128)S(1)}, f32[48]{0:T(128)}, u32[]{:S(2)}) copy-start(f32[48]{0:T(128)} %param.47) | copy-start | bytes 580
  582.0 132.6 %copy-start.14 = (f32[16,7]{0,1:T(8,128)S(1)}, f32[16,7]{0,1:T(8,128)}, u32[]{:S(2)}) copy-start(f32[16,7]{0,1:T(8,128)} %param.33) | copy-start | bytes 1348
  582.0 132.6 %copy-start.16 = (f32[16,7]{0,1:T(8,128)S(1)}, f32[16,7]{0,1:T(8,128)}, u32[]{:S(2)}) copy-start(f32[16,7]{0,1:T(8,128)} %param.51) | copy-start | bytes 1348
  582.0 132.6 %copy-start.17 = (f32[16,7]{0,1:T(8,128)S(1)}, f32[16,7]{0,1:T(8,128)}, u32[]{:S(2)}) copy-start(f32[16,7]{0,1:T(8,128)} %param.42) | copy-start | bytes 1348
  (16 other events, 193.8 us)
Sparse Core Ops, SparseCore 0:
  9.6 31.9 all-gather.3
  43.1 29.1 all-gather.5
  160.2 63.0 reduce-scatter.7
  268.6 62.0 reduce-scatter.5
  333.1 219.6 all-reduce.18
  578.3 135.4 reduce-scatter.9
where the time goes:
time: 723 us; the launch traced here: 722 us
  waiting for transfers between devices  411 us (57%)
  blocking collectives  184 us (25%)
  other arithmetic  73.1 us (10%)
  matrix products  27.2 us (4%)
  between operations  14.6 us (2%)
  local copies, waits for them, and re-layouts  11.8 us (2%)
    psum x1, waiting for transfers between devices, per_device(): branch = lax.psum(partial_out, 'tp') + down_shift  221 us
    unnamed x7, waiting for transfers between devices  83 us
    unnamed x2, blocking collectives  77.1 us
    reduce_scatter x1, waiting for transfers between devices, per_device(): lax.psum_scatter(grad_down, 'dp', scatter_dimension=0, tiled=True)  63 us
    reduce_scatter x1, waiting for transfers between devices, per_device(): lax.psum_scatter(grad_up, 'dp', scatter_dimension=0, tiled=True)  44.5 us
    all_gather x1, blocking collectives, per_device(): lax.all_gather(conv_weight, ('dp', 'tp'), axis=0, tiled=True)  44.2 us
    all_gather x1, blocking collectives, per_device(): lax.all_gather(up_weight.astype(jnp.bfloat16), 'dp', axis=0, tiled=True)  31.3 us
    all_gather x1, blocking collectives, per_device(): lax.all_gather(down_weight.astype(jnp.bfloat16), 'dp', axis=0, tiled=True)  31.1 us
  transfers between devices with their start and end apart: 6, of which 4 were waited for; matrix products, arithmetic and copies ran while one was open for 5% of the time, Pallas kernels for 0%

commit v1 on v0

v1 whole, which is shorter than its diff:
```python
import functools

import jax
import jax.numpy as jnp
from jax import lax
from jax.experimental import pallas as pl
from jax.experimental.pallas import tpu as pltpu
from jax.sharding import PartitionSpec as P

STEP = 4


norm_eps = 1e-06
learn_rate = 0.05
first_decay = 0.9
second_decay = 0.999
adam_eps = 1e-08
weight_decay = 0.1
update_flags = (False, False, True, False, False, False, False, False, True)

LANES = 128
EDGE = 8
HALO = 2 * EDGE
CHUNK = 16
MIB = 1 << 20

f32 = jnp.float32
bf16 = jnp.bfloat16


def adam_step(weights_now, gradient, moment, square, step_number):
    next_moment = first_decay * moment + (1.0 - first_decay) * gradient
    next_square = second_decay * square + (1.0 - second_decay) * gradient * gradient
    first_fix = 1.0 - jnp.power(jnp.float32(first_decay), step_number)
    second_fix = 1.0 - jnp.power(jnp.float32(second_decay), step_number)
    step_ratio = next_moment / first_fix / (jnp.sqrt(next_square / second_fix) + adam_eps)
    update = -(learn_rate * (step_ratio + weight_decay * weights_now))
    return (weights_now + update, next_moment, next_square, update)


def vmem():
    return pl.BlockSpec(memory_space=pltpu.VMEM)


def smem():
    return pl.BlockSpec(memory_space=pltpu.SMEM)


FAST_MASKS = ((16, 8, 4, 2), (16, 8, 2, 4))


def position(core, dp_rel, x_rel):
    high, low, y = (dp_rel >> 2) & 1, (dp_rel >> 1) & 1, dp_rel & 1
    pair = (y | (x_rel << 1)) if core == 0 else (x_rel | (y << 1))
    return high | (low << 1) | (pair << 2)


def fill_shifted(s, lengths_ref, start, frames_get, left_get, right_get, sh, quarter, width):
    length = lengths_ref[s]
    zeros = jnp.zeros((EDGE, LANES), f32)
    blocks = width // LANES

    def masked(rows, first):
        place = lax.broadcasted_iota(jnp.int32, (rows.shape[0], LANES), 0) + first
        return lambda part: jnp.where(place < length, part, 0.0)

    left, right = left_get().astype(f32), right_get().astype(f32)
    mask_left, mask_right = masked(left, start - EDGE), masked(right, start + quarter)
    for j in range(blocks):
        lane = slice(j * LANES, (j + 1) * LANES)
        sh[j, 0:EDGE, :] = zeros
        sh[j, EDGE : 2 * EDGE, :] = mask_left(left[:, lane])
        sh[j, 2 * EDGE + quarter : 3 * EDGE + quarter, :] = mask_right(right[:, lane])
        sh[j, 3 * EDGE + quarter : 4 * EDGE + quarter, :] = zeros

    def step(i, _):
        row = pl.multiple_of(i * CHUNK, CHUNK)
        part = frames_get(row).astype(f32)
        mask = masked(part, start + row)
        for j in range(blocks):
            sh[j, pl.ds(row + 2 * EDGE, CHUNK), :] = mask(part[:, j * LANES : (j + 1) * LANES])
        return 0

    lax.fori_loop(0, quarter // CHUNK, step, 0)


def front_kernel(slots, quarter, width, taps, ints, frames, cot, left, right, params,
                 normed, unit, inv, bg, normed_t, bg_t, bg_sum, sh):
    half = taps // 2
    blocks = width // LANES
    own_rows = slots * quarter
    start = ints[slots]

    def lanes(j):
        return slice(j * LANES, (j + 1) * LANES)

    def norm_rows(pieces):
        conv = []
        for j in range(blocks):
            parts = []
            for first, rows in pieces:
                acc = jnp.broadcast_to(params[taps : taps + 1, lanes(j)], (rows, LANES))
                for k in range(taps):
                    acc = acc + sh[j, pl.ds(first + k - half, rows), :] * params[k : k + 1, lanes(j)]
                parts.append(acc)
            conv.append(parts[0] if len(parts) == 1 else jnp.concatenate(parts, axis=0))
        total = conv[0]
        for j in range(1, blocks):
            total = total + conv[j]
        mean = jnp.sum(total, axis=1, keepdims=True) * (1.0 / width)
        conv = [c - mean for c in conv]
        total = conv[0] * conv[0]
        for j in range(1, blocks):
            total = total + conv[j] * conv[j]
        inverse = lax.rsqrt(jnp.sum(total, axis=1, keepdims=True) * (1.0 / width) + norm_eps)
        return [c * inverse for c in conv], inverse

    def put_rows(row, pieces):
        parts, inverse = norm_rows(pieces)
        rows = pl.ds(row, CHUNK)
        inv[rows, :] = jnp.broadcast_to(inverse, (CHUNK, LANES))
        for j in range(blocks):
            unit[rows, lanes(j)] = parts[j]
            normed[rows, lanes(j)] = (
                parts[j] * params[taps + 1 : taps + 2, lanes(j)] + params[taps + 2 : taps + 3, lanes(j)]
            ).astype(bf16)

    bg_sum[...] = jnp.zeros_like(bg_sum)
    for s in range(slots):
        length = ints[s]
        fill_shifted(
            s, ints, start,
            lambda row: frames[s, pl.ds(row, CHUNK), :],
            lambda: left[s, 0], lambda: right[s, 0], sh, quarter, width,
        )

        def step(i, _):
            row = pl.multiple_of(i * CHUNK, CHUNK)
            put_rows(pl.multiple_of(s * quarter + row, CHUNK), [(row + 2 * EDGE, CHUNK)])
            place = lax.broadcasted_iota(jnp.int32, (CHUNK, width), 0) + (start + row)
            back = jnp.where(place < length, cot[s, pl.ds(row, CHUNK), :].astype(f32), 0.0)
            low = (back * params[taps + 4 : taps + 5, :]).astype(bf16)
            bg[pl.ds(pl.multiple_of(s * quarter + row, CHUNK), CHUNK), :] = low
            wide = low.astype(f32)
            bg_sum[...] += wide[0:8] + wide[8:16]
            return 0

        lax.fori_loop(0, quarter // CHUNK, step, 0)
        tail = own_rows + s * HALO
        put_rows(tail, [(EDGE, EDGE), (2 * EDGE + quarter, EDGE)])
        edge = jnp.concatenate([left[s, 1].astype(f32), right[s, 1].astype(f32)], axis=0)
        ids = lax.broadcasted_iota(jnp.int32, (HALO, width), 0)
        place = jnp.where(ids < EDGE, start - EDGE + ids, start + quarter - EDGE + ids)
        back = jnp.where(place < length, edge, 0.0)
        bg[tail : tail + HALO, :] = (back * params[taps + 4 : taps + 5, :]).astype(bf16)
        own = slice(s * quarter, (s + 1) * quarter)
        normed_t[:, own] = normed[own, :].T
        bg_t[:, own] = bg[own, :].T


def hidden_kernel(own_rows, row_step, blocks_of, ints, normed, bg, normed_t, bg_t, params, *refs):
    slots, taps, dp_count, own_width, fast = blocks_of
    if fast:
        low_ref, high_ref, refs = refs[0], refs[1], refs[2:]
    else:
        in_up, in_down, refs = refs[0], refs[1], refs[2:]
    act, hg, grads, bias_grad, up, down, hidden, pulled, grad_up, grad_down = refs
    all_rows = normed.shape[0]
    rows_dp = up.shape[0] // dp_count
    dp_own, core = ints[slots + 1], ints[slots + 2]

    def each_block(put):
        for c in range(2):
            @pl.when(core == c)
            def _():
                for dp_rel in range(dp_count):
                    first = pl.multiple_of((dp_rel ^ dp_own) * rows_dp, rows_dp)
                    for x_rel in range(2):
                        put(position(c, dp_rel, x_rel), pl.ds(first, rows_dp), slice(x_rel * own_width, (x_rel + 1) * own_width))

    if fast:
        def gather(place, rows, columns):
            source = (low_ref, high_ref)[place >> 3]
            up[rows, columns] = source[place & 7, :, 0:own_width]
            down[rows, columns] = source[place & 7, :, own_width : 2 * own_width]
        each_block(gather)
    else:
        up[...] = in_up[...]
        down[...] = in_down[...]

    base = taps + 5
    bias = jnp.concatenate(
        [params[pl.ds(base + ints[slots + 3 + x], 1), 0:own_width] for x in range(2)], axis=1
    )
    wide = 2 * own_width
    column_step = 256

    def rows_step(i, _):
        rows = pl.ds(pl.multiple_of(i * row_step, CHUNK), row_step)
        hidden[...] = jnp.dot(normed[rows, :], up[...], preferred_element_type=f32)
        pulled[...] = jnp.dot(bg[rows, :], down[...], preferred_element_type=f32)

        def part(r, _):
            sub = pl.ds(pl.multiple_of(r * CHUNK, CHUNK), CHUNK)
            out = pl.ds(pl.multiple_of(i * row_step + r * CHUNK, CHUNK), CHUNK)
            for column in range(0, wide, column_step):
                columns = slice(column, column + column_step)
                v = hidden[sub, columns] + bias[:, columns]
                fall = jnp.exp(v * v * -0.5)
                t = 1.0 / (1.0 + jnp.abs(v) * (0.3275911 * 0.7071067811865476))
                tail = t * (0.5 * 0.254829592 + t * (0.5 * -0.284496736 + t * (0.5 * 1.421413741 + t * (0.5 * -1.453152027 + t * (0.5 * 1.061405429)))))
                tail = tail * fall
                below = jnp.where(v < 0.0, tail, 1.0 - tail)
                act[out, columns] = (v * below).astype(bf16)
                slope = below + v * (fall * 0.3989422804014327)
                hg[out, columns] = (pulled[sub, columns] * slope).astype(bf16)
            return 0

        lax.fori_loop(0, row_step // CHUNK, part, 0)
        return 0

    lax.fori_loop(0, all_rows // row_step, rows_step, 0)
    grad_up[...] = jnp.dot(normed_t[...], hg[0:own_rows, :], preferred_element_type=f32).astype(grad_up.dtype)
    grad_down[...] = jnp.dot(bg_t[...], act[0:own_rows, :], preferred_element_type=f32).astype(grad_down.dtype)
    bias_grad[...] = jnp.dot(jnp.ones((8, own_rows), bf16), hg[0:own_rows, :], preferred_element_type=f32)
    if fast:
        def scatter(place, rows, columns):
            grads[place, :, 0:own_width] = grad_up[rows, columns]
            grads[place, :, own_width : 2 * own_width] = grad_down[rows, columns]
        each_block(scatter)
    else:
        grads[0] = grad_up[...]
        grads[1] = grad_down[...]


def back_kernel(shape, ints, params, left, right, act0, act1, hg0, hg1, up0, up1, down0, down1, unit, inv, bias0, bias1, bg_sum,
                frames, cot, output, input_grad, small, sh, cgs, ngs, branch, ng_halo, acc):
    slots, quarter, width, taps, own_width = shape
    half = taps // 2
    blocks = width // LANES
    own_rows = slots * quarter
    s = pl.program_id(0)
    start = ints[slots]
    length = ints[s]
    NT = (((1,), (1,)), ((), ()))

    def lanes(j):
        return slice(j * LANES, (j + 1) * LANES)

    def product(a0, a1, w0, w1, rows):
        return lax.dot_general(a0[rows, :], w0[...], NT, preferred_element_type=f32) + lax.dot_general(
            a1[rows, :], w1[...], NT, preferred_element_type=f32
        )

    @pl.when(s == 0)
    def _():
        acc[...] = jnp.zeros_like(acc)
        ng_halo[...] = product(hg0, hg1, up0, up1, pl.ds(own_rows, slots * HALO))

    fill_shifted(
        s, ints, start, lambda row: frames[0, pl.ds(row, CHUNK), :],
        lambda: left[s, 0], lambda: right[s, 0], sh, quarter, width,
    )
    own = pl.ds(pl.multiple_of(s * quarter, CHUNK), quarter)
    ngs[...] = product(hg0, hg1, up0, up1, own)
    branch[...] = product(act0, act1, down0, down1, own)

    def norm_back(ng, rows):
        u = [unit[rows, lanes(j)] for j in range(blocks)]
        scaled = [ng[j] * params[taps + 1 : taps + 2, lanes(j)] for j in range(blocks)]
        first, second = scaled[0], scaled[0] * u[0]
        for j in range(1, blocks):
            first = first + scaled[j]
            second = second + scaled[j] * u[j]
        first = jnp.sum(first, axis=1, keepdims=True) * (1.0 / width)
        second = jnp.sum(second, axis=1, keepdims=True) * (1.0 / width)
        inverse = inv[rows, :]
        return u, [inverse * (scaled[j] - first - u[j] * second) for j in range(blocks)]

    def fold(value):
        return value[0:8] + value[8:16]

    def norm_step(i, _):
        row = pl.multiple_of(i * CHUNK, CHUNK)
        ng = [ngs[pl.ds(row, CHUNK), lanes(j)] for j in range(blocks)]
        u, cg = norm_back(ng, pl.ds(pl.multiple_of(s * quarter + row, CHUNK), CHUNK))
        for j in range(blocks):
            cgs[j, pl.ds(row + 2 * EDGE, CHUNK), :] = cg[j]
            acc[taps + 1, :, lanes(j)] += fold(ng[j] * u[j])
            acc[taps + 2, :, lanes(j)] += fold(ng[j])
            acc[taps, :, lanes(j)] += fold(cg[j])
        return 0

    lax.fori_loop(0, quarter // CHUNK, norm_step, 0)
    tail = pl.multiple_of(s * HALO, HALO)
    ng = [ng_halo[pl.ds(tail, HALO), lanes(j)] for j in range(blocks)]
    _, cg = norm_back(ng, pl.ds(pl.multiple_of(own_rows + tail, HALO), HALO))
    for j in range(blocks):
        cgs[j, 0:EDGE, :] = jnp.zeros((EDGE, LANES), f32)
        cgs[j, EDGE : 2 * EDGE, :] = cg[j][0:EDGE]
        cgs[j, 2 * EDGE + quarter : 3 * EDGE + quarter, :] = cg[j][EDGE:HALO]
        cgs[j, 3 * EDGE + quarter : 4 * EDGE + quarter, :] = jnp.zeros((EDGE, LANES), f32)

    def out_step(i, _):
        row = pl.multiple_of(i * CHUNK, CHUNK)
        rows = pl.ds(row, CHUNK)
        for j in range(blocks):
            place = lax.broadcasted_iota(jnp.int32, (CHUNK, LANES), 0) + (start + row)
            live = place < length
            back = jnp.where(live, cot[0, rows, lanes(j)].astype(f32), 0.0)
            total = branch[rows, lanes(j)] + params[taps + 3 : taps + 4, lanes(j)]
            acc[taps + 4, :, lanes(j)] += fold(back * total)
            shown = frames[0, rows, lanes(j)].astype(f32) + params[taps + 4 : taps + 5, lanes(j)] * total
            output[0, rows, lanes(j)] = jnp.where(live, shown, 0.0)
            first = row + 2 * EDGE
            here = cgs[j, pl.ds(first, CHUNK), :]
            pulled = jnp.zeros((CHUNK, LANES), f32)
            for k in range(taps):
                pulled = pulled + cgs[j, pl.ds(first + half - k, CHUNK), :] * params[k : k + 1, lanes(j)]
                acc[k, :, lanes(j)] += fold(here * sh[j, pl.ds(first + k - half, CHUNK), :])
            input_grad[0, rows, lanes(j)] = back + jnp.where(live, pulled, 0.0)
        return 0

    lax.fori_loop(0, quarter // CHUNK, out_step, 0)

    @pl.when(s == slots - 1)
    def _():
        small[...] = jnp.zeros_like(small)
        for k in range(taps + 3):
            small[k : k + 1, :] = jnp.sum(acc[k], axis=0, keepdims=True)
        small[taps + 3 : taps + 4, :] = jnp.sum(bg_sum[...], axis=0, keepdims=True)
        small[taps + 4 : taps + 5, :] = jnp.sum(acc[taps + 4], axis=0, keepdims=True)
        for n, bias_grad in enumerate((bias0, bias1)):
            for x in range(2):
                place = ints[slots + 3 + 2 * n + x]
                small[pl.ds(taps + 5 + place, 1), 0:own_width] = bias_grad[0:1, x * own_width : (x + 1) * own_width]


def call(kernel, outs, in_specs, scratch, limit, flops=0, moved=0, grid=None, out_specs=None, name=None):
    grid_spec = pltpu.PrefetchScalarGridSpec(
        num_scalar_prefetch=0,
        grid=grid or (),
        in_specs=in_specs,
        out_specs=out_specs or [vmem()] * len(outs),
        scratch_shapes=scratch,
    )
    return pl.pallas_call(
        kernel,
        out_shape=[jax.ShapeDtypeStruct(shape, dtype) for shape, dtype in outs],
        grid_spec=grid_spec,
        compiler_params=pltpu.CompilerParams(vmem_limit_bytes=limit * MIB),
        cost_estimate=pl.CostEstimate(flops=flops, bytes_accessed=moved, transcendentals=0),
        name=name,
    )


def per_device(
    dp_count,
    tp_count,
    frames,
    cotangent,
    lengths,
    conv_weight,
    conv_bias,
    norm_gain,
    norm_bias,
    up_weight,
    up_bias,
    down_weight,
    down_bias,
    layer_scale,
    moment_conv_weight,
    moment_conv_bias,
    moment_norm_gain,
    moment_norm_bias,
    moment_up_weight,
    moment_up_bias,
    moment_down_weight,
    moment_down_bias,
    moment_layer_scale,
    square_conv_weight,
    square_conv_bias,
    square_norm_gain,
    square_norm_bias,
    square_up_weight,
    square_up_bias,
    square_down_weight,
    square_down_bias,
    square_layer_scale,
):
    both = ("dp", "tp")
    count = dp_count * tp_count
    dp_own, tp_own = lax.axis_index("dp"), lax.axis_index("tp")
    own = dp_own * tp_count + tp_own
    slots, quarter, width = frames.shape
    own_channels, taps = conv_weight.shape
    own_bias = up_bias.shape[0]
    own_rows_w, own_width = up_weight.shape
    hidden_width = own_width * tp_count
    all_rows = slots * (quarter + HALO)
    own_rows = slots * quarter
    fast = (dp_count, tp_count) == (8, 4) and own_rows_w % CHUNK == 0
    core = own & 1

    def swap(value, masks):
        return lax.ppermute(value, both, [(i, i ^ masks[i & 1]) for i in range(count)])

    if fast:
        steps = [(FAST_MASKS[0][k], FAST_MASKS[1][k]) for k in range(4)]
        held = jnp.concatenate([up_weight.astype(bf16), down_weight.astype(bf16)], axis=1)[None]
        for k in range(3):
            held = jnp.concatenate([held, swap(held, steps[k])], axis=0)
        far = swap(held, steps[3])
        other = swap(held, (1, 1))
        other_far = swap(far, (1, 1))
        weights = ((held, far), (other, other_far))
        blocks = [[tp_own ^ (2 * x + n) for x in range(2)] for n in range(2)]
    else:
        whole = [
            lax.all_gather(lax.all_gather(w.astype(bf16), "dp", axis=0, tiled=True), "tp", axis=1, tiled=True)
            for w in (up_weight, down_weight)
        ]
        middle = hidden_width // 2
        weights = tuple(tuple(w[:, n * middle : (n + 1) * middle] for w in whole) for n in range(2))
        blocks = [[jnp.int32(2 * n + x) for x in range(2)] for n in range(2)]

    pair = jnp.stack([frames, cotangent], axis=1)
    left = lax.ppermute(pair[:, :, quarter - EDGE :, :], "tp", [(i, i + 1) for i in range(tp_count - 1)])
    right = lax.ppermute(pair[:, :, :EDGE, :], "tp", [(i + 1, i) for i in range(tp_count - 1)])

    small_rows = taps + 5 + tp_count
    channels = jnp.concatenate(
        [conv_weight.T, conv_bias[None], norm_gain[None], norm_bias[None], down_bias[None], layer_scale[None]], axis=0
    )
    params = jnp.zeros((small_rows, width), f32)
    params = lax.dynamic_update_slice(params, channels, (0, own * own_channels))
    params = lax.dynamic_update_slice(
        params, up_bias[None], (taps + 5 + own * own_bias // own_width, own * own_bias % own_width)
    )
    bits = [1 << k for k in range(count.bit_length() - 1)]
    assert 1 << len(bits) == count

    def sum_all(value):
        for bit in bits:
            value = value + swap(value, (bit, bit))
        return value

    params = sum_all(params)

    ints = jnp.stack(
        [*[lengths[s] for s in range(slots)], tp_own * quarter, dp_own, core, *blocks[0], *blocks[1]]
    ).astype(jnp.int32)

    front = call(
        functools.partial(front_kernel, slots, quarter, width, taps),
        [
            ((all_rows, width), bf16),
            ((all_rows, width), f32),
            ((all_rows, LANES), f32),
            ((all_rows, width), bf16),
            ((width, own_rows), bf16),
            ((width, own_rows), bf16),
            ((8, width), f32),
        ],
        [smem(), vmem(), vmem(), vmem(), vmem(), vmem()],
        [pltpu.VMEM((width // LANES, quarter + 4 * EDGE, LANES), f32)],
        16, flops=10 * all_rows * width * taps, moved=8 * all_rows * width, name="front",
    )
    normed, unit, inv, bg, normed_t, bg_t, bg_sum = front(ints, frames, cotangent, left, right, params)

    wide = 2 * own_width
    row_step = 272 if all_rows % 272 == 0 else CHUNK
    results = []
    for n in range(2):
        half_ints = jnp.concatenate(
            [ints[: slots + 2], (ints[slots + 2] ^ n)[None], ints[slots + 3 + 2 * n : slots + 5 + 2 * n]]
        )
        grads_shape = (2 * dp_count, own_rows_w, wide) if fast else (2, width, wide)
        half = call(
            functools.partial(
                hidden_kernel, own_rows, row_step, (slots, taps, dp_count, own_width, fast)
            ),
            [
                ((all_rows, wide), bf16),
                ((all_rows, wide), bf16),
                (grads_shape, bf16 if fast else f32),
                ((8, wide), f32),
                ((width, wide), bf16),
                ((width, wide), bf16),
            ],
            [smem()] + [vmem()] * 7,
            [
                pltpu.VMEM((row_step, wide), f32),
                pltpu.VMEM((row_step, wide), f32),
                pltpu.VMEM((width, wide), bf16 if fast else f32),
                pltpu.VMEM((width, wide), bf16 if fast else f32),
            ],
            24, flops=8 * all_rows * width * wide, moved=8 * all_rows * wide, name=f"hidden{n}",
        )
        results.append(half(half_ints, normed, bg, normed_t, bg_t, params, *weights[n]))
    (act0, hg0, grads0, bias0, up0, down0), (act1, hg1, grads1, bias1, up1, down1) = results

    slot_spec = pl.BlockSpec((1, quarter, width), lambda s: (s, 0, 0))
    back = call(
        functools.partial(back_kernel, (slots, quarter, width, taps, own_width)),
        [
            ((slots, quarter, width), f32),
            ((slots, quarter, width), f32),
            ((small_rows, width), f32),
        ],
        [smem()] + [vmem()] * 16 + [slot_spec, slot_spec],
        [
            pltpu.VMEM((width // LANES, quarter + 4 * EDGE, LANES), f32),
            pltpu.VMEM((width // LANES, quarter + 4 * EDGE, LANES), f32),
            pltpu.VMEM((quarter, width), f32),
            pltpu.VMEM((quarter, width), f32),
            pltpu.VMEM((slots * HALO, width), f32),
            pltpu.VMEM((taps + 5, 8, width), f32),
        ],
        24, flops=4 * all_rows * width * hidden_width, moved=8 * all_rows * width,
        grid=(slots,), out_specs=[slot_spec, slot_spec, vmem()], name="back",
    )
    output_own, input_own, small = back(
        ints, params, left, right, act0, act1, hg0, hg1, up0, up1, down0, down1, unit, inv, bias0, bias1, bg_sum,
        frames, cotangent,
    )

    if fast:
        def plus(a, b):
            return (a.astype(f32) + b.astype(f32)).astype(bf16)

        arrived = swap(grads1, (1, 1))
        keep, send = plus(grads0[:8], arrived[:8]), plus(grads0[8:], arrived[8:])
        for k in range(3, 0, -1):
            size = keep.shape[0] // 2
            arrived = swap(send, steps[k])
            send = plus(keep[size:], arrived[size:])
            keep = plus(keep[:size], arrived[:size])
        arrived = swap(send, steps[0])
        total = keep[0].astype(f32) + arrived[0].astype(f32)
        up_share, down_share = total[:, :own_width], total[:, own_width:]
    else:
        up_share, down_share = (
            lax.psum_scatter(
                lax.psum_scatter(
                    jnp.concatenate([grads0[n], grads1[n]], axis=1), "tp", scatter_dimension=1, tiled=True
                ),
                "dp", scatter_dimension=0, tiled=True,
            )
            for n in range(2)
        )

    small = sum_all(small)
    own_small = lax.dynamic_slice(small, (0, own * own_channels), (taps + 5, own_channels))
    share_up = lax.dynamic_slice(
        small, (taps + 5 + own * own_bias // own_width, own * own_bias % own_width), (1, own_bias)
    )[0]

    step_number = jnp.float32(STEP)
    params_own = (
        conv_weight,
        conv_bias,
        norm_gain,
        norm_bias,
        up_weight,
        up_bias,
        down_weight,
        down_bias,
        layer_scale,
    )
    gradients = (
        own_small[:taps].T,
        own_small[taps],
        own_small[taps + 1],
        own_small[taps + 2],
        up_share,
        share_up,
        down_share,
        own_small[taps + 3],
        own_small[taps + 4],
    )
    moments = (
        moment_conv_weight,
        moment_conv_bias,
        moment_norm_gain,
        moment_norm_bias,
        moment_up_weight,
        moment_up_bias,
        moment_down_weight,
        moment_down_bias,
        moment_layer_scale,
    )
    squares = (
        square_conv_weight,
        square_conv_bias,
        square_norm_gain,
        square_norm_bias,
        square_up_weight,
        square_up_bias,
        square_down_weight,
        square_down_bias,
        square_layer_scale,
    )
    flat = [output_own, input_own]
    for weights_now, gradient, moment, square, use_update in zip(
        params_own, gradients, moments, squares, update_flags
    ):
        next_weights, next_moment, next_square, update = adam_step(
            weights_now, gradient, moment, square, step_number
        )
        shown = update if use_update else next_weights
        flat = flat + [gradient, shown, next_moment, next_square]
    return tuple(flat)


def solution(mesh):
    vector, matrix = P(("dp", "tp")), P("dp", "tp")
    taps = P(("dp", "tp"), None)
    frames = P("dp", "tp", None)
    parameters = (taps, vector, vector, vector, matrix, vector, matrix, vector, vector)
    return jax.shard_map(
        functools.partial(per_device, mesh.shape["dp"], mesh.shape["tp"]),
        mesh=mesh,
        in_specs=(frames, frames, P("dp")) + parameters * 3,
        out_specs=(frames, frames) + tuple(spec for spec in parameters for _ in range(4)),
        check_vma=False,
    )
```

time: 723 us -> 162 us (0.22)
  waiting for transfers between devices: 411 us -> 62.1 us
  blocking collectives: 184 us -> 0 us
  other arithmetic: 73.1 us -> 11.3 us
  Pallas kernels: 0 us -> 43.5 us
  starting transfers between devices: 0.64 us -> 32.6 us
  matrix products: 27.2 us -> 0 us
  between operations: 14.6 us -> 1.29 us
    psum x1 -> x0, waiting for transfers between devices: 221 us -> none  [per_device(): branch = lax.psum(partial_out, 'tp') + down_shift]
    reduce_scatter x2 -> x0, waiting for transfers between devices: 107 us -> none  [the longest x1 63 us: per_device(): lax.psum_scatter(grad_down, 'dp', scatter_dimension=0, tiled=True)]
    all_gather x3 -> x0, blocking collectives: 107 us -> none  [the longest x1 44.2 us: per_device(): lax.all_gather(conv_weight, ('dp', 'tp'), axis=0, tiled=True)]
    unnamed x7 -> x0, waiting for transfers between devices: 83 us -> none
    unnamed x2 -> x0, blocking collectives: 77.1 us -> none
    ppermute x0 -> x23, waiting for transfers between devices: none -> 62.1 us  [the longest x21 62.1 us: swap(): lax.ppermute(value, both, [(i, i ^ masks[i & 1]) for i in range(count)])]
    pallas_call x0 -> x4, Pallas kernels: none -> 43.5 us  [the longest x2 18.3 us: per_device(): half(half_ints, normed, bg, normed_t, bg_t, params, *weights[n])]
    ppermute x0 -> x23, starting transfers between devices: none -> 32.6 us  [the longest x21 30 us: swap(): lax.ppermute(value, both, [(i, i ^ masks[i & 1]) for i in range(count)])]
  transfers between devices with their start and end apart: 6 -> 23, of which waited for: 4 -> 16; matrix products, arithmetic and copies ran while one was open for 5% -> 2% of each run, Pallas kernels for 0% -> 21%
where the time goes in v1:
time: 162 us; the launch traced here: 161 us
  waiting for transfers between devices  62.1 us (38%)
  Pallas kernels  43.5 us (27%)
  starting transfers between devices  32.6 us (20%)
  other arithmetic  11.3 us (7%)
  local copies, waits for them, and re-layouts  10.6 us (7%)
    ppermute x21, waiting for transfers between devices, swap(): lax.ppermute(value, both, [(i, i ^ masks[i & 1]) for i in range(count)])  62.1 us
    ppermute x21, starting transfers between devices, swap(): lax.ppermute(value, both, [(i, i ^ masks[i & 1]) for i in range(count)])  30 us
    pallas_call x2, Pallas kernels, per_device(): half(half_ints, normed, bg, normed_t, bg_t, params, *weights[n])  18.3 us
    pallas_call x1, Pallas kernels, per_device(): back(ints, params, left, right, act0, act1, hg0, hg1, up0, up1, down0, do...  13.7 us
    pallas_call x1, Pallas kernels, per_device(): front(ints, frames, cotangent, left, right, params)  11.5 us
    unnamed x96, local copies, waits for them, and re-layouts  9.46 us
    convert_element_type x4, other arithmetic, plus(): return (a.astype(f32) + b.astype(f32)).astype(bf16)  4.82 us
  transfers between devices with their start and end apart: 23, of which 16 were waited for; matrix products, arithmetic and copies ran while one was open for 2% of the time, Pallas kernels for 21%

profile of v1, /device:TPU:0, one launch (start us, length us, event | category | flops | bytes accessed | tf_op | source)
XLA Modules:
  0.0 161.5 jit_solution(1672674702533293711)
XLA Ops:
  2.6 4.1 %collective-permute-start.7 = (bf16[1,64,768]{2,1,0:T(8,128)(2,1)S(1)}, bf16[1,64,768]{2,1,0:T(8,128)(2,1)S(1)}, u32[]{:S(2)}, u32[]{:S(2)}) collective-permute-start(bf16[1,64,768]{2,1,0:T(8,128)(2,1)S(1)} %maximum_bitcast_fusion), channel_id=1, source_target_pairs={{0,16},{1,17},{2,18},{3,19},{4,20},{5,21},{6,22},{7,23},{8,24},{9,... | collective-permute-start | bytes 294920 | tf_op jit(solution)/shard_map/ppermute | solution.py:406
  6.8 4.9 %collective-permute-done.7 = bf16[1,64,768]{2,1,0:T(8,128)(2,1)S(1)} collective-permute-done((bf16[1,64,768]{2,1,0:T(8,128)(2,1)S(1)}, bf16[1,64,768]{2,1,0:T(8,128)(2,1)S(1)}, u32[]{:S(2)}, u32[]{:S(2)}) %collective-permute-start.7) | collective-permute-done | bytes 98336 | tf_op jit(solution)/shard_map/ppermute | solution.py:406
  12.5 5.3 %collective-permute-done.8 = bf16[2,64,768]{2,1,0:T(8,128)(2,1)S(1)} collective-permute-done((bf16[2,64,768]{2,1,0:T(8,128)(2,1)S(1)}, bf16[2,64,768]{2,1,0:T(8,128)(2,1)S(1)}, u32[]{:S(2)}, u32[]{:S(2)}) %collective-permute-start.8) | collective-permute-done | bytes 196640 | tf_op jit(solution)/shard_map/ppermute | solution.py:406
  17.9 1.3 collective-permute-start.9
  19.2 6.5 %collective-permute-done.9 = bf16[4,64,768]{2,1,0:T(8,128)(2,1)S(1)} collective-permute-done((bf16[4,64,768]{2,1,0:T(8,128)(2,1)S(1)}, bf16[4,64,768]{2,1,0:T(8,128)(2,1)S(1)}, u32[]{:S(2)}, u32[]{:S(2)}) %collective-permute-start.9) | collective-permute-done | bytes 393248 | tf_op jit(solution)/shard_map/ppermute | solution.py:406
  27.9 11.1 %collective-permute-done.10.refs_1_ = bf16[8,64,768]{2,1,0:T(8,128)(2,1)} collective-permute-done((bf16[8,64,768]{2,1,0:T(8,128)(2,1)}, bf16[8,64,768]{2,1,0:T(8,128)(2,1)}, u32[]{:S(2)}, u32[]{:S(2)}) %collective-permute-start.10) | collective-permute-done | bytes 786464 | tf_op jit(solution)/shard_map/ppermute | solution.py:406
  42.9 2.7 %collective-permute-done.1 = f32[16,512]{1,0:T(8,128)S(1)} collective-permute-done((f32[16,512]{1,0:T(8,128)S(1)}, f32[16,512]{1,0:T(8,128)S(1)}, u32[]{:S(2)}, u32[]{:S(2)}) %collective-permute-start.1) | collective-permute-done | bytes 32800 | tf_op jit(solution)/shard_map/ppermute | solution.py:406
  46.9 2.7 %collective-permute-done.2 = f32[16,512]{1,0:T(8,128)S(1)} collective-permute-done((f32[16,512]{1,0:T(8,128)S(1)}, f32[16,512]{1,0:T(8,128)S(1)}, u32[]{:S(2)}, u32[]{:S(2)}) %collective-permute-start.2) | collective-permute-done | bytes 32800 | tf_op jit(solution)/shard_map/ppermute | solution.py:406
  49.5 1.5 collective-permute-start.3
  51.0 1.3 collective-permute-start.5
  53.7 3.4 %collective-permute-start.4 = (f32[16,512]{1,0:T(8,128)S(1)}, f32[16,512]{1,0:T(8,128)S(1)}, u32[]{:S(2)}, u32[]{:S(2)}) collective-permute-start(f32[16,512]{1,0:T(8,128)S(1)} %add.231), channel_id=1, source_target_pairs={{0,16},{1,17},{2,18},{3,19},{4,20},{5,21},{6,22},{7,23},{8,24},{9,... | collective-permute-start | bytes 98312 | tf_op jit(solution)/shard_map/ppermute | solution.py:406
  57.2 1.7 %collective-permute-done.4 = f32[16,512]{1,0:T(8,128)S(1)} collective-permute-done((f32[16,512]{1,0:T(8,128)S(1)}, f32[16,512]{1,0:T(8,128)S(1)}, u32[]{:S(2)}, u32[]{:S(2)}) %collective-permute-start.4) | collective-permute-done | bytes 32800 | tf_op jit(solution)/shard_map/ppermute | solution.py:406
  58.9 11.5 %front.1 = (bf16[816,512]{1,0:T(8,128)(2,1)S(1)}, f32[816,512]{1,0:T(8,128)S(1)}, f32[816,128]{1,0:T(8,128)S(1)}, bf16[816,512]{1,0:T(8,128)(2,1)S(1)}, bf16[512...) custom-call(s32[10]{0:T(128)S(1)} %stack.40.ints, bf16[3,256,512]{2,1,0:T(8,128)(2,1)S(1)} %copy-done.1, ...), custom_call_target="tpu_custom_call" | custom-call | flops 29245440 | bytes 3342336 | tf_op jit(solution)/shard_map/front/pallas_call | solution.py:469
  71.3 10.3 %hidden1.1 = (bf16[816,768]{1,0:T(8,128)(2,1)S(1)}, bf16[816,768]{1,0:T(8,128)(2,1)S(1)}, bf16[16,64,768]{2,1,0:T(8,128)(2,1)}, f32[8,768]{1,0:T(8,128)S(1)}, bf...) custom-call(s32[8]{0:T(128)S(1)} %concatenate.35.ints, bf16[816,512]{1,0:T(8,128)(2,1)S(1)} %get-tuple-element.60.normed, ...), custom_call_target="tpu_custom_call" | custom-call | flops 2566914048 | bytes 5013504 | tf_op jit(solution)/shard_map/hidden1/pallas_call | solution.py:500
  85.6 2.1 %collective-permute-start.18 = (bf16[16,64,768]{2,1,0:T(8,128)(2,1)}, bf16[16,64,768]{2,1,0:T(8,128)(2,1)}, u32[]{:S(2)}, u32[]{:S(2)}) collective-permute-start(bf16[16,64,768]{2,1,0:T(8,128)(2,1)} %get-tuple-element.81), channel_id=1, source_target_pairs={{0,1},{1,0},{2,3},{3,2},{4,5},{5,4},{6,7},{7,6},{8,9},{9,8},{10,11... | collective-permute-start | bytes 4718600 | tf_op jit(solution)/shard_map/ppermute | solution.py:406
  92.3 8.0 %hidden0.1 = (bf16[816,768]{1,0:T(8,128)(2,1)S(1)}, bf16[816,768]{1,0:T(8,128)(2,1)S(1)}, bf16[16,64,768]{2,1,0:T(8,128)(2,1)S(1)}, f32[8,768]{1,0:T(8,128)S(1)}...) custom-call(s32[8]{0:T(128)S(1)} %concatenate.30.ints, bf16[816,512]{1,0:T(8,128)(2,1)S(1)} %copy-done.13, ...), custom_call_target="tpu_custom_call" | custom-call | flops 2566914048 | bytes 5013504 | tf_op jit(solution)/shard_map/hidden0/pallas_call | solution.py:500
  100.4 3.1 %add_convert_fusion.1 = (bf16[8,64,768]{2,1,0:T(8,128)(2,1)}, bf16[8,64,768]{2,1,0:T(8,128)(2,1)}) fusion(bf16[16,64,768]{2,1,0:T(8,128)(2,1)} %collective-permute-done.18, bf16[16,64,768]{2,1,0:T(8,128)(2,1)S(1)} %get-tuple-element.80), kind=kLoop, calls=%fused_computation.1 | loop fusion | flops 3145728 | bytes 4718592 | tf_op jit(solution)/shard_map/convert_element_type | solution.py:530
  103.5 2.5 %collective-permute-start.19 = (bf16[8,64,768]{2,1,0:T(8,128)(2,1)}, bf16[8,64,768]{2,1,0:T(8,128)(2,1)}, u32[]{:S(2)}, u32[]{:S(2)}) collective-permute-start(bf16[8,64,768]{2,1,0:T(8,128)(2,1)} %get-tuple-element.119), channel_id=1, source_target_pairs={{0,2},{1,5},{2,0},{3,7},{4,6},{5,1},{6,4},{7,3},{8,10},{9,13},{10,... | collective-permute-start | bytes 2359304 | tf_op jit(solution)/shard_map/ppermute | solution.py:406
  106.1 13.7 %back.1 = (f32[3,256,512]{2,1,0:T(8,128)}, f32[3,256,512]{2,1,0:T(8,128)}, f32[16,512]{1,0:T(8,128)S(1)}) custom-call(s32[10]{0:T(128)S(1)} %stack.40.ints, f32[16,512]{1,0:T(8,128)S(1)} %add.232.params, bf16[3,2,8,512]{3,2,1,0:T(8,128)(2,1)S(1)} %collective-permute-done.5.left, bf16[3,2,8,512]{3,2,1,0:T(8,128)(2,1)S(1)} %collective-permute-done.6.right, ...), custom_call_target="tpu_custom_call" | custom-call | flops 2566914048 | bytes 3342336 | tf_op jit(solution)/shard_map/back/pallas_call | solution.py:523
  121.1 1.4 collective-permute-start.14
  122.5 2.5 %collective-permute-done.14 = f32[16,512]{1,0:T(8,128)S(1)} collective-permute-done((f32[16,512]{1,0:T(8,128)S(1)}, f32[16,512]{1,0:T(8,128)S(1)}, u32[]{:S(2)}, u32[]{:S(2)}) %collective-permute-start.14) | collective-permute-done | bytes 32800 | tf_op jit(solution)/shard_map/ppermute | solution.py:406
  125.1 1.5 collective-permute-start.15
  126.6 2.4 %collective-permute-done.15 = f32[16,512]{1,0:T(8,128)S(1)} collective-permute-done((f32[16,512]{1,0:T(8,128)S(1)}, f32[16,512]{1,0:T(8,128)S(1)}, u32[]{:S(2)}, u32[]{:S(2)}) %collective-permute-start.15) | collective-permute-done | bytes 32800 | tf_op jit(solution)/shard_map/ppermute | solution.py:406
  129.2 3.7 %collective-permute-done.16 = f32[16,512]{1,0:T(8,128)S(1)} collective-permute-done((f32[16,512]{1,0:T(8,128)S(1)}, f32[16,512]{1,0:T(8,128)S(1)}, u32[]{:S(2)}, u32[]{:S(2)}) %collective-permute-start.16) | collective-permute-done | bytes 32800 | tf_op jit(solution)/shard_map/ppermute | solution.py:406
  132.9 2.8 %collective-permute-start.17 = (f32[16,512]{1,0:T(8,128)S(1)}, f32[16,512]{1,0:T(8,128)S(1)}, u32[]{:S(2)}, u32[]{:S(2)}) collective-permute-start(f32[16,512]{1,0:T(8,128)S(1)} %add.236), channel_id=1, source_target_pairs={{0,16},{1,17},{2,18},{3,19},{4,20},{5,21},{6,22},{7,23},{8,24},{9,... | collective-permute-start | bytes 98312 | tf_op jit(solution)/shard_map/ppermute | solution.py:406
  135.7 2.0 %collective-permute-done.17 = f32[16,512]{1,0:T(8,128)S(1)} collective-permute-done((f32[16,512]{1,0:T(8,128)S(1)}, f32[16,512]{1,0:T(8,128)S(1)}, u32[]{:S(2)}, u32[]{:S(2)}) %collective-permute-start.17) | collective-permute-done | bytes 32800 | tf_op jit(solution)/shard_map/ppermute | solution.py:406
  137.8 1.6 add_convert_fusion.3
  139.4 1.6 collective-permute-start.20
  142.5 4.8 %collective-permute-done.20 = bf16[4,64,768]{2,1,0:T(8,128)(2,1)S(1)} collective-permute-done((bf16[4,64,768]{2,1,0:T(8,128)(2,1)S(1)}, bf16[4,64,768]{2,1,0:T(8,128)(2,1)S(1)}, u32[]{:S(2)}, u32[]{:S(2)}) %collective-permute-start.20) | collective-permute-done | bytes 393248 | tf_op jit(solution)/shard_map/ppermute | solution.py:406
  148.2 5.8 %collective-permute-done.21 = bf16[2,64,768]{2,1,0:T(8,128)(2,1)S(1)} collective-permute-done((bf16[2,64,768]{2,1,0:T(8,128)(2,1)S(1)}, bf16[2,64,768]{2,1,0:T(8,128)(2,1)S(1)}, u32[]{:S(2)}, u32[]{:S(2)}) %collective-permute-start.21) | collective-permute-done | bytes 196640 | tf_op jit(solution)/shard_map/ppermute | solution.py:406
  154.1 1.8 %collective-permute-start.22 = (bf16[1,64,768]{2,1,0:T(8,128)(2,1)S(1)}, bf16[1,64,768]{2,1,0:T(8,128)(2,1)S(1)}, u32[]{:S(2)}, u32[]{:S(2)}) collective-permute-start(bf16[1,64,768]{2,1,0:T(8,128)(2,1)S(1)} %add_convert_fusion.6), channel_id=1, source_target_pairs={{0,16},{1,17},{2,18},{3,19},{4,20},{5,21},{6,22},{7,23},{8,24},{9,... | collective-permute-start | bytes 294920 | tf_op jit(solution)/shard_map/ppermute | solution.py:406
  156.6 3.9 %collective-permute-done.22 = bf16[1,64,768]{2,1,0:T(8,128)(2,1)S(1)} collective-permute-done((bf16[1,64,768]{2,1,0:T(8,128)(2,1)S(1)}, bf16[1,64,768]{2,1,0:T(8,128)(2,1)S(1)}, u32[]{:S(2)}, u32[]{:S(2)}) %collective-permute-start.22) | collective-permute-done | bytes 98336 | tf_op jit(solution)/shard_map/ppermute | solution.py:406
  (148 shorter events, 26.5 us)
Async XLA Ops:
  1.6 37.4 %copy-start.26 = (f32[16,7]{0,1:T(8,128)S(1)}, f32[16,7]{0,1:T(8,128)}, u32[]{:S(2)}) copy-start(f32[16,7]{0,1:T(8,128)} %param.33) | copy-start | bytes 1348
  1.6 37.4 %copy-start.31 = (f32[16]{0:T(128)S(1)}, f32[16]{0:T(128)}, u32[]{:S(2)}) copy-start(f32[16]{0:T(128)} %param.35) | copy-start | bytes 196
  1.6 37.4 %copy-start.32 = (f32[16]{0:T(128)S(1)}, f32[16]{0:T(128)}, u32[]{:S(2)}) copy-start(f32[16]{0:T(128)} %param.36) | copy-start | bytes 196
  1.6 37.4 %copy-start.33 = (f32[16]{0:T(128)S(1)}, f32[16]{0:T(128)}, u32[]{:S(2)}) copy-start(f32[16]{0:T(128)} %param.40) | copy-start | bytes 196
  1.6 37.4 %copy-start.34 = (f32[16]{0:T(128)S(1)}, f32[16]{0:T(128)}, u32[]{:S(2)}) copy-start(f32[16]{0:T(128)} %param.41) | copy-start | bytes 196
  1.6 37.4 %copy-start.35 = (f32[16]{0:T(128)S(1)}, f32[16]{0:T(128)}, u32[]{:S(2)}) copy-start(f32[16]{0:T(128)} %param.34) | copy-start | bytes 196
  2.6 48.4 %copy-start = (bf16[3,256,512]{2,1,0:T(8,128)(2,1)S(1)}, bf16[3,256,512]{2,1,0:T(8,128)(2,1)}, u32[]{:S(2)}) copy-start(bf16[3,256,512]{2,1,0:T(8,128)(2,1)} %cot.3) | copy-start | bytes 2359300
  2.6 48.4 %copy-start.1 = (bf16[3,256,512]{2,1,0:T(8,128)(2,1)S(1)}, bf16[3,256,512]{2,1,0:T(8,128)(2,1)}, u32[]{:S(2)}) copy-start(bf16[3,256,512]{2,1,0:T(8,128)(2,1)} %frames.3) | copy-start | bytes 2359300
  2.6 9.0 %collective-permute-start.7 = (bf16[1,64,768]{2,1,0:T(8,128)(2,1)S(1)}, bf16[1,64,768]{2,1,0:T(8,128)(2,1)S(1)}, u32[]{:S(2)}, u32[]{:S(2)}) collective-permute-start(bf16[1,64,768]{2,1,0:T(8,128)(2,1)S(1)} %maximum_bitcast_fusion), channel_id=1, source_target_pairs={{0,16},{1,17},{2,18},{3,19},{4,20},{5,21},{6,22},{7,23},{8,24},{9,... | collective-permute-start | bytes 294920 | tf_op jit(solution)/shard_map/ppermute | solution.py:406
  11.7 6.1 %collective-permute-start.8 = (bf16[2,64,768]{2,1,0:T(8,128)(2,1)S(1)}, bf16[2,64,768]{2,1,0:T(8,128)(2,1)S(1)}, u32[]{:S(2)}, u32[]{:S(2)}) collective-permute-start(bf16[2,64,768]{2,1,0:T(8,128)(2,1)S(1)} %pad_maximum_fusion.2), channel_id=1, source_target_pairs={{0,8},{1,9},{2,10},{3,11},{4,12},{5,13},{6,14},{7,15},{8,0},{9,1},... | collective-permute-start | bytes 589832 | tf_op jit(solution)/shard_map/ppermute | solution.py:406
  17.9 39.2 %copy-start.27 = (s32[3]{0:T(128)S(1)}, s32[3]{0:T(128)}, u32[]{:S(2)}) copy-start(s32[3]{0:T(128)} %param.32) | copy-start | bytes 40
  17.9 7.8 %collective-permute-start.9 = (bf16[4,64,768]{2,1,0:T(8,128)(2,1)S(1)}, bf16[4,64,768]{2,1,0:T(8,128)(2,1)S(1)}, u32[]{:S(2)}, u32[]{:S(2)}) collective-permute-start(bf16[4,64,768]{2,1,0:T(8,128)(2,1)S(1)} %pad_maximum_fusion.1), channel_id=1, source_target_pairs={{0,4},{1,3},{2,6},{3,1},{4,0},{5,7},{6,2},{7,5},{8,12},{9,11},{10,... | collective-permute-start | bytes 1179656 | tf_op jit(solution)/shard_map/ppermute | solution.py:406
  26.7 12.3 %collective-permute-start.10 = (bf16[8,64,768]{2,1,0:T(8,128)(2,1)}, bf16[8,64,768]{2,1,0:T(8,128)(2,1)}, u32[]{:S(2)}, u32[]{:S(2)}) collective-permute-start(bf16[8,64,768]{2,1,0:T(8,128)(2,1)} %pad_maximum_fusion.refs_0_), channel_id=1, source_target_pairs={{0,2},{1,5},{2,0},{3,7},{4,6},{5,1},{6,4},{7,3},{8,10},{9,13},{10,... | collective-permute-start | bytes 2359304 | tf_op jit(solution)/shard_map/ppermute | solution.py:406
  27.9 43.4 %collective-permute-start.11 = (bf16[8,64,768]{2,1,0:T(8,128)(2,1)}, bf16[8,64,768]{2,1,0:T(8,128)(2,1)}, u32[]{:S(2)}, u32[]{:S(2)}) collective-permute-start(bf16[8,64,768]{2,1,0:T(8,128)(2,1)} %pad_maximum_fusion.refs_0_), channel_id=1, source_target_pairs={{0,1},{1,0},{2,3},{3,2},{4,5},{5,4},{6,7},{7,6},{8,9},{9,8},{10,11... | collective-permute-start | bytes 2359304 | tf_op jit(solution)/shard_map/ppermute | solution.py:406
  39.0 32.3 %collective-permute-start.12 = (bf16[8,64,768]{2,1,0:T(8,128)(2,1)}, bf16[8,64,768]{2,1,0:T(8,128)(2,1)}, u32[]{:S(2)}, u32[]{:S(2)}) collective-permute-start(bf16[8,64,768]{2,1,0:T(8,128)(2,1)} %collective-permute-done.10.refs_1_), channel_id=1, source_target_pairs={{0,1},{1,0},{2,3},{3,2},{4,5},{5,4},{6,7},{7,6},{8,9},{9,8},{10,11... | collective-permute-start | bytes 2359304 | tf_op jit(solution)/shard_map/ppermute | solution.py:406
  39.9 1.8 %collective-permute-start = (f32[16,512]{1,0:T(8,128)S(1)}, f32[16,512]{1,0:T(8,128)S(1)}, u32[]{:S(2)}, u32[]{:S(2)}) collective-permute-start(f32[16,512]{1,0:T(8,128)S(1)} %dynamic_update_slice.7), channel_id=1, source_target_pairs={{0,1},{1,0},{2,3},{3,2},{4,5},{5,4},{6,7},{7,6},{8,9},{9,8},{10,11... | collective-permute-start | bytes 98312 | tf_op jit(solution)/shard_map/ppermute | solution.py:406
  41.7 3.9 %collective-permute-start.1 = (f32[16,512]{1,0:T(8,128)S(1)}, f32[16,512]{1,0:T(8,128)S(1)}, u32[]{:S(2)}, u32[]{:S(2)}) collective-permute-start(f32[16,512]{1,0:T(8,128)S(1)} %add.228), channel_id=1, source_target_pairs={{0,2},{1,3},{2,0},{3,1},{4,6},{5,7},{6,4},{7,5},{8,10},{9,11},{10,... | collective-permute-start | bytes 98312 | tf_op jit(solution)/shard_map/ppermute | solution.py:406
  45.6 3.9 %collective-permute-start.2 = (f32[16,512]{1,0:T(8,128)S(1)}, f32[16,512]{1,0:T(8,128)S(1)}, u32[]{:S(2)}, u32[]{:S(2)}) collective-permute-start(f32[16,512]{1,0:T(8,128)S(1)} %add.229), channel_id=1, source_target_pairs={{0,4},{1,5},{2,6},{3,7},{4,0},{5,1},{6,2},{7,3},{8,12},{9,13},{10,... | collective-permute-start | bytes 98312 | tf_op jit(solution)/shard_map/ppermute | solution.py:406
  49.5 4.1 %collective-permute-start.3 = (f32[16,512]{1,0:T(8,128)S(1)}, f32[16,512]{1,0:T(8,128)S(1)}, u32[]{:S(2)}, u32[]{:S(2)}) collective-permute-start(f32[16,512]{1,0:T(8,128)S(1)} %add.230), channel_id=1, source_target_pairs={{0,8},{1,9},{2,10},{3,11},{4,12},{5,13},{6,14},{7,15},{8,0},{9,1},... | collective-permute-start | bytes 98312 | tf_op jit(solution)/shard_map/ppermute | solution.py:406
  51.0 7.9 %collective-permute-start.5 = (bf16[3,2,8,512]{3,2,1,0:T(8,128)(2,1)S(1)}, bf16[3,2,8,512]{3,2,1,0:T(8,128)(2,1)S(1)}, u32[]{:S(2)}, u32[]{:S(2)}) collective-permute-start(bf16[3,2,8,512]{3,2,1,0:T(8,128)(2,1)S(1)} %get-tuple-element.123), channel_id=1, source_target_pairs={{0,1},{1,2},{2,3},{4,5},{5,6},{6,7},{8,9},{9,10},{10,11},{12,13},{... | collective-permute-start | bytes 147464 | tf_op jit(solution)/shard_map/ppermute | solution.py:428
  52.3 6.6 %collective-permute-start.6 = (bf16[3,2,8,512]{3,2,1,0:T(8,128)(2,1)S(1)}, bf16[3,2,8,512]{3,2,1,0:T(8,128)(2,1)S(1)}, u32[]{:S(2)}, u32[]{:S(2)}) collective-permute-start(bf16[3,2,8,512]{3,2,1,0:T(8,128)(2,1)S(1)} %get-tuple-element.122), channel_id=1, source_target_pairs={{1,0},{2,1},{3,2},{5,4},{6,5},{7,6},{9,8},{10,9},{11,10},{13,12},{... | collective-permute-start | bytes 147464 | tf_op jit(solution)/shard_map/ppermute | solution.py:429
  53.7 5.3 %collective-permute-start.4 = (f32[16,512]{1,0:T(8,128)S(1)}, f32[16,512]{1,0:T(8,128)S(1)}, u32[]{:S(2)}, u32[]{:S(2)}) collective-permute-start(f32[16,512]{1,0:T(8,128)S(1)} %add.231), channel_id=1, source_target_pairs={{0,16},{1,17},{2,18},{3,19},{4,20},{5,21},{6,22},{7,23},{8,24},{9,... | collective-permute-start | bytes 98312 | tf_op jit(solution)/shard_map/ppermute | solution.py:406
  85.6 14.8 %collective-permute-start.18 = (bf16[16,64,768]{2,1,0:T(8,128)(2,1)}, bf16[16,64,768]{2,1,0:T(8,128)(2,1)}, u32[]{:S(2)}, u32[]{:S(2)}) collective-permute-start(bf16[16,64,768]{2,1,0:T(8,128)(2,1)} %get-tuple-element.81), channel_id=1, source_target_pairs={{0,1},{1,0},{2,3},{3,2},{4,5},{5,4},{6,7},{7,6},{8,9},{9,8},{10,11... | collective-permute-start | bytes 4718600 | tf_op jit(solution)/shard_map/ppermute | solution.py:406
  103.5 34.2 %collective-permute-start.19 = (bf16[8,64,768]{2,1,0:T(8,128)(2,1)}, bf16[8,64,768]{2,1,0:T(8,128)(2,1)}, u32[]{:S(2)}, u32[]{:S(2)}) collective-permute-start(bf16[8,64,768]{2,1,0:T(8,128)(2,1)} %get-tuple-element.119), channel_id=1, source_target_pairs={{0,2},{1,5},{2,0},{3,7},{4,6},{5,1},{6,4},{7,3},{8,10},{9,13},{10,... | collective-permute-start | bytes 2359304 | tf_op jit(solution)/shard_map/ppermute | solution.py:406
  119.9 1.3 collective-permute-start.13
  121.1 3.9 %collective-permute-start.14 = (f32[16,512]{1,0:T(8,128)S(1)}, f32[16,512]{1,0:T(8,128)S(1)}, u32[]{:S(2)}, u32[]{:S(2)}) collective-permute-start(f32[16,512]{1,0:T(8,128)S(1)} %add.233), channel_id=1, source_target_pairs={{0,2},{1,3},{2,0},{3,1},{4,6},{5,7},{6,4},{7,5},{8,10},{9,11},{10,... | collective-permute-start | bytes 98312 | tf_op jit(solution)/shard_map/ppermute | solution.py:406
  125.1 3.9 %collective-permute-start.15 = (f32[16,512]{1,0:T(8,128)S(1)}, f32[16,512]{1,0:T(8,128)S(1)}, u32[]{:S(2)}, u32[]{:S(2)}) collective-permute-start(f32[16,512]{1,0:T(8,128)S(1)} %add.234), channel_id=1, source_target_pairs={{0,4},{1,5},{2,6},{3,7},{4,0},{5,1},{6,2},{7,3},{8,12},{9,13},{10,... | collective-permute-start | bytes 98312 | tf_op jit(solution)/shard_map/ppermute | solution.py:406
  129.0 3.9 %collective-permute-start.16 = (f32[16,512]{1,0:T(8,128)S(1)}, f32[16,512]{1,0:T(8,128)S(1)}, u32[]{:S(2)}, u32[]{:S(2)}) collective-permute-start(f32[16,512]{1,0:T(8,128)S(1)} %add.235), channel_id=1, source_target_pairs={{0,8},{1,9},{2,10},{3,11},{4,12},{5,13},{6,14},{7,15},{8,0},{9,1},... | collective-permute-start | bytes 98312 | tf_op jit(solution)/shard_map/ppermute | solution.py:406
  132.9 4.8 %collective-permute-start.17 = (f32[16,512]{1,0:T(8,128)S(1)}, f32[16,512]{1,0:T(8,128)S(1)}, u32[]{:S(2)}, u32[]{:S(2)}) collective-permute-start(f32[16,512]{1,0:T(8,128)S(1)} %add.236), channel_id=1, source_target_pairs={{0,16},{1,17},{2,18},{3,19},{4,20},{5,21},{6,22},{7,23},{8,24},{9,... | collective-permute-start | bytes 98312 | tf_op jit(solution)/shard_map/ppermute | solution.py:406
  139.4 7.8 %collective-permute-start.20 = (bf16[4,64,768]{2,1,0:T(8,128)(2,1)S(1)}, bf16[4,64,768]{2,1,0:T(8,128)(2,1)S(1)}, u32[]{:S(2)}, u32[]{:S(2)}) collective-permute-start(bf16[4,64,768]{2,1,0:T(8,128)(2,1)S(1)} %get-tuple-element.121), channel_id=1, source_target_pairs={{0,4},{1,3},{2,6},{3,1},{4,0},{5,7},{6,2},{7,5},{8,12},{9,11},{10,... | collective-permute-start | bytes 1179656 | tf_op jit(solution)/shard_map/ppermute | solution.py:406
  147.3 6.7 %collective-permute-start.21 = (bf16[2,64,768]{2,1,0:T(8,128)(2,1)S(1)}, bf16[2,64,768]{2,1,0:T(8,128)(2,1)S(1)}, u32[]{:S(2)}, u32[]{:S(2)}) collective-permute-start(bf16[2,64,768]{2,1,0:T(8,128)(2,1)S(1)} %get-tuple-element.125), channel_id=1, source_target_pairs={{0,8},{1,9},{2,10},{3,11},{4,12},{5,13},{6,14},{7,15},{8,0},{9,1},... | collective-permute-start | bytes 589832 | tf_op jit(solution)/shard_map/ppermute | solution.py:406
  154.1 6.3 %collective-permute-start.22 = (bf16[1,64,768]{2,1,0:T(8,128)(2,1)S(1)}, bf16[1,64,768]{2,1,0:T(8,128)(2,1)S(1)}, u32[]{:S(2)}, u32[]{:S(2)}) collective-permute-start(bf16[1,64,768]{2,1,0:T(8,128)(2,1)S(1)} %add_convert_fusion.6), channel_id=1, source_target_pairs={{0,16},{1,17},{2,18},{3,19},{4,20},{5,21},{6,22},{7,23},{8,24},{9,... | collective-permute-start | bytes 294920 | tf_op jit(solution)/shard_map/ppermute | solution.py:406
  (39 other events, 513.2 us)

commit v2 on v1

v2 whole, which is shorter than its diff:
```python
import functools

import jax
import jax.numpy as jnp
from jax import lax
from jax.experimental import pallas as pl
from jax.experimental.pallas import tpu as pltpu
from jax.sharding import PartitionSpec as P


STEP = 4


norm_eps = 1e-06
learn_rate = 0.05
first_decay = 0.9
second_decay = 0.999
adam_eps = 1e-08
weight_decay = 0.1
update_flags = (False, False, True, False, False, False, False, False, True)

LANES = 128
EDGE = 8
HALO = 2 * EDGE
CHUNK = 16
MIB = 1 << 20

f32 = jnp.float32
bf16 = jnp.bfloat16


def adam_step(weights_now, gradient, moment, square, step_number):
    next_moment = first_decay * moment + (1.0 - first_decay) * gradient
    next_square = second_decay * square + (1.0 - second_decay) * gradient * gradient
    first_fix = 1.0 - jnp.power(jnp.float32(first_decay), step_number)
    second_fix = 1.0 - jnp.power(jnp.float32(second_decay), step_number)
    step_ratio = next_moment / first_fix / (jnp.sqrt(next_square / second_fix) + adam_eps)
    update = -(learn_rate * (step_ratio + weight_decay * weights_now))
    return (weights_now + update, next_moment, next_square, update)


def vmem():
    return pl.BlockSpec(memory_space=pltpu.VMEM)


def smem():
    return pl.BlockSpec(memory_space=pltpu.SMEM)


FAST_MASKS = ((16, 8, 4, 2), (16, 8, 2, 4))


def position(core, dp_rel, x_rel):
    high, low, y = (dp_rel >> 2) & 1, (dp_rel >> 1) & 1, dp_rel & 1
    pair = (y | (x_rel << 1)) if core == 0 else (x_rel | (y << 1))
    return high | (low << 1) | (pair << 2)


def fill_shifted(s, lengths_ref, start, frames_get, left_get, right_get, sh, quarter, width):
    length = lengths_ref[s]
    zeros = jnp.zeros((EDGE, LANES), f32)
    blocks = width // LANES

    def masked(rows, first):
        place = lax.broadcasted_iota(jnp.int32, (rows.shape[0], LANES), 0) + first
        return lambda part: jnp.where(place < length, part, 0.0)

    left, right = left_get().astype(f32), right_get().astype(f32)
    mask_left, mask_right = masked(left, start - EDGE), masked(right, start + quarter)
    for j in range(blocks):
        lane = slice(j * LANES, (j + 1) * LANES)
        sh[j, 0:EDGE, :] = zeros
        sh[j, EDGE : 2 * EDGE, :] = mask_left(left[:, lane])
        sh[j, 2 * EDGE + quarter : 3 * EDGE + quarter, :] = mask_right(right[:, lane])
        sh[j, 3 * EDGE + quarter : 4 * EDGE + quarter, :] = zeros

    def step(i, _):
        row = pl.multiple_of(i * CHUNK, CHUNK)
        part = frames_get(row).astype(f32)
        mask = masked(part, start + row)
        for j in range(blocks):
            sh[j, pl.ds(row + 2 * EDGE, CHUNK), :] = mask(part[:, j * LANES : (j + 1) * LANES])
        return 0

    lax.fori_loop(0, quarter // CHUNK, step, 0)


GROUP = 4


def front_kernel(slots, quarter, width, taps, ints, frames, cot, left, right, params,
                 normed, unit, bg, normed_t, bg_t, bg_sum, sh):
    half = taps // 2
    blocks = width // LANES
    own_rows = slots * quarter
    start = ints[slots]

    def lanes(j):
        return slice(j * LANES, (j + 1) * LANES)

    def put_rows(chunks):
        conv = []
        for _, pieces in chunks:
            conv.append([])
            for j in range(blocks):
                parts = []
                for first, rows in pieces:
                    acc = jnp.broadcast_to(params[taps : taps + 1, lanes(j)], (rows, LANES))
                    for k in range(taps):
                        acc = acc + sh[j, pl.ds(first + k - half, rows), :] * params[k : k + 1, lanes(j)]
                    parts.append(acc)
                conv[-1].append(parts[0] if len(parts) == 1 else jnp.concatenate(parts, axis=0))
        means = [jnp.sum(functools.reduce(jnp.add, c), axis=1, keepdims=True) * (1.0 / width) for c in conv]
        conv = [[part - mean for part in c] for c, mean in zip(conv, means)]
        spread = [
            jnp.sum(functools.reduce(jnp.add, [part * part for part in c]), axis=1, keepdims=True) * (1.0 / width)
            for c in conv
        ]
        inverses = [lax.rsqrt(v + norm_eps) for v in spread]
        for (row, _), c, inverse in zip(chunks, conv, inverses):
            rows = pl.ds(row, CHUNK)
            unit[rows, lanes(blocks)] = jnp.broadcast_to(inverse, (CHUNK, LANES))
            for j in range(blocks):
                part = c[j] * inverse
                unit[rows, lanes(j)] = part
                normed[rows, lanes(j)] = (
                    part * params[taps + 1 : taps + 2, lanes(j)] + params[taps + 2 : taps + 3, lanes(j)]
                ).astype(bf16)

    bg_sum[...] = jnp.zeros_like(bg_sum)
    for s in range(slots):
        length = ints[s]
        fill_shifted(
            s, ints, start,
            lambda row: frames[s, pl.ds(row, CHUNK), :],
            lambda: left[s, 0], lambda: right[s, 0], sh, quarter, width,
        )

        def step(i, _):
            chunks = []
            for u in range(GROUP):
                row = pl.multiple_of(i * (GROUP * CHUNK) + u * CHUNK, CHUNK)
                chunks.append((pl.multiple_of(s * quarter + row, CHUNK), [(row + 2 * EDGE, CHUNK)]))
            put_rows(chunks)
            total = None
            for u in range(GROUP):
                row = pl.multiple_of(i * (GROUP * CHUNK) + u * CHUNK, CHUNK)
                place = lax.broadcasted_iota(jnp.int32, (CHUNK, width), 0) + (start + row)
                back = jnp.where(place < length, cot[s, pl.ds(row, CHUNK), :].astype(f32), 0.0)
                low = (back * params[taps + 4 : taps + 5, :]).astype(bf16)
                bg[pl.ds(pl.multiple_of(s * quarter + row, CHUNK), CHUNK), :] = low
                wide = low.astype(f32)
                wide = wide[0:8] + wide[8:16]
                total = wide if total is None else total + wide
            bg_sum[...] += total
            return 0

        lax.fori_loop(0, quarter // (GROUP * CHUNK), step, 0)
        tail = own_rows + s * HALO
        put_rows([(tail, [(EDGE, EDGE), (2 * EDGE + quarter, EDGE)])])
        edge = jnp.concatenate([left[s, 1].astype(f32), right[s, 1].astype(f32)], axis=0)
        ids = lax.broadcasted_iota(jnp.int32, (HALO, width), 0)
        place = jnp.where(ids < EDGE, start - EDGE + ids, start + quarter - EDGE + ids)
        back = jnp.where(place < length, edge, 0.0)
        bg[tail : tail + HALO, :] = (back * params[taps + 4 : taps + 5, :]).astype(bf16)
        own = slice(s * quarter, (s + 1) * quarter)
        normed_t[:, own] = normed[own, :].T
        bg_t[:, own] = bg[own, :].T


TILE = 256


def hidden_kernel(slots, taps, dp_count, own_width, own_rows, fast, ints, normed, bg, normed_t, bg_t, params, *refs):
    sources, refs = (refs[:4], refs[4:]) if fast else (refs[:2], refs[2:])
    act, hg, *grads, bias_grad, up, down, hid_a, hid_b, pull_a, pull_b = refs
    all_rows, width = normed.shape
    wide = 2 * own_width
    rows_dp = width // dp_count
    dp_own, core = ints[slots + 1], ints[slots + 2]

    if fast:
        for n in range(2):
            for c in range(2):
                @pl.when(core == c)
                def _():
                    for dp_rel in range(dp_count):
                        rows = pl.ds(pl.multiple_of((dp_rel ^ dp_own) * rows_dp, rows_dp), rows_dp)
                        for x_rel in range(2):
                            place = position(c ^ n, dp_rel, x_rel)
                            source = sources[2 * n + (place >> 3)]
                            columns = slice(n * wide + x_rel * own_width, n * wide + (x_rel + 1) * own_width)
                            up[rows, columns] = source[place & 7, :, 0:own_width]
                            down[rows, columns] = source[place & 7, :, own_width : 2 * own_width]
    else:
        up[...] = sources[0][...]
        down[...] = sources[1][...]

    base = taps + 5
    bias = [
        jnp.concatenate(
            [params[pl.ds(base + ints[slots + 3 + 2 * n + x], 1), 0:own_width] for x in range(2)], axis=1
        )
        for n in range(2)
    ]
    thirds = [slice(k * (own_rows // 3), (k + 1) * (own_rows // 3)) for k in range(3)]
    thirds[2] = slice(thirds[2].start, all_rows)
    stages = [(n, rows) for n in (1, 0) for rows in thirds]

    def products(k):
        n, rows = stages[k]
        count = rows.stop - rows.start
        hid, pull = ((hid_a, pull_a), (hid_b, pull_b))[k % 2]

        def one(out, left, right, column):
            columns = slice(n * wide + column, n * wide + column + TILE)
            out[0:count, column : column + TILE] = jnp.dot(left[rows, :], right[:, columns], preferred_element_type=f32)

        return [
            functools.partial(one, out, left, right, column)
            for column in range(0, wide, TILE)
            for out, left, right in ((hid, normed, up), (pull, bg, down))
        ]

    def elementwise(k):
        n, rows = stages[k]
        count = rows.stop - rows.start
        hid, pull = ((hid_a, pull_a), (hid_b, pull_b))[k % 2]

        def one(sub, column):
            source = (slice(sub, sub + CHUNK), slice(column, column + TILE))
            first = rows.start + sub
            place = (slice(first, first + CHUNK), slice(n * wide + column, n * wide + column + TILE))
            v = hid[source] + bias[n][:, column : column + TILE]
            fall = jnp.exp2(v * v * (-0.5 * 1.4426950408889634))
            t = 1.0 / (1.0 + jnp.abs(v) * (0.3275911 * 0.7071067811865476))
            tail = 0.5 * -1.453152027 + t * (0.5 * 1.061405429)
            tail = 0.5 * 1.421413741 + t * tail
            tail = 0.5 * -0.284496736 + t * tail
            tail = 0.5 * 0.254829592 + t * tail
            tail = t * tail * fall
            below = jnp.where(v < 0.0, tail, 1.0 - tail)
            if first < own_rows:
                act[place] = (v * below).astype(bf16)
            slope = below + v * (fall * 0.3989422804014327)
            hg[place] = (pull[source] * slope).astype(bf16)

        return [
            functools.partial(one, sub, column) for column in range(0, wide, TILE) for sub in range(0, count, CHUNK)
        ]

    def weight_grads(n):
        def one(which, row, column):
            columns = slice(n * wide + column, n * wide + column + TILE)
            left, right = ((normed_t, hg), (bg_t, act))[which]
            value = jnp.dot(left[row : row + TILE, :], right[0:own_rows, columns], preferred_element_type=f32)
            if not fast:
                grads[0][which, row : row + TILE, columns] = value
                return
            value = value.astype(bf16)
            for dp in range(row // rows_dp, (row + TILE) // rows_dp):
                dp_rel = dp ^ dp_own
                high, low, y = (dp_rel >> 2) & 1, (dp_rel >> 1) & 1, dp_rel & 1
                owner = core ^ n
                for x in range(2):
                    first, last = max(column, x * own_width), min(column + TILE, (x + 1) * own_width)
                    if first >= last:
                        continue
                    place = high + 2 * low + 4 * (y * (1 + owner) + x * (2 - owner))
                    out = slice(which * own_width + first - x * own_width, which * own_width + last - x * own_width)
                    grads[n][place, :, out] = value[
                        dp * rows_dp - row : (dp + 1) * rows_dp - row, first - column : last - column
                    ]

        def sums():
            columns = slice(n * wide, (n + 1) * wide)
            bias_grad[:, columns] = jnp.dot(
                jnp.ones((8, own_rows), bf16), hg[0:own_rows, columns], preferred_element_type=f32
            )

        pieces = [
            functools.partial(one, which, row, column)
            for column in range(0, wide, TILE)
            for which in range(2)
            for row in range(0, width, TILE)
        ]
        return pieces + [sums]

    def run(matrix, vector):
        done = 0
        for k, piece in enumerate(matrix):
            piece()
            upto = len(vector) * (k + 1) // len(matrix)
            for other in vector[done:upto]:
                other()
            done = upto

    run(products(0), [])
    run(products(1), elementwise(0))
    run(products(2), elementwise(1))
    run(products(3), elementwise(2))
    grads_1 = weight_grads(1)
    run(products(4) + grads_1[:6], elementwise(3))
    run(products(5) + grads_1[6:], elementwise(4))
    for piece in elementwise(5):
        piece()
    run(weight_grads(0), [])


NT = (((1,), (1,)), ((), ()))


def output_kernel(slots, quarter, width, taps, ints, params, act, down, frames, cot, output, scale_sum, branch):
    s = pl.program_id(0)
    start, length = ints[slots], ints[s]

    @pl.when(s == 0)
    def _():
        scale_sum[...] = jnp.zeros_like(scale_sum)

    own = pl.ds(pl.multiple_of(s * quarter, CHUNK), quarter)
    branch[...] = lax.dot_general(act[own, :], down[...], NT, preferred_element_type=f32)

    def step(i, total_sum):
        row = pl.multiple_of(i * CHUNK, CHUNK)
        rows = pl.ds(row, CHUNK)
        live = lax.broadcasted_iota(jnp.int32, (CHUNK, width), 0) + (start + row) < length
        back = jnp.where(live, cot[0, rows, :].astype(f32), 0.0)
        total = branch[rows, :] + params[taps + 3 : taps + 4, :]
        shown = frames[0, rows, :].astype(f32) + params[taps + 4 : taps + 5, :] * total
        output[0, rows, :] = jnp.where(live, shown, 0.0)
        part = back * total
        return total_sum + (part[0:8] + part[8:16])

    scale_sum[...] += lax.fori_loop(0, quarter // CHUNK, step, jnp.zeros((8, width), f32))


def back_kernel(shape, ints, params, left, right, hg, up, unit, bias_grad, bg_sum, scale_sum,
                frames, cot, input_grad, small, sh, cgs, ngs, ng_halo, acc):
    slots, quarter, width, taps, own_width = shape
    half = taps // 2
    blocks = width // LANES
    own_rows = slots * quarter
    s = pl.program_id(0)
    start = ints[slots]
    length = ints[s]

    def lanes(j):
        return slice(j * LANES, (j + 1) * LANES)

    def product(rows):
        return lax.dot_general(hg[rows, :], up[...], NT, preferred_element_type=f32)

    @pl.when(s == 0)
    def _():
        acc[...] = jnp.zeros_like(acc)
        ng_halo[...] = product(pl.ds(own_rows, slots * HALO))

    fill_shifted(
        s, ints, start, lambda row: frames[0, pl.ds(row, CHUNK), :],
        lambda: left[s, 0], lambda: right[s, 0], sh, quarter, width,
    )
    ngs[...] = product(pl.ds(pl.multiple_of(s * quarter, CHUNK), quarter))

    def norm_back(chunks):
        units, scales, firsts, seconds = [], [], [], []
        for ng, rows in chunks:
            u = [unit[rows, lanes(j)] for j in range(blocks)]
            scaled = [ng[j] * params[taps + 1 : taps + 2, lanes(j)] for j in range(blocks)]
            units.append(u)
            scales.append(scaled)
            firsts.append(functools.reduce(jnp.add, scaled))
            seconds.append(functools.reduce(jnp.add, [a * b for a, b in zip(scaled, u)]))
        firsts = [jnp.sum(v, axis=1, keepdims=True) * (1.0 / width) for v in firsts]
        seconds = [jnp.sum(v, axis=1, keepdims=True) * (1.0 / width) for v in seconds]
        grads = []
        for (_, rows), u, scaled, first, second in zip(chunks, units, scales, firsts, seconds):
            inverse = unit[rows, lanes(blocks)]
            grads.append([inverse * (scaled[j] - first - u[j] * second) for j in range(blocks)])
        return units, grads

    def fold(value):
        return value[0:8] + value[8:16]

    def norm_step(i, _):
        firsts = [pl.multiple_of(i * (2 * CHUNK) + u * CHUNK, CHUNK) for u in range(2)]
        ngs_here = [[ngs[pl.ds(row, CHUNK), lanes(j)] for j in range(blocks)] for row in firsts]
        units, grads = norm_back(
            [(ng, pl.ds(pl.multiple_of(s * quarter + row, CHUNK), CHUNK)) for ng, row in zip(ngs_here, firsts)]
        )
        for j in range(blocks):
            for row, cg in zip(firsts, grads):
                cgs[j, pl.ds(row + 2 * EDGE, CHUNK), :] = cg[j]
            acc[taps + 1, :, lanes(j)] += functools.reduce(jnp.add, [fold(ng[j] * u[j]) for ng, u in zip(ngs_here, units)])
            acc[taps + 2, :, lanes(j)] += functools.reduce(jnp.add, [fold(ng[j]) for ng in ngs_here])
            acc[taps, :, lanes(j)] += functools.reduce(jnp.add, [fold(cg[j]) for cg in grads])
        return 0

    lax.fori_loop(0, quarter // (2 * CHUNK), norm_step, 0)
    tail = pl.multiple_of(s * HALO, HALO)
    ng = [ng_halo[pl.ds(tail, HALO), lanes(j)] for j in range(blocks)]
    _, (cg,) = norm_back([(ng, pl.ds(pl.multiple_of(own_rows + tail, HALO), HALO))])
    for j in range(blocks):
        cgs[j, 0:EDGE, :] = jnp.zeros((EDGE, LANES), f32)
        cgs[j, EDGE : 2 * EDGE, :] = cg[j][0:EDGE]
        cgs[j, 2 * EDGE + quarter : 3 * EDGE + quarter, :] = cg[j][EDGE:HALO]
        cgs[j, 3 * EDGE + quarter : 4 * EDGE + quarter, :] = jnp.zeros((EDGE, LANES), f32)

    for j in range(blocks):
        def conv_step(i, sums):
            row = pl.multiple_of(i * CHUNK, CHUNK)
            rows = pl.ds(row, CHUNK)
            live = lax.broadcasted_iota(jnp.int32, (CHUNK, LANES), 0) + (start + row) < length
            back = jnp.where(live, cot[0, rows, lanes(j)].astype(f32), 0.0)
            first = row + 2 * EDGE
            here = cgs[j, pl.ds(first, CHUNK), :]
            pulled = jnp.zeros((CHUNK, LANES), f32)
            out = []
            for k in range(taps):
                pulled = pulled + cgs[j, pl.ds(first + half - k, CHUNK), :] * params[k : k + 1, lanes(j)]
                out.append(sums[k] + fold(here * sh[j, pl.ds(first + k - half, CHUNK), :]))
            input_grad[0, rows, lanes(j)] = back + jnp.where(live, pulled, 0.0)
            return tuple(out)

        sums = lax.fori_loop(
            0, quarter // CHUNK, conv_step, tuple(jnp.zeros((8, LANES), f32) for _ in range(taps))
        )
        for k in range(taps):
            acc[k, :, lanes(j)] += sums[k]

    @pl.when(s == slots - 1)
    def _():
        small[...] = jnp.zeros_like(small)
        for k in range(taps + 3):
            small[k : k + 1, :] = jnp.sum(acc[k], axis=0, keepdims=True)
        small[taps + 3 : taps + 4, :] = jnp.sum(bg_sum[...], axis=0, keepdims=True)
        small[taps + 4 : taps + 5, :] = jnp.sum(scale_sum[...], axis=0, keepdims=True)
        for x in range(4):
            place = ints[slots + 3 + x]
            small[pl.ds(taps + 5 + place, 1), 0:own_width] = bias_grad[0:1, x * own_width : (x + 1) * own_width]


def call(kernel, outs, in_specs, scratch, limit, flops=0, moved=0, grid=None, out_specs=None):
    grid_spec = pltpu.PrefetchScalarGridSpec(
        num_scalar_prefetch=0,
        grid=grid or (),
        in_specs=in_specs,
        out_specs=out_specs or [vmem()] * len(outs),
        scratch_shapes=scratch,
    )
    return pl.pallas_call(
        kernel,
        out_shape=[jax.ShapeDtypeStruct(shape, dtype) for shape, dtype in outs],
        grid_spec=grid_spec,
        compiler_params=pltpu.CompilerParams(vmem_limit_bytes=limit * MIB),
        cost_estimate=pl.CostEstimate(flops=flops, bytes_accessed=moved, transcendentals=0),
    )


def per_device(
    dp_count,
    tp_count,
    frames,
    cotangent,
    lengths,
    conv_weight,
    conv_bias,
    norm_gain,
    norm_bias,
    up_weight,
    up_bias,
    down_weight,
    down_bias,
    layer_scale,
    moment_conv_weight,
    moment_conv_bias,
    moment_norm_gain,
    moment_norm_bias,
    moment_up_weight,
    moment_up_bias,
    moment_down_weight,
    moment_down_bias,
    moment_layer_scale,
    square_conv_weight,
    square_conv_bias,
    square_norm_gain,
    square_norm_bias,
    square_up_weight,
    square_up_bias,
    square_down_weight,
    square_down_bias,
    square_layer_scale,
):
    both = ("dp", "tp")
    count = dp_count * tp_count
    dp_own, tp_own = lax.axis_index("dp"), lax.axis_index("tp")
    own = dp_own * tp_count + tp_own
    slots, quarter, width = frames.shape
    own_channels, taps = conv_weight.shape
    own_bias = up_bias.shape[0]
    own_rows_w, own_width = up_weight.shape
    hidden_width = own_width * tp_count
    all_rows = slots * (quarter + HALO)
    own_rows = slots * quarter
    fast = (dp_count, tp_count) == (8, 4) and own_rows_w % CHUNK == 0
    core = own & 1

    def swap(value, masks):
        return lax.ppermute(value, both, [(i, i ^ masks[i & 1]) for i in range(count)])

    if fast:
        steps = [(FAST_MASKS[0][k], FAST_MASKS[1][k]) for k in range(4)]
        held = jnp.concatenate([up_weight.astype(bf16), down_weight.astype(bf16)], axis=1)[None]
        for k in range(3):
            arrived = swap(held, steps[k])
            held = jnp.concatenate([held, arrived], axis=0)
        far = swap(held, steps[3])
        other = swap(held, (1, 1))
        other_far = swap(far, (1, 1))
        weights = (held, far, other, other_far)
        blocks = [[tp_own ^ (2 * x + n) for x in range(2)] for n in range(2)]
    else:
        weights = [
            lax.all_gather(lax.all_gather(w.astype(bf16), "dp", axis=0, tiled=True), "tp", axis=1, tiled=True)
            for w in (up_weight, down_weight)
        ]
        blocks = [[jnp.int32(2 * n + x) for x in range(2)] for n in range(2)]

    pair = jnp.stack([frames, cotangent], axis=1)
    left = lax.ppermute(pair[:, :, quarter - EDGE :, :], "tp", [(i, i + 1) for i in range(tp_count - 1)])
    right = lax.ppermute(pair[:, :, :EDGE, :], "tp", [(i + 1, i) for i in range(tp_count - 1)])

    small_rows = taps + 5 + tp_count
    channels = jnp.concatenate(
        [conv_weight.T, conv_bias[None], norm_gain[None], norm_bias[None], down_bias[None], layer_scale[None]], axis=0
    )
    params = jnp.zeros((small_rows, width), f32)
    params = lax.dynamic_update_slice(params, channels, (0, own * own_channels))
    params = lax.dynamic_update_slice(
        params, up_bias[None], (taps + 5 + own * own_bias // own_width, own * own_bias % own_width)
    )
    bits = [1 << k for k in range(count.bit_length() - 1)]
    assert 1 << len(bits) == count

    def sum_all(value, order):
        for bit in order:
            arrived = swap(value, (bit, bit))
            value = value + arrived
        return value

    params = sum_all(params, bits)

    ints = jnp.stack(
        [*[lengths[s] for s in range(slots)], tp_own * quarter, dp_own, core, *blocks[0], *blocks[1]]
    ).astype(jnp.int32)

    front = call(
        functools.partial(front_kernel, slots, quarter, width, taps),
        [
            ((all_rows, width), bf16),
            ((all_rows, width + LANES), f32),
            ((all_rows, width), bf16),
            ((width, own_rows), bf16),
            ((width, own_rows), bf16),
            ((8, width), f32),
        ],
        [smem(), vmem(), vmem(), vmem(), vmem(), vmem()],
        [pltpu.VMEM((width // LANES, quarter + 4 * EDGE, LANES), f32)],
        4, flops=10 * all_rows * width * taps, moved=8 * all_rows * width,
    )
    normed, unit, bg, normed_t, bg_t, bg_sum = front(ints, frames, cotangent, left, right, params)

    wide = 2 * own_width
    grads_shape = (2 * dp_count, own_rows_w, wide)
    most = own_rows // 3 + all_rows - own_rows
    hidden = call(
        functools.partial(hidden_kernel, slots, taps, dp_count, own_width, own_rows, fast),
        [((own_rows, hidden_width), bf16), ((all_rows, hidden_width), bf16)]
        + ([(grads_shape, bf16)] * 2 if fast else [((2, width, hidden_width), f32)])
        + [((8, hidden_width), f32), ((width, hidden_width), bf16), ((width, hidden_width), bf16)],
        [smem()] + [vmem()] * (5 + len(weights)),
        [pltpu.VMEM((most, wide), f32)] * 4,
        10, flops=8 * all_rows * width * hidden_width, moved=8 * all_rows * hidden_width,
    )
    act, hg, *grads, bias_grad, up, down = hidden(ints, normed, bg, normed_t, bg_t, params, *weights)

    slot_spec = pl.BlockSpec((1, quarter, width), lambda s: (s, 0, 0))
    output = call(
        functools.partial(output_kernel, slots, quarter, width, taps),
        [((slots, quarter, width), f32), ((8, width), f32)],
        [smem(), vmem(), vmem(), vmem(), slot_spec, slot_spec],
        [pltpu.VMEM((quarter, width), f32)],
        8, flops=2 * own_rows * width * hidden_width, moved=8 * all_rows * width,
        grid=(slots,), out_specs=[slot_spec, vmem()],
    )
    output_own, scale_sum = output(ints, params, act, down, frames, cotangent)
    back = call(
        functools.partial(back_kernel, (slots, quarter, width, taps, own_width)),
        [((slots, quarter, width), f32), ((small_rows, width), f32)],
        [smem()] + [vmem()] * 9 + [slot_spec, slot_spec],
        [
            pltpu.VMEM((width // LANES, quarter + 4 * EDGE, LANES), f32),
            pltpu.VMEM((width // LANES, quarter + 4 * EDGE, LANES), f32),
            pltpu.VMEM((quarter, width), f32),
            pltpu.VMEM((slots * HALO, width), f32),
            pltpu.VMEM((taps + 5, 8, width), f32),
        ],
        8, flops=2 * all_rows * width * hidden_width, moved=8 * all_rows * width,
        grid=(slots,), out_specs=[slot_spec, vmem()],
    )
    input_own, small = back(ints, params, left, right, hg, up, unit, bias_grad, bg_sum, scale_sum, frames, cotangent)

    if fast:
        def plus(a, b):
            return (a.astype(f32) + b.astype(f32)).astype(bf16)

        arrived = swap(grads[1], (1, 1))
        keep, send = plus(grads[0][:8], arrived[:8]), plus(grads[0][8:], arrived[8:])
        for k in range(3, 0, -1):
            size = keep.shape[0] // 2
            arrived = swap(send, steps[k])
            send = plus(keep[size:], arrived[size:])
            keep = plus(keep[:size], arrived[:size])
        arrived = swap(send, steps[0])
        total = keep[0].astype(f32) + arrived[0].astype(f32)
        up_share, down_share = total[:, :own_width], total[:, own_width:]
    else:
        up_share, down_share = (
            lax.psum_scatter(
                lax.psum_scatter(grads[0][n], "tp", scatter_dimension=1, tiled=True),
                "dp", scatter_dimension=0, tiled=True,
            )
            for n in range(2)
        )

    small = sum_all(small, (1, 8, 2, 4, 16) if fast else bits)
    own_small = lax.dynamic_slice(small, (0, own * own_channels), (taps + 5, own_channels))
    share_up = lax.dynamic_slice(
        small, (taps + 5 + own * own_bias // own_width, own * own_bias % own_width), (1, own_bias)
    )[0]

    step_number = jnp.float32(STEP)
    params_own = (
        conv_weight,
        conv_bias,
        norm_gain,
        norm_bias,
        up_weight,
        up_bias,
        down_weight,
        down_bias,
        layer_scale,
    )
    gradients = (
        own_small[:taps].T,
        own_small[taps],
        own_small[taps + 1],
        own_small[taps + 2],
        up_share,
        share_up,
        down_share,
        own_small[taps + 3],
        own_small[taps + 4],
    )
    moments = (
        moment_conv_weight,
        moment_conv_bias,
        moment_norm_gain,
        moment_norm_bias,
        moment_up_weight,
        moment_up_bias,
        moment_down_weight,
        moment_down_bias,
        moment_layer_scale,
    )
    squares = (
        square_conv_weight,
        square_conv_bias,
        square_norm_gain,
        square_norm_bias,
        square_up_weight,
        square_up_bias,
        square_down_weight,
        square_down_bias,
        square_layer_scale,
    )
    flat = [output_own, input_own]
    for weights_now, gradient, moment, square, use_update in zip(
        params_own, gradients, moments, squares, update_flags
    ):
        next_weights, next_moment, next_square, update = adam_step(
            weights_now, gradient, moment, square, step_number
        )
        shown = update if use_update else next_weights
        flat = flat + [gradient, shown, next_moment, next_square]
    return tuple(flat)


def body(dp_count, tp_count, *args):
    return per_device(dp_count, tp_count, *args)


def solution(mesh):
    vector, matrix = P(("dp", "tp")), P("dp", "tp")
    taps = P(("dp", "tp"), None)
    frames = P("dp", "tp", None)
    parameters = (taps, vector, vector, vector, matrix, vector, matrix, vector, vector)
    return jax.shard_map(
        functools.partial(body, mesh.shape["dp"], mesh.shape["tp"]),
        mesh=mesh,
        in_specs=(frames, frames, P("dp")) + parameters * 3,
        out_specs=(frames, frames) + tuple(spec for spec in parameters for _ in range(4)),
        check_vma=False,
    )
```

time: 162 us -> 138 us (0.85)
  Pallas kernels: 43.5 us -> 28.6 us
  local copies, waits for them, and re-layouts: 10.6 us -> 1.1 us
  waiting for transfers between devices: 62.1 us -> 65.4 us
  other arithmetic: 11.3 us -> 8.48 us
    unnamed x96 -> x60, local copies, waits for them, and re-layouts: 9.46 us -> 0.17 us
    pallas_call x3, Pallas kernels: 32 us -> 23.8 us  [the longest x1 10.1 us: per_device(): back(ints, params, left, right, hg, up, unit, bias_grad, bg_sum, scale_su...]
    pallas_call x1, Pallas kernels: 11.5 us -> 4.88 us  [per_device(): front(ints, frames, cotangent, left, right, params)]
    ppermute x21, waiting for transfers between devices: 62.1 us -> 65.4 us  [swap(): lax.ppermute(value, both, [(i, i ^ masks[i & 1]) for i in range(count)])]
    convert_element_type x4, other arithmetic: 4.82 us -> 2.86 us  [plus(): return (a.astype(f32) + b.astype(f32)).astype(bf16)]
  transfers between devices with their start and end apart: 23 -> 23, of which waited for: 16 -> 17; matrix products, arithmetic and copies ran while one was open for 2% -> 3% of each run, Pallas kernels for 21% -> 14%
where the time goes in v2:
time: 138 us; the launch traced here: 137 us
  waiting for transfers between devices  65.4 us (47%)
  starting transfers between devices  32.6 us (24%)
  Pallas kernels  28.6 us (21%)
  other arithmetic  8.48 us (6%)
    ppermute x21, waiting for transfers between devices, swap(): lax.ppermute(value, both, [(i, i ^ masks[i & 1]) for i in range(count)])  65.4 us
    ppermute x21, starting transfers between devices, swap(): lax.ppermute(value, both, [(i, i ^ masks[i & 1]) for i in range(count)])  30 us
    pallas_call x1, Pallas kernels, per_device(): back(ints, params, left, right, hg, up, unit, bias_grad, bg_sum, scale_su...  10.1 us
    pallas_call x1, Pallas kernels, per_device(): hidden(ints, normed, bg, normed_t, bg_t, params, *weights)  9.69 us
    pallas_call x1, Pallas kernels, per_device(): front(ints, frames, cotangent, left, right, params)  4.88 us
    pallas_call x1, Pallas kernels, per_device(): output_own, scale_sum = output(ints, params, act, down, frames, cotangent)  3.96 us
    convert_element_type x4, other arithmetic, plus(): return (a.astype(f32) + b.astype(f32)).astype(bf16)  2.86 us
    add x4, other arithmetic, adam_step(): return (weights_now + update, next_moment, next_square, update)  2.84 us
  transfers between devices with their start and end apart: 23, of which 17 were waited for; matrix products, arithmetic and copies ran while one was open for 3% of the time, Pallas kernels for 14%

profile of v2, /device:TPU:0, one launch (start us, length us, event | category | flops | bytes accessed | tf_op | source)
XLA Modules:
  0.0 137.4 jit_solution(16782711014271408091)
XLA Ops:
  2.6 4.1 %collective-permute-start.7 = (bf16[1,64,768]{2,1,0:T(8,128)(2,1)S(1)}, bf16[1,64,768]{2,1,0:T(8,128)(2,1)S(1)}, u32[]{:S(2)}, u32[]{:S(2)}) collective-permute-start(bf16[1,64,768]{2,1,0:T(8,128)(2,1)S(1)} %maximum_bitcast_fusion), channel_id=1, source_target_pairs={{0,16},{1,17},{2,18},{3,19},{4,20},{5,21},{6,22},{7,23},{8,24},{9,... | collective-permute-start | bytes 294920 | tf_op jit(solution)/shard_map/ppermute | solution.py:509
  6.8 4.9 %collective-permute-done.7 = bf16[1,64,768]{2,1,0:T(8,128)(2,1)S(1)} collective-permute-done((bf16[1,64,768]{2,1,0:T(8,128)(2,1)S(1)}, bf16[1,64,768]{2,1,0:T(8,128)(2,1)S(1)}, u32[]{:S(2)}, u32[]{:S(2)}) %collective-permute-start.7) | collective-permute-done | bytes 98336 | tf_op jit(solution)/shard_map/ppermute | solution.py:509
  12.5 5.3 %collective-permute-done.8 = bf16[2,64,768]{2,1,0:T(8,128)(2,1)S(1)} collective-permute-done((bf16[2,64,768]{2,1,0:T(8,128)(2,1)S(1)}, bf16[2,64,768]{2,1,0:T(8,128)(2,1)S(1)}, u32[]{:S(2)}, u32[]{:S(2)}) %collective-permute-start.8) | collective-permute-done | bytes 196640 | tf_op jit(solution)/shard_map/ppermute | solution.py:509
  17.9 1.3 collective-permute-start.9
  19.2 6.5 %collective-permute-done.9 = bf16[4,64,768]{2,1,0:T(8,128)(2,1)S(1)} collective-permute-done((bf16[4,64,768]{2,1,0:T(8,128)(2,1)S(1)}, bf16[4,64,768]{2,1,0:T(8,128)(2,1)S(1)}, u32[]{:S(2)}, u32[]{:S(2)}) %collective-permute-start.9) | collective-permute-done | bytes 393248 | tf_op jit(solution)/shard_map/ppermute | solution.py:509
  25.8 1.3 collective-permute-start.10
  27.1 10.8 %collective-permute-done.10.refs_1_ = bf16[8,64,768]{2,1,0:T(8,128)(2,1)S(1)} collective-permute-done((bf16[8,64,768]{2,1,0:T(8,128)(2,1)S(1)}, bf16[8,64,768]{2,1,0:T(8,128)(2,1)S(1)}, u32[]{:S(2)}, u32[]{:S(2)}) %collective-permute-start.10) | collective-permute-done | bytes 786464 | tf_op jit(solution)/shard_map/ppermute | solution.py:509
  41.8 2.7 %collective-permute-done.1 = f32[16,512]{1,0:T(8,128)S(1)} collective-permute-done((f32[16,512]{1,0:T(8,128)S(1)}, f32[16,512]{1,0:T(8,128)S(1)}, u32[]{:S(2)}, u32[]{:S(2)}) %collective-permute-start.1) | collective-permute-done | bytes 32800 | tf_op jit(solution)/shard_map/ppermute | solution.py:509
  45.7 2.7 %collective-permute-done.2 = f32[16,512]{1,0:T(8,128)S(1)} collective-permute-done((f32[16,512]{1,0:T(8,128)S(1)}, f32[16,512]{1,0:T(8,128)S(1)}, u32[]{:S(2)}, u32[]{:S(2)}) %collective-permute-start.2) | collective-permute-done | bytes 32800 | tf_op jit(solution)/shard_map/ppermute | solution.py:509
  48.4 1.5 %collective-permute-start.3 = (f32[16,512]{1,0:T(8,128)S(1)}, f32[16,512]{1,0:T(8,128)S(1)}, u32[]{:S(2)}, u32[]{:S(2)}) collective-permute-start(f32[16,512]{1,0:T(8,128)S(1)} %add.230), channel_id=1, source_target_pairs={{0,8},{1,9},{2,10},{3,11},{4,12},{5,13},{6,14},{7,15},{8,0},{9,1},... | collective-permute-start | bytes 98312 | tf_op jit(solution)/shard_map/ppermute | solution.py:509
  52.5 3.4 %collective-permute-start.4 = (f32[16,512]{1,0:T(8,128)S(1)}, f32[16,512]{1,0:T(8,128)S(1)}, u32[]{:S(2)}, u32[]{:S(2)}) collective-permute-start(f32[16,512]{1,0:T(8,128)S(1)} %add.231), channel_id=1, source_target_pairs={{0,16},{1,17},{2,18},{3,19},{4,20},{5,21},{6,22},{7,23},{8,24},{9,... | collective-permute-start | bytes 98312 | tf_op jit(solution)/shard_map/ppermute | solution.py:509
  56.0 1.8 %collective-permute-done.4 = f32[16,512]{1,0:T(8,128)S(1)} collective-permute-done((f32[16,512]{1,0:T(8,128)S(1)}, f32[16,512]{1,0:T(8,128)S(1)}, u32[]{:S(2)}, u32[]{:S(2)}) %collective-permute-start.4) | collective-permute-done | bytes 32800 | tf_op jit(solution)/shard_map/ppermute | solution.py:509
  57.8 4.9 %shard_map.581 = (bf16[816,512]{1,0:T(8,128)(2,1)S(1)}, f32[816,640]{1,0:T(8,128)S(1)}, bf16[816,512]{1,0:T(8,128)(2,1)S(1)}, bf16[512,768]{1,0:T(8,128)(2,1)S(1...) custom-call(s32[10]{0:T(128)S(1)} %stack.40.ints, bf16[3,256,512]{2,1,0:T(8,128)(2,1)S(1)} %copy-done, ...), custom_call_target="tpu_custom_call" | custom-call | flops 29245440 | bytes 3342336 | tf_op jit(solution)/shard_map/pallas_call | solution.py:571
  62.7 9.7 %shard_map.582 = (bf16[768,1536]{1,0:T(8,128)(2,1)S(1)}, bf16[816,1536]{1,0:T(8,128)(2,1)S(1)}, bf16[16,64,768]{2,1,0:T(8,128)(2,1)S(1)}, bf16[16,64,768]{2,1,0:...) custom-call(s32[10]{0:T(128)S(1)} %stack.40.ints, ...), custom_call_target="tpu_custom_call" | custom-call | flops 5133828096 | bytes 10027008 | tf_op jit(solution)/shard_map/pallas_call | solution.py:585
  72.4 2.1 %collective-permute-start.18 = (bf16[16,64,768]{2,1,0:T(8,128)(2,1)S(1)}, bf16[16,64,768]{2,1,0:T(8,128)(2,1)S(1)}, u32[]{:S(2)}, u32[]{:S(2)}) collective-permute-start(bf16[16,64,768]{2,1,0:T(8,128)(2,1)S(1)} %get-tuple-element.71), channel_id=1, source_target_pairs={{0,1},{1,0},{2,3},{3,2},{4,5},{5,4},{6,7},{7,6},{8,9},{9,8},{10,11... | collective-permute-start | bytes 4718600 | tf_op jit(solution)/shard_map/ppermute | solution.py:509
  74.5 3.0 %collective-permute-done.18 = bf16[16,64,768]{2,1,0:T(8,128)(2,1)S(1)} collective-permute-done((bf16[16,64,768]{2,1,0:T(8,128)(2,1)S(1)}, bf16[16,64,768]{2,1,0:T(8,128)(2,1)S(1)}, u32[]{:S(2)}, u32[]{:S(2)}) %collective-permute-start.18) | collective-permute-done | bytes 1572896 | tf_op jit(solution)/shard_map/ppermute | solution.py:509
  77.6 1.4 %add_convert_fusion.1 = (bf16[8,64,768]{2,1,0:T(8,128)(2,1)S(1)}, bf16[8,64,768]{2,1,0:T(8,128)(2,1)}) fusion(bf16[16,64,768]{2,1,0:T(8,128)(2,1)S(1)} %collective-permute-done.18, bf16[16,64,768]{2,1,0:T(8,128)(2,1)S(1)} %get-tuple-element.70), kind=kLoop, calls=%fused_computation.1 | loop fusion | flops 3145728 | bytes 4718592 | tf_op jit(solution)/shard_map/convert_element_type | solution.py:615
  79.0 2.9 %collective-permute-start.19 = (bf16[8,64,768]{2,1,0:T(8,128)(2,1)}, bf16[8,64,768]{2,1,0:T(8,128)(2,1)}, u32[]{:S(2)}, u32[]{:S(2)}) collective-permute-start(bf16[8,64,768]{2,1,0:T(8,128)(2,1)} %get-tuple-element.109), channel_id=1, source_target_pairs={{0,2},{1,5},{2,0},{3,7},{4,6},{5,1},{6,4},{7,3},{8,10},{9,13},{10,... | collective-permute-start | bytes 2359304 | tf_op jit(solution)/shard_map/ppermute | solution.py:509
  81.9 4.0 %shard_map.583 = (f32[3,256,512]{2,1,0:T(8,128)}, f32[8,512]{1,0:T(8,128)S(1)}) custom-call(s32[10]{0:T(128)S(1)} %stack.40.ints, f32[16,512]{1,0:T(8,128)S(1)} %add.232.params, bf16[768,1536]{1,0:T(8,128)(2,1)S(1)} %get-tuple-element.59.act, bf16[512,1536]{1,0:T(8,128)(2,1)S(1)} %get-tuple-element.60.down, bf16[3,256,512]{2,1,0:T(8,128)(2,1)S(1)} %copy-done, ...), custom_call_target="tpu_custom_call" | custom-call | flops 1207959552 | bytes 3342336 | tf_op jit(solution)/shard_map/pallas_call | solution.py:596
  85.8 10.1 %shard_map.584 = (f32[3,256,512]{2,1,0:T(8,128)}, f32[16,512]{1,0:T(8,128)S(1)}) custom-call(s32[10]{0:T(128)S(1)} %stack.40.ints, f32[16,512]{1,0:T(8,128)S(1)} %add.232.params, bf16[3,2,8,512]{3,2,1,0:T(8,128)(2,1)S(1)} %collective-permute-done.5.left, bf16[3,2,8,512]{3,2,1,0:T(8,128)(2,1)S(1)} %collective-permute-done.6.right, ...), custom_call_target="tpu_custom_call" | custom-call | flops 1283457024 | bytes 3342336 | tf_op jit(solution)/shard_map/pallas_call | solution.py:611
  97.5 3.7 %collective-permute-done.14 = f32[16,512]{1,0:T(8,128)S(1)} collective-permute-done((f32[16,512]{1,0:T(8,128)S(1)}, f32[16,512]{1,0:T(8,128)S(1)}, u32[]{:S(2)}, u32[]{:S(2)}) %collective-permute-start.14) | collective-permute-done | bytes 32800 | tf_op jit(solution)/shard_map/ppermute | solution.py:509
  102.2 2.9 %collective-permute-done.15 = f32[16,512]{1,0:T(8,128)S(1)} collective-permute-done((f32[16,512]{1,0:T(8,128)S(1)}, f32[16,512]{1,0:T(8,128)S(1)}, u32[]{:S(2)}, u32[]{:S(2)}) %collective-permute-start.15) | collective-permute-done | bytes 32800 | tf_op jit(solution)/shard_map/ppermute | solution.py:509
  105.1 1.5 %collective-permute-start.16 = (f32[16,512]{1,0:T(8,128)S(1)}, f32[16,512]{1,0:T(8,128)S(1)}, u32[]{:S(2)}, u32[]{:S(2)}) collective-permute-start(f32[16,512]{1,0:T(8,128)S(1)} %add.235), channel_id=1, source_target_pairs={{0,4},{1,5},{2,6},{3,7},{4,0},{5,1},{6,2},{7,3},{8,12},{9,13},{10,... | collective-permute-start | bytes 98312 | tf_op jit(solution)/shard_map/ppermute | solution.py:509
  106.7 2.4 %collective-permute-done.16 = f32[16,512]{1,0:T(8,128)S(1)} collective-permute-done((f32[16,512]{1,0:T(8,128)S(1)}, f32[16,512]{1,0:T(8,128)S(1)}, u32[]{:S(2)}, u32[]{:S(2)}) %collective-permute-start.16) | collective-permute-done | bytes 32800 | tf_op jit(solution)/shard_map/ppermute | solution.py:509
  109.1 2.8 %collective-permute-start.17 = (f32[16,512]{1,0:T(8,128)S(1)}, f32[16,512]{1,0:T(8,128)S(1)}, u32[]{:S(2)}, u32[]{:S(2)}) collective-permute-start(f32[16,512]{1,0:T(8,128)S(1)} %add.236), channel_id=1, source_target_pairs={{0,16},{1,17},{2,18},{3,19},{4,20},{5,21},{6,22},{7,23},{8,24},{9,... | collective-permute-start | bytes 98312 | tf_op jit(solution)/shard_map/ppermute | solution.py:509
  111.8 2.1 %collective-permute-done.17 = f32[16,512]{1,0:T(8,128)S(1)} collective-permute-done((f32[16,512]{1,0:T(8,128)S(1)}, f32[16,512]{1,0:T(8,128)S(1)}, u32[]{:S(2)}, u32[]{:S(2)}) %collective-permute-start.17) | collective-permute-done | bytes 32800 | tf_op jit(solution)/shard_map/ppermute | solution.py:509
  113.9 1.3 add_convert_fusion.3
  115.4 1.6 %collective-permute-start.20 = (bf16[4,64,768]{2,1,0:T(8,128)(2,1)S(1)}, bf16[4,64,768]{2,1,0:T(8,128)(2,1)S(1)}, u32[]{:S(2)}, u32[]{:S(2)}) collective-permute-start(bf16[4,64,768]{2,1,0:T(8,128)(2,1)S(1)} %get-tuple-element.111), channel_id=1, source_target_pairs={{0,4},{1,3},{2,6},{3,1},{4,0},{5,7},{6,2},{7,5},{8,12},{9,11},{10,... | collective-permute-start | bytes 1179656 | tf_op jit(solution)/shard_map/ppermute | solution.py:509
  118.4 4.8 %collective-permute-done.20 = bf16[4,64,768]{2,1,0:T(8,128)(2,1)S(1)} collective-permute-done((bf16[4,64,768]{2,1,0:T(8,128)(2,1)S(1)}, bf16[4,64,768]{2,1,0:T(8,128)(2,1)S(1)}, u32[]{:S(2)}, u32[]{:S(2)}) %collective-permute-start.20) | collective-permute-done | bytes 393248 | tf_op jit(solution)/shard_map/ppermute | solution.py:509
  124.2 5.8 %collective-permute-done.21 = bf16[2,64,768]{2,1,0:T(8,128)(2,1)S(1)} collective-permute-done((bf16[2,64,768]{2,1,0:T(8,128)(2,1)S(1)}, bf16[2,64,768]{2,1,0:T(8,128)(2,1)S(1)}, u32[]{:S(2)}, u32[]{:S(2)}) %collective-permute-start.21) | collective-permute-done | bytes 196640 | tf_op jit(solution)/shard_map/ppermute | solution.py:509
  130.1 1.8 %collective-permute-start.22 = (bf16[1,64,768]{2,1,0:T(8,128)(2,1)S(1)}, bf16[1,64,768]{2,1,0:T(8,128)(2,1)S(1)}, u32[]{:S(2)}, u32[]{:S(2)}) collective-permute-start(bf16[1,64,768]{2,1,0:T(8,128)(2,1)S(1)} %add_convert_fusion.6), channel_id=1, source_target_pairs={{0,16},{1,17},{2,18},{3,19},{4,20},{5,21},{6,22},{7,23},{8,24},{9,... | collective-permute-start | bytes 294920 | tf_op jit(solution)/shard_map/ppermute | solution.py:509
  132.5 3.9 %collective-permute-done.22 = bf16[1,64,768]{2,1,0:T(8,128)(2,1)S(1)} collective-permute-done((bf16[1,64,768]{2,1,0:T(8,128)(2,1)S(1)}, bf16[1,64,768]{2,1,0:T(8,128)(2,1)S(1)}, u32[]{:S(2)}, u32[]{:S(2)}) %collective-permute-start.22) | collective-permute-done | bytes 98336 | tf_op jit(solution)/shard_map/ppermute | solution.py:509
  (110 shorter events, 17.3 us)
Async XLA Ops:
  1.6 36.3 %copy-start.8 = (f32[16,7]{0,1:T(8,128)S(1)}, f32[16,7]{0,1:T(8,128)}, u32[]{:S(2)}) copy-start(f32[16,7]{0,1:T(8,128)} %param.33) | copy-start | bytes 1348
  1.6 36.3 %copy-start.12 = (f32[16]{0:T(128)S(1)}, f32[16]{0:T(128)}, u32[]{:S(2)}) copy-start(f32[16]{0:T(128)} %param.35) | copy-start | bytes 196
  1.6 36.3 %copy-start.13 = (f32[16]{0:T(128)S(1)}, f32[16]{0:T(128)}, u32[]{:S(2)}) copy-start(f32[16]{0:T(128)} %param.36) | copy-start | bytes 196
  1.6 36.3 %copy-start.14 = (f32[16]{0:T(128)S(1)}, f32[16]{0:T(128)}, u32[]{:S(2)}) copy-start(f32[16]{0:T(128)} %param.40) | copy-start | bytes 196
  1.6 36.3 %copy-start.15 = (f32[16]{0:T(128)S(1)}, f32[16]{0:T(128)}, u32[]{:S(2)}) copy-start(f32[16]{0:T(128)} %param.41) | copy-start | bytes 196
  1.6 36.3 %copy-start.16 = (f32[16]{0:T(128)S(1)}, f32[16]{0:T(128)}, u32[]{:S(2)}) copy-start(f32[16]{0:T(128)} %param.34) | copy-start | bytes 196
  2.6 47.3 %copy-start = (bf16[3,256,512]{2,1,0:T(8,128)(2,1)S(1)}, bf16[3,256,512]{2,1,0:T(8,128)(2,1)}, u32[]{:S(2)}) copy-start(bf16[3,256,512]{2,1,0:T(8,128)(2,1)} %frames.5) | copy-start | bytes 2359300
  2.6 47.3 %copy-start.1 = (bf16[3,256,512]{2,1,0:T(8,128)(2,1)S(1)}, bf16[3,256,512]{2,1,0:T(8,128)(2,1)}, u32[]{:S(2)}) copy-start(bf16[3,256,512]{2,1,0:T(8,128)(2,1)} %cot.5) | copy-start | bytes 2359300
  2.6 9.0 %collective-permute-start.7 = (bf16[1,64,768]{2,1,0:T(8,128)(2,1)S(1)}, bf16[1,64,768]{2,1,0:T(8,128)(2,1)S(1)}, u32[]{:S(2)}, u32[]{:S(2)}) collective-permute-start(bf16[1,64,768]{2,1,0:T(8,128)(2,1)S(1)} %maximum_bitcast_fusion), channel_id=1, source_target_pairs={{0,16},{1,17},{2,18},{3,19},{4,20},{5,21},{6,22},{7,23},{8,24},{9,... | collective-permute-start | bytes 294920 | tf_op jit(solution)/shard_map/ppermute | solution.py:509
  11.7 6.1 %collective-permute-start.8 = (bf16[2,64,768]{2,1,0:T(8,128)(2,1)S(1)}, bf16[2,64,768]{2,1,0:T(8,128)(2,1)S(1)}, u32[]{:S(2)}, u32[]{:S(2)}) collective-permute-start(bf16[2,64,768]{2,1,0:T(8,128)(2,1)S(1)} %pad_maximum_fusion.2), channel_id=1, source_target_pairs={{0,8},{1,9},{2,10},{3,11},{4,12},{5,13},{6,14},{7,15},{8,0},{9,1},... | collective-permute-start | bytes 589832 | tf_op jit(solution)/shard_map/ppermute | solution.py:509
  17.9 38.0 %copy-start.17 = (s32[3]{0:T(128)S(1)}, s32[3]{0:T(128)}, u32[]{:S(2)}) copy-start(s32[3]{0:T(128)} %param.32) | copy-start | bytes 40
  17.9 7.8 %collective-permute-start.9 = (bf16[4,64,768]{2,1,0:T(8,128)(2,1)S(1)}, bf16[4,64,768]{2,1,0:T(8,128)(2,1)S(1)}, u32[]{:S(2)}, u32[]{:S(2)}) collective-permute-start(bf16[4,64,768]{2,1,0:T(8,128)(2,1)S(1)} %pad_maximum_fusion.1), channel_id=1, source_target_pairs={{0,4},{1,3},{2,6},{3,1},{4,0},{5,7},{6,2},{7,5},{8,12},{9,11},{10,... | collective-permute-start | bytes 1179656 | tf_op jit(solution)/shard_map/ppermute | solution.py:509
  25.8 12.1 %collective-permute-start.10 = (bf16[8,64,768]{2,1,0:T(8,128)(2,1)S(1)}, bf16[8,64,768]{2,1,0:T(8,128)(2,1)S(1)}, u32[]{:S(2)}, u32[]{:S(2)}) collective-permute-start(bf16[8,64,768]{2,1,0:T(8,128)(2,1)S(1)} %pad_maximum_fusion.refs_0_), channel_id=1, source_target_pairs={{0,2},{1,5},{2,0},{3,7},{4,6},{5,1},{6,4},{7,3},{8,10},{9,13},{10,... | collective-permute-start | bytes 2359304 | tf_op jit(solution)/shard_map/ppermute | solution.py:509
  27.1 35.6 %collective-permute-start.11 = (bf16[8,64,768]{2,1,0:T(8,128)(2,1)S(1)}, bf16[8,64,768]{2,1,0:T(8,128)(2,1)}, u32[]{:S(2)}, u32[]{:S(2)}) collective-permute-start(bf16[8,64,768]{2,1,0:T(8,128)(2,1)S(1)} %pad_maximum_fusion.refs_0_), channel_id=1, source_target_pairs={{0,1},{1,0},{2,3},{3,2},{4,5},{5,4},{6,7},{7,6},{8,9},{9,8},{10,11... | collective-permute-start | bytes 2359304 | tf_op jit(solution)/shard_map/ppermute | solution.py:509
  37.9 24.9 %collective-permute-start.12 = (bf16[8,64,768]{2,1,0:T(8,128)(2,1)S(1)}, bf16[8,64,768]{2,1,0:T(8,128)(2,1)}, u32[]{:S(2)}, u32[]{:S(2)}) collective-permute-start(bf16[8,64,768]{2,1,0:T(8,128)(2,1)S(1)} %collective-permute-done.10.refs_1_), channel_id=1, source_target_pairs={{0,1},{1,0},{2,3},{3,2},{4,5},{5,4},{6,7},{7,6},{8,9},{9,8},{10,11... | collective-permute-start | bytes 2359304 | tf_op jit(solution)/shard_map/ppermute | solution.py:509
  38.8 1.8 %collective-permute-start = (f32[16,512]{1,0:T(8,128)S(1)}, f32[16,512]{1,0:T(8,128)S(1)}, u32[]{:S(2)}, u32[]{:S(2)}) collective-permute-start(f32[16,512]{1,0:T(8,128)S(1)} %dynamic_update_slice.7), channel_id=1, source_target_pairs={{0,1},{1,0},{2,3},{3,2},{4,5},{5,4},{6,7},{7,6},{8,9},{9,8},{10,11... | collective-permute-start | bytes 98312 | tf_op jit(solution)/shard_map/ppermute | solution.py:509
  40.6 3.9 %collective-permute-start.1 = (f32[16,512]{1,0:T(8,128)S(1)}, f32[16,512]{1,0:T(8,128)S(1)}, u32[]{:S(2)}, u32[]{:S(2)}) collective-permute-start(f32[16,512]{1,0:T(8,128)S(1)} %add.228), channel_id=1, source_target_pairs={{0,2},{1,3},{2,0},{3,1},{4,6},{5,7},{6,4},{7,5},{8,10},{9,11},{10,... | collective-permute-start | bytes 98312 | tf_op jit(solution)/shard_map/ppermute | solution.py:509
  44.5 3.9 %collective-permute-start.2 = (f32[16,512]{1,0:T(8,128)S(1)}, f32[16,512]{1,0:T(8,128)S(1)}, u32[]{:S(2)}, u32[]{:S(2)}) collective-permute-start(f32[16,512]{1,0:T(8,128)S(1)} %add.229), channel_id=1, source_target_pairs={{0,4},{1,5},{2,6},{3,7},{4,0},{5,1},{6,2},{7,3},{8,12},{9,13},{10,... | collective-permute-start | bytes 98312 | tf_op jit(solution)/shard_map/ppermute | solution.py:509
  48.4 4.1 %collective-permute-start.3 = (f32[16,512]{1,0:T(8,128)S(1)}, f32[16,512]{1,0:T(8,128)S(1)}, u32[]{:S(2)}, u32[]{:S(2)}) collective-permute-start(f32[16,512]{1,0:T(8,128)S(1)} %add.230), channel_id=1, source_target_pairs={{0,8},{1,9},{2,10},{3,11},{4,12},{5,13},{6,14},{7,15},{8,0},{9,1},... | collective-permute-start | bytes 98312 | tf_op jit(solution)/shard_map/ppermute | solution.py:509
  49.9 7.9 %collective-permute-start.5 = (bf16[3,2,8,512]{3,2,1,0:T(8,128)(2,1)S(1)}, bf16[3,2,8,512]{3,2,1,0:T(8,128)(2,1)S(1)}, u32[]{:S(2)}, u32[]{:S(2)}) collective-permute-start(bf16[3,2,8,512]{3,2,1,0:T(8,128)(2,1)S(1)} %get-tuple-element.113), channel_id=1, source_target_pairs={{0,1},{1,2},{2,3},{4,5},{5,6},{6,7},{8,9},{9,10},{10,11},{12,13},{... | collective-permute-start | bytes 147464 | tf_op jit(solution)/shard_map/ppermute | solution.py:530
  51.2 6.6 %collective-permute-start.6 = (bf16[3,2,8,512]{3,2,1,0:T(8,128)(2,1)S(1)}, bf16[3,2,8,512]{3,2,1,0:T(8,128)(2,1)S(1)}, u32[]{:S(2)}, u32[]{:S(2)}) collective-permute-start(bf16[3,2,8,512]{3,2,1,0:T(8,128)(2,1)S(1)} %get-tuple-element.112), channel_id=1, source_target_pairs={{1,0},{2,1},{3,2},{5,4},{6,5},{7,6},{9,8},{10,9},{11,10},{13,12},{... | collective-permute-start | bytes 147464 | tf_op jit(solution)/shard_map/ppermute | solution.py:531
  52.5 5.3 %collective-permute-start.4 = (f32[16,512]{1,0:T(8,128)S(1)}, f32[16,512]{1,0:T(8,128)S(1)}, u32[]{:S(2)}, u32[]{:S(2)}) collective-permute-start(f32[16,512]{1,0:T(8,128)S(1)} %add.231), channel_id=1, source_target_pairs={{0,16},{1,17},{2,18},{3,19},{4,20},{5,21},{6,22},{7,23},{8,24},{9,... | collective-permute-start | bytes 98312 | tf_op jit(solution)/shard_map/ppermute | solution.py:509
  72.4 5.2 %collective-permute-start.18 = (bf16[16,64,768]{2,1,0:T(8,128)(2,1)S(1)}, bf16[16,64,768]{2,1,0:T(8,128)(2,1)S(1)}, u32[]{:S(2)}, u32[]{:S(2)}) collective-permute-start(bf16[16,64,768]{2,1,0:T(8,128)(2,1)S(1)} %get-tuple-element.71), channel_id=1, source_target_pairs={{0,1},{1,0},{2,3},{3,2},{4,5},{5,4},{6,7},{7,6},{8,9},{9,8},{10,11... | collective-permute-start | bytes 4718600 | tf_op jit(solution)/shard_map/ppermute | solution.py:509
  79.0 34.9 %collective-permute-start.19 = (bf16[8,64,768]{2,1,0:T(8,128)(2,1)}, bf16[8,64,768]{2,1,0:T(8,128)(2,1)}, u32[]{:S(2)}, u32[]{:S(2)}) collective-permute-start(bf16[8,64,768]{2,1,0:T(8,128)(2,1)} %get-tuple-element.109), channel_id=1, source_target_pairs={{0,2},{1,5},{2,0},{3,7},{4,6},{5,1},{6,4},{7,3},{8,10},{9,13},{10,... | collective-permute-start | bytes 2359304 | tf_op jit(solution)/shard_map/ppermute | solution.py:509
  96.0 1.3 collective-permute-start.13
  97.3 3.9 %collective-permute-start.14 = (f32[16,512]{1,0:T(8,128)S(1)}, f32[16,512]{1,0:T(8,128)S(1)}, u32[]{:S(2)}, u32[]{:S(2)}) collective-permute-start(f32[16,512]{1,0:T(8,128)S(1)} %add.233), channel_id=1, source_target_pairs={{0,8},{1,9},{2,10},{3,11},{4,12},{5,13},{6,14},{7,15},{8,0},{9,1},... | collective-permute-start | bytes 98312 | tf_op jit(solution)/shard_map/ppermute | solution.py:509
  101.2 3.9 %collective-permute-start.15 = (f32[16,512]{1,0:T(8,128)S(1)}, f32[16,512]{1,0:T(8,128)S(1)}, u32[]{:S(2)}, u32[]{:S(2)}) collective-permute-start(f32[16,512]{1,0:T(8,128)S(1)} %add.234), channel_id=1, source_target_pairs={{0,2},{1,3},{2,0},{3,1},{4,6},{5,7},{6,4},{7,5},{8,10},{9,11},{10,... | collective-permute-start | bytes 98312 | tf_op jit(solution)/shard_map/ppermute | solution.py:509
  105.1 3.9 %collective-permute-start.16 = (f32[16,512]{1,0:T(8,128)S(1)}, f32[16,512]{1,0:T(8,128)S(1)}, u32[]{:S(2)}, u32[]{:S(2)}) collective-permute-start(f32[16,512]{1,0:T(8,128)S(1)} %add.235), channel_id=1, source_target_pairs={{0,4},{1,5},{2,6},{3,7},{4,0},{5,1},{6,2},{7,3},{8,12},{9,13},{10,... | collective-permute-start | bytes 98312 | tf_op jit(solution)/shard_map/ppermute | solution.py:509
  109.1 4.8 %collective-permute-start.17 = (f32[16,512]{1,0:T(8,128)S(1)}, f32[16,512]{1,0:T(8,128)S(1)}, u32[]{:S(2)}, u32[]{:S(2)}) collective-permute-start(f32[16,512]{1,0:T(8,128)S(1)} %add.236), channel_id=1, source_target_pairs={{0,16},{1,17},{2,18},{3,19},{4,20},{5,21},{6,22},{7,23},{8,24},{9,... | collective-permute-start | bytes 98312 | tf_op jit(solution)/shard_map/ppermute | solution.py:509
  115.4 7.8 %collective-permute-start.20 = (bf16[4,64,768]{2,1,0:T(8,128)(2,1)S(1)}, bf16[4,64,768]{2,1,0:T(8,128)(2,1)S(1)}, u32[]{:S(2)}, u32[]{:S(2)}) collective-permute-start(bf16[4,64,768]{2,1,0:T(8,128)(2,1)S(1)} %get-tuple-element.111), channel_id=1, source_target_pairs={{0,4},{1,3},{2,6},{3,1},{4,0},{5,7},{6,2},{7,5},{8,12},{9,11},{10,... | collective-permute-start | bytes 1179656 | tf_op jit(solution)/shard_map/ppermute | solution.py:509
  123.3 6.7 %collective-permute-start.21 = (bf16[2,64,768]{2,1,0:T(8,128)(2,1)S(1)}, bf16[2,64,768]{2,1,0:T(8,128)(2,1)S(1)}, u32[]{:S(2)}, u32[]{:S(2)}) collective-permute-start(bf16[2,64,768]{2,1,0:T(8,128)(2,1)S(1)} %get-tuple-element.115), channel_id=1, source_target_pairs={{0,8},{1,9},{2,10},{3,11},{4,12},{5,13},{6,14},{7,15},{8,0},{9,1},... | collective-permute-start | bytes 589832 | tf_op jit(solution)/shard_map/ppermute | solution.py:509
  130.1 6.3 %collective-permute-start.22 = (bf16[1,64,768]{2,1,0:T(8,128)(2,1)S(1)}, bf16[1,64,768]{2,1,0:T(8,128)(2,1)S(1)}, u32[]{:S(2)}, u32[]{:S(2)}) collective-permute-start(bf16[1,64,768]{2,1,0:T(8,128)(2,1)S(1)} %add_convert_fusion.6), channel_id=1, source_target_pairs={{0,16},{1,17},{2,18},{3,19},{4,20},{5,21},{6,22},{7,23},{8,24},{9,... | collective-permute-start | bytes 294920 | tf_op jit(solution)/shard_map/ppermute | solution.py:509
  (21 other events, 429.6 us)

commit v3 on v2

--- a/solution.py
+++ b/solution.py
@@ -32,8 +32,11 @@
 def adam_step(weights_now, gradient, moment, square, step_number):
     next_moment = first_decay * moment + (1.0 - first_decay) * gradient
     next_square = second_decay * square + (1.0 - second_decay) * gradient * gradient
-    first_fix = 1.0 - jnp.power(jnp.float32(first_decay), step_number)
-    second_fix = 1.0 - jnp.power(jnp.float32(second_decay), step_number)
+    if step_number is None:
+        first_fix, second_fix = 1.0 - first_decay**STEP, 1.0 - second_decay**STEP
+    else:
+        first_fix = 1.0 - jnp.power(jnp.float32(first_decay), step_number)
+        second_fix = 1.0 - jnp.power(jnp.float32(second_decay), step_number)
     step_ratio = next_moment / first_fix / (jnp.sqrt(next_square / second_fix) + adam_eps)
     update = -(learn_rate * (step_ratio + weight_decay * weights_now))
     return (weights_now + update, next_moment, next_square, update)
@@ -43,17 +46,25 @@
     return pl.BlockSpec(memory_space=pltpu.VMEM)
 
 
+def whole(shape):
+    return pl.BlockSpec(shape, lambda: (0,) * len(shape))
+
+
 def smem():
     return pl.BlockSpec(memory_space=pltpu.SMEM)
 
 
-FAST_MASKS = ((16, 8, 4, 2), (16, 8, 2, 4))
+FAST_MASKS = ((16, 8, 4, 2), (8, 16, 2, 4))
+
+FEW_ORDER = ((1, 1), (4, 2), (2, 4), (8, 8), (16, 16))
+SUM_ORDER = ((1, 1), (16, 16), (2, 4), (4, 2), (8, 8))
 
 
 def position(core, dp_rel, x_rel):
     high, low, y = (dp_rel >> 2) & 1, (dp_rel >> 1) & 1, dp_rel & 1
-    pair = (y | (x_rel << 1)) if core == 0 else (x_rel | (y << 1))
-    return high | (low << 1) | (pair << 2)
+    if core == 0:
+        return high | (low << 1) | (y << 2) | (x_rel << 3)
+    return low | (high << 1) | (x_rel << 2) | (y << 3)
 
 
 def fill_shifted(s, lengths_ref, start, frames_get, left_get, right_get, sh, quarter, width):
@@ -86,6 +97,7 @@
 
 
 GROUP = 4
+STRIDE = 64
 
 
 def front_kernel(slots, quarter, width, taps, ints, frames, cot, left, right, params,
@@ -266,7 +278,7 @@
                     first, last = max(column, x * own_width), min(column + TILE, (x + 1) * own_width)
                     if first >= last:
                         continue
-                    place = high + 2 * low + 4 * (y * (1 + owner) + x * (2 - owner))
+                    place = high * (1 + owner) + low * (2 - owner) + 4 * (y * (1 + owner) + x * (2 - owner))
                     out = slice(which * own_width + first - x * own_width, which * own_width + last - x * own_width)
                     grads[n][place, :, out] = value[
                         dp * rows_dp - row : (dp + 1) * rows_dp - row, first - column : last - column
@@ -325,9 +337,9 @@
         row = pl.multiple_of(i * CHUNK, CHUNK)
         rows = pl.ds(row, CHUNK)
         live = lax.broadcasted_iota(jnp.int32, (CHUNK, width), 0) + (start + row) < length
-        back = jnp.where(live, cot[0, rows, :].astype(f32), 0.0)
+        back = jnp.where(live, cot[s, rows, :].astype(f32), 0.0)
         total = branch[rows, :] + params[taps + 3 : taps + 4, :]
-        shown = frames[0, rows, :].astype(f32) + params[taps + 4 : taps + 5, :] * total
+        shown = frames[s, rows, :].astype(f32) + params[taps + 4 : taps + 5, :] * total
         output[0, rows, :] = jnp.where(live, shown, 0.0)
         part = back * total
         return total_sum + (part[0:8] + part[8:16])
@@ -357,7 +369,7 @@
         ng_halo[...] = product(pl.ds(own_rows, slots * HALO))
 
     fill_shifted(
-        s, ints, start, lambda row: frames[0, pl.ds(row, CHUNK), :],
+        s, ints, start, lambda row: frames[s, pl.ds(row, CHUNK), :],
         lambda: left[s, 0], lambda: right[s, 0], sh, quarter, width,
     )
     ngs[...] = product(pl.ds(pl.multiple_of(s * quarter, CHUNK), quarter))
@@ -383,7 +395,7 @@
         return value[0:8] + value[8:16]
 
     def norm_step(i, _):
-        firsts = [pl.multiple_of(i * (2 * CHUNK) + u * CHUNK, CHUNK) for u in range(2)]
+        firsts = [pl.multiple_of(i * (GROUP * CHUNK) + u * CHUNK, CHUNK) for u in range(GROUP)]
         ngs_here = [[ngs[pl.ds(row, CHUNK), lanes(j)] for j in range(blocks)] for row in firsts]
         units, grads = norm_back(
             [(ng, pl.ds(pl.multiple_of(s * quarter + row, CHUNK), CHUNK)) for ng, row in zip(ngs_here, firsts)]
@@ -396,7 +408,7 @@
             acc[taps, :, lanes(j)] += functools.reduce(jnp.add, [fold(cg[j]) for cg in grads])
         return 0
 
-    lax.fori_loop(0, quarter // (2 * CHUNK), norm_step, 0)
+    lax.fori_loop(0, quarter // (GROUP * CHUNK), norm_step, 0)
     tail = pl.multiple_of(s * HALO, HALO)
     ng = [ng_halo[pl.ds(tail, HALO), lanes(j)] for j in range(blocks)]
     _, (cg,) = norm_back([(ng, pl.ds(pl.multiple_of(own_rows + tail, HALO), HALO))])
@@ -408,22 +420,23 @@
 
     for j in range(blocks):
         def conv_step(i, sums):
-            row = pl.multiple_of(i * CHUNK, CHUNK)
-            rows = pl.ds(row, CHUNK)
-            live = lax.broadcasted_iota(jnp.int32, (CHUNK, LANES), 0) + (start + row) < length
-            back = jnp.where(live, cot[0, rows, lanes(j)].astype(f32), 0.0)
+            row = pl.multiple_of(i * STRIDE, STRIDE)
+            rows = pl.ds(row, STRIDE)
+            live = lax.broadcasted_iota(jnp.int32, (STRIDE, LANES), 0) + (start + row) < length
+            back = jnp.where(live, cot[s, rows, lanes(j)].astype(f32), 0.0)
             first = row + 2 * EDGE
-            here = cgs[j, pl.ds(first, CHUNK), :]
-            pulled = jnp.zeros((CHUNK, LANES), f32)
+            here = cgs[j, pl.ds(first, STRIDE), :]
+            pulled = jnp.zeros((STRIDE, LANES), f32)
             out = []
             for k in range(taps):
-                pulled = pulled + cgs[j, pl.ds(first + half - k, CHUNK), :] * params[k : k + 1, lanes(j)]
-                out.append(sums[k] + fold(here * sh[j, pl.ds(first + k - half, CHUNK), :]))
+                pulled = pulled + cgs[j, pl.ds(first + half - k, STRIDE), :] * params[k : k + 1, lanes(j)]
+                product = here * sh[j, pl.ds(first + k - half, STRIDE), :]
+                out.append(sums[k] + functools.reduce(jnp.add, [product[r : r + 8] for r in range(0, STRIDE, 8)]))
             input_grad[0, rows, lanes(j)] = back + jnp.where(live, pulled, 0.0)
             return tuple(out)
 
         sums = lax.fori_loop(
-            0, quarter // CHUNK, conv_step, tuple(jnp.zeros((8, LANES), f32) for _ in range(taps))
+            0, quarter // STRIDE, conv_step, tuple(jnp.zeros((8, LANES), f32) for _ in range(taps))
         )
         for k in range(taps):
             acc[k, :, lanes(j)] += sums[k]
@@ -438,6 +451,43 @@
         for x in range(4):
             place = ints[slots + 3 + x]
             small[pl.ds(taps + 5 + place, 1), 0:own_width] = bias_grad[0:1, x * own_width : (x + 1) * own_width]
+
+
+def update_kernel(keep, arrived, *refs):
+    width = refs[0].shape[1]
+    for n in range(2):
+        weights, moment, square = refs[n], refs[2 + n], refs[4 + n]
+        shown = refs[6 + 4 * n : 10 + 4 * n]
+        lanes = slice(n * width, (n + 1) * width)
+        gradient = keep[0, :, lanes].astype(f32) + arrived[0, :, lanes].astype(f32)
+        next_weights, next_moment, next_square, _ = adam_step(
+            weights[...], gradient, moment[...], square[...], None
+        )
+        shown[0][...] = gradient
+        shown[1][...] = next_weights
+        shown[2][...] = next_moment
+        shown[3][...] = next_square
+
+
+def finish_kernel(taps, ints, small, *refs):
+    own_channels, own_bias = refs[0].shape[1], refs[6].shape[1]
+    own = ints[0]
+    shift = own * own_channels
+    width = small.shape[1]
+    channels = pltpu.roll(small[0:16, :], width - shift, 1)
+    bias_row = small[pl.ds(ints[1], 1), :]
+    bias = pltpu.roll(jnp.broadcast_to(bias_row, (8, width)), width - ints[2], 1)[0:1, 0:own_bias]
+    for n in range(7):
+        rows = slice(0, taps) if n == 0 else slice(taps + n - 1, taps + n)
+        gradient = bias if n == 6 else channels[rows, 0:own_channels]
+        shown = refs[21 + 4 * n : 25 + 4 * n]
+        next_weights, next_moment, next_square, update = adam_step(
+            refs[n][...], gradient, refs[7 + n][...], refs[14 + n][...], None
+        )
+        shown[0][...] = gradient
+        shown[1][...] = update if n in (2, 5) else next_weights
+        shown[2][...] = next_moment
+        shown[3][...] = next_square
 
 
 def call(kernel, outs, in_specs, scratch, limit, flops=0, moved=0, grid=None, out_specs=None):
@@ -510,7 +560,11 @@
 
     if fast:
         steps = [(FAST_MASKS[0][k], FAST_MASKS[1][k]) for k in range(4)]
-        held = jnp.concatenate([up_weight.astype(bf16), down_weight.astype(bf16)], axis=1)[None]
+        none = jnp.zeros((), bf16)
+        held = (
+            lax.pad(up_weight.astype(bf16), none, ((0, 0, 0), (0, own_width, 0)))
+            + lax.pad(down_weight.astype(bf16), none, ((0, 0, 0), (own_width, 0, 0)))
+        )[None]
         for k in range(3):
             arrived = swap(held, steps[k])
             held = jnp.concatenate([held, arrived], axis=0)
@@ -539,16 +593,16 @@
     params = lax.dynamic_update_slice(
         params, up_bias[None], (taps + 5 + own * own_bias // own_width, own * own_bias % own_width)
     )
-    bits = [1 << k for k in range(count.bit_length() - 1)]
+    bits = [(1 << k, 1 << k) for k in range(count.bit_length() - 1)]
     assert 1 << len(bits) == count
 
     def sum_all(value, order):
-        for bit in order:
-            arrived = swap(value, (bit, bit))
+        for masks in order:
+            arrived = swap(value, masks)
             value = value + arrived
         return value
 
-    params = sum_all(params, bits)
+    params = sum_all(params, FEW_ORDER if fast else bits)
 
     ints = jnp.stack(
         [*[lengths[s] for s in range(slots)], tp_own * quarter, dp_own, core, *blocks[0], *blocks[1]]
@@ -588,7 +642,7 @@
     output = call(
         functools.partial(output_kernel, slots, quarter, width, taps),
         [((slots, quarter, width), f32), ((8, width), f32)],
-        [smem(), vmem(), vmem(), vmem(), slot_spec, slot_spec],
+        [smem()] + [vmem()] * 5,
         [pltpu.VMEM((quarter, width), f32)],
         8, flops=2 * own_rows * width * hidden_width, moved=8 * all_rows * width,
         grid=(slots,), out_specs=[slot_spec, vmem()],
@@ -597,7 +651,7 @@
     back = call(
         functools.partial(back_kernel, (slots, quarter, width, taps, own_width)),
         [((slots, quarter, width), f32), ((small_rows, width), f32)],
-        [smem()] + [vmem()] * 9 + [slot_spec, slot_spec],
+        [smem()] + [vmem()] * 11,
         [
             pltpu.VMEM((width // LANES, quarter + 4 * EDGE, LANES), f32),
             pltpu.VMEM((width // LANES, quarter + 4 * EDGE, LANES), f32),
@@ -622,9 +676,19 @@
             send = plus(keep[size:], arrived[size:])
             keep = plus(keep[:size], arrived[:size])
         arrived = swap(send, steps[0])
-        total = keep[0].astype(f32) + arrived[0].astype(f32)
-        up_share, down_share = total[:, :own_width], total[:, own_width:]
+        shape = (own_rows_w, own_width)
+        updated = call(
+            update_kernel, [(shape, f32)] * 8, [vmem()] * 8, [], 4,
+            flops=40 * own_rows_w * own_width, moved=64 * own_rows_w * own_width,
+            out_specs=[whole(shape)] * 8,
+        )(
+            keep, arrived, up_weight, down_weight, moment_up_weight, moment_down_weight,
+            square_up_weight, square_down_weight,
+        )
+        updated = {4: tuple(updated[:4]), 6: tuple(updated[4:])}
+        up_share = down_share = None
     else:
+        updated = {}
         up_share, down_share = (
             lax.psum_scatter(
                 lax.psum_scatter(grads[0][n], "tp", scatter_dimension=1, tiled=True),
@@ -633,12 +697,33 @@
             for n in range(2)
         )
 
-    small = sum_all(small, (1, 8, 2, 4, 16) if fast else bits)
-    own_small = lax.dynamic_slice(small, (0, own * own_channels), (taps + 5, own_channels))
-    share_up = lax.dynamic_slice(
-        small, (taps + 5 + own * own_bias // own_width, own * own_bias % own_width), (1, own_bias)
-    )[0]
-
+    small = sum_all(small, SUM_ORDER if fast else bits)
+    order = (0, 1, 2, 3, 7, 8, 5)
+    lists = (
+        (conv_weight, conv_bias, norm_gain, norm_bias, up_weight, up_bias, down_weight, down_bias, layer_scale),
+        (
+            moment_conv_weight, moment_conv_bias, moment_norm_gain, moment_norm_bias, moment_up_weight,
+            moment_up_bias, moment_down_weight, moment_down_bias, moment_layer_scale,
+        ),
+        (
+            square_conv_weight, square_conv_bias, square_norm_gain, square_norm_bias, square_up_weight,
+            square_up_bias, square_down_weight, square_down_bias, square_layer_scale,
+        ),
+    )
+    given = [v.T if v.ndim == 2 else v[None] for values in lists for v in [values[n] for n in order]]
+    shapes = [v.shape for v in given[:7]]
+    finished = call(
+        functools.partial(finish_kernel, taps),
+        [(shape, f32) for shape in shapes for _ in range(4)],
+        [smem(), vmem()] + [vmem()] * 21, [], 4,
+        out_specs=[whole(shape) for shape in shapes for _ in range(4)],
+    )(
+        jnp.stack([own, taps + 5 + own * own_bias // own_width, own * own_bias % own_width]).astype(jnp.int32),
+        small, *given,
+    )
+    for k, n in enumerate(order):
+        values = finished[4 * k : 4 * k + 4]
+        updated[n] = tuple(v.T if n == 0 else v[0] for v in values)
     step_number = jnp.float32(STEP)
     params_own = (
         conv_weight,
@@ -651,17 +736,7 @@
         down_bias,
         layer_scale,
     )
-    gradients = (
-        own_small[:taps].T,
-        own_small[taps],
-        own_small[taps + 1],
-        own_small[taps + 2],
-        up_share,
-        share_up,
-        down_share,
-        own_small[taps + 3],
-        own_small[taps + 4],
-    )
+    gradients = (None,) * 4 + (up_share, None, down_share, None, None)
     moments = (
         moment_conv_weight,
         moment_conv_bias,
@@ -685,12 +760,13 @@
         square_layer_scale,
     )
     flat = [output_own, input_own]
-    for weights_now, gradient, moment, square, use_update in zip(
-        params_own, gradients, moments, squares, update_flags
+    for n, (weights_now, gradient, moment, square, use_update) in enumerate(
+        zip(params_own, gradients, moments, squares, update_flags)
     ):
-        next_weights, next_moment, next_square, update = adam_step(
-            weights_now, gradient, moment, square, step_number
-        )
+        if n in updated:
+            flat = flat + [*updated[n]]
+            continue
+        next_weights, next_moment, next_square, update = adam_step(weights_now, gradient, moment, square, step_number)
         shown = update if use_update else next_weights
         flat = flat + [gradient, shown, next_moment, next_square]
     return tuple(flat)

time: 138 us -> 130 us (0.942)
  waiting for transfers between devices: 65.4 us -> 57.1 us
  starting transfers between devices: 32.6 us -> 38.5 us
  other arithmetic: 8.48 us -> 2.96 us
    ppermute x21, waiting for transfers between devices: 65.4 us -> 57.1 us  [swap(): lax.ppermute(value, both, [(i, i ^ masks[i & 1]) for i in range(count)])]
    ppermute x21, starting transfers between devices: 30 us -> 34.2 us  [swap(): lax.ppermute(value, both, [(i, i ^ masks[i & 1]) for i in range(count)])]
    add x5 -> x0, other arithmetic: 2.87 us -> none  [the longest x4 2.84 us: adam_step(): return (weights_now + update, next_moment, next_square, update)]
    pallas_call x0 -> x2, Pallas kernels: none -> 2.33 us  [the longest x1 1.37 us: per_device(): call(functools.partial(finish_kernel, taps), [(shape, f32) for shape in s...]
    convert_element_type x4, other arithmetic: 2.86 us -> 0.83 us  [plus(): return (a.astype(f32) + b.astype(f32)).astype(bf16)]
    pallas_call x1, Pallas kernels: 10.1 us -> 8.16 us  [per_device(): back(ints, params, left, right, hg, up, unit, bias_grad, bg_sum, scale_su...]
    ppermute x1, starting transfers between devices: 1.29 us -> 3.03 us  [per_device(): lax.ppermute(pair[:, :, quarter - EDGE:, :], 'tp', [(i, i + 1) for i in r...]
  transfers between devices with their start and end apart: 23 -> 23, of which waited for: 17 -> 17; matrix products, arithmetic and copies ran while one was open for 3% -> 1% of each run, Pallas kernels for 14% -> 14%
where the time goes in v3:
time: 130 us
  waiting for transfers between devices  57.1 us (44%)
  starting transfers between devices  38.5 us (30%)
  Pallas kernels  29.1 us (22%)
  other arithmetic  2.96 us (2%)
    ppermute x21, waiting for transfers between devices, swap(): lax.ppermute(value, both, [(i, i ^ masks[i & 1]) for i in range(count)])  57.1 us
    ppermute x21, starting transfers between devices, swap(): lax.ppermute(value, both, [(i, i ^ masks[i & 1]) for i in range(count)])  34.2 us
    pallas_call x1, Pallas kernels, per_device(): hidden(ints, normed, bg, normed_t, bg_t, params, *weights)  9.68 us
    pallas_call x1, Pallas kernels, per_device(): back(ints, params, left, right, hg, up, unit, bias_grad, bg_sum, scale_su...  8.16 us
    pallas_call x1, Pallas kernels, per_device(): front(ints, frames, cotangent, left, right, params)  4.88 us
    pallas_call x1, Pallas kernels, per_device(): output_own, scale_sum = output(ints, params, act, down, frames, cotangent)  4 us
    ppermute x1, starting transfers between devices, per_device(): lax.ppermute(pair[:, :, quarter - EDGE:, :], 'tp', [(i, i + 1) for i in r...  3.03 us
  transfers between devices with their start and end apart: 23, of which 17 were waited for; matrix products, arithmetic and copies ran while one was open for 1% of the time, Pallas kernels for 14%

profile of v3, /device:TPU:0, one launch (start us, length us, event | category | flops | bytes accessed | tf_op | source)
XLA Modules:
  0.0 129.9 jit_solution(9293343750203008909)
XLA Ops:
  2.6 4.1 %collective-permute-start.7 = (bf16[1,64,768]{2,1,0:T(8,128)(2,1)S(1)}, bf16[1,64,768]{2,1,0:T(8,128)(2,1)S(1)}, u32[]{:S(2)}, u32[]{:S(2)}) collective-permute-start(bf16[1,64,768]{2,1,0:T(8,128)(2,1)S(1)} %add_bitcast_fusion), channel_id=1, source_target_pairs={{0,16},{1,9},{2,18},{3,11},{4,20},{5,13},{6,22},{7,15},{8,24},{9,1... | collective-permute-start | bytes 294920 | tf_op jit(solution)/shard_map/ppermute | solution.py:559
  6.8 2.6 %collective-permute-done.7 = bf16[1,64,768]{2,1,0:T(8,128)(2,1)S(1)} collective-permute-done((bf16[1,64,768]{2,1,0:T(8,128)(2,1)S(1)}, bf16[1,64,768]{2,1,0:T(8,128)(2,1)S(1)}, u32[]{:S(2)}, u32[]{:S(2)}) %collective-permute-start.7) | collective-permute-done | bytes 98336 | tf_op jit(solution)/shard_map/ppermute | solution.py:559
  9.4 2.1 %collective-permute-start.8 = (bf16[2,64,768]{2,1,0:T(8,128)(2,1)S(1)}, bf16[2,64,768]{2,1,0:T(8,128)(2,1)S(1)}, u32[]{:S(2)}, u32[]{:S(2)}) collective-permute-start(bf16[2,64,768]{2,1,0:T(8,128)(2,1)S(1)} %pad_maximum_fusion.2), channel_id=1, source_target_pairs={{0,8},{1,17},{2,10},{3,19},{4,12},{5,21},{6,14},{7,23},{8,0},{9,25... | collective-permute-start | bytes 589832 | tf_op jit(solution)/shard_map/ppermute | solution.py:559
  11.5 4.6 %collective-permute-done.8 = bf16[2,64,768]{2,1,0:T(8,128)(2,1)S(1)} collective-permute-done((bf16[2,64,768]{2,1,0:T(8,128)(2,1)S(1)}, bf16[2,64,768]{2,1,0:T(8,128)(2,1)S(1)}, u32[]{:S(2)}, u32[]{:S(2)}) %collective-permute-start.8) | collective-permute-done | bytes 196640 | tf_op jit(solution)/shard_map/ppermute | solution.py:559
  16.2 1.9 %collective-permute-start.9 = (bf16[4,64,768]{2,1,0:T(8,128)(2,1)S(1)}, bf16[4,64,768]{2,1,0:T(8,128)(2,1)S(1)}, u32[]{:S(2)}, u32[]{:S(2)}) collective-permute-start(bf16[4,64,768]{2,1,0:T(8,128)(2,1)S(1)} %pad_maximum_fusion.1), channel_id=1, source_target_pairs={{0,4},{1,3},{2,6},{3,1},{4,0},{5,7},{6,2},{7,5},{8,12},{9,11},{10,... | collective-permute-start | bytes 1179656 | tf_op jit(solution)/shard_map/ppermute | solution.py:559
  18.1 5.9 %collective-permute-done.9 = bf16[4,64,768]{2,1,0:T(8,128)(2,1)S(1)} collective-permute-done((bf16[4,64,768]{2,1,0:T(8,128)(2,1)S(1)}, bf16[4,64,768]{2,1,0:T(8,128)(2,1)S(1)}, u32[]{:S(2)}, u32[]{:S(2)}) %collective-permute-start.9) | collective-permute-done | bytes 393248 | tf_op jit(solution)/shard_map/ppermute | solution.py:559
  24.1 1.9 %collective-permute-start.10 = (bf16[8,64,768]{2,1,0:T(8,128)(2,1)S(1)}, bf16[8,64,768]{2,1,0:T(8,128)(2,1)S(1)}, u32[]{:S(2)}, u32[]{:S(2)}) collective-permute-start(bf16[8,64,768]{2,1,0:T(8,128)(2,1)S(1)} %pad_maximum_fusion.refs_0_), channel_id=1, source_target_pairs={{0,2},{1,5},{2,0},{3,7},{4,6},{5,1},{6,4},{7,3},{8,10},{9,13},{10,... | collective-permute-start | bytes 2359304 | tf_op jit(solution)/shard_map/ppermute | solution.py:559
  26.0 10.1 %collective-permute-done.10.refs_1_ = bf16[8,64,768]{2,1,0:T(8,128)(2,1)S(1)} collective-permute-done((bf16[8,64,768]{2,1,0:T(8,128)(2,1)S(1)}, bf16[8,64,768]{2,1,0:T(8,128)(2,1)S(1)}, u32[]{:S(2)}, u32[]{:S(2)}) %collective-permute-start.10) | collective-permute-done | bytes 786464 | tf_op jit(solution)/shard_map/ppermute | solution.py:559
  38.9 1.9 %collective-permute-start.1 = (f32[16,512]{1,0:T(8,128)S(1)}, f32[16,512]{1,0:T(8,128)S(1)}, u32[]{:S(2)}, u32[]{:S(2)}) collective-permute-start(f32[16,512]{1,0:T(8,128)S(1)} %add.91), channel_id=1, source_target_pairs={{0,4},{1,3},{2,6},{3,1},{4,0},{5,7},{6,2},{7,5},{8,12},{9,11},{10,... | collective-permute-start | bytes 98312 | tf_op jit(solution)/shard_map/ppermute | solution.py:559
  40.7 2.0 %collective-permute-done.1 = f32[16,512]{1,0:T(8,128)S(1)} collective-permute-done((f32[16,512]{1,0:T(8,128)S(1)}, f32[16,512]{1,0:T(8,128)S(1)}, u32[]{:S(2)}, u32[]{:S(2)}) %collective-permute-start.1) | collective-permute-done | bytes 32800 | tf_op jit(solution)/shard_map/ppermute | solution.py:559
  42.8 1.8 %collective-permute-start.2 = (f32[16,512]{1,0:T(8,128)S(1)}, f32[16,512]{1,0:T(8,128)S(1)}, u32[]{:S(2)}, u32[]{:S(2)}) collective-permute-start(f32[16,512]{1,0:T(8,128)S(1)} %add.92), channel_id=1, source_target_pairs={{0,2},{1,5},{2,0},{3,7},{4,6},{5,1},{6,4},{7,3},{8,10},{9,13},{10,... | collective-permute-start | bytes 98312 | tf_op jit(solution)/shard_map/ppermute | solution.py:559
  44.6 2.1 %collective-permute-done.2 = f32[16,512]{1,0:T(8,128)S(1)} collective-permute-done((f32[16,512]{1,0:T(8,128)S(1)}, f32[16,512]{1,0:T(8,128)S(1)}, u32[]{:S(2)}, u32[]{:S(2)}) %collective-permute-start.2) | collective-permute-done | bytes 32800 | tf_op jit(solution)/shard_map/ppermute | solution.py:559
  47.8 1.3 collective-permute-start.6
  49.1 3.0 %collective-permute-start.5 = (bf16[3,2,8,512]{3,2,1,0:T(8,128)(2,1)S(1)}, bf16[3,2,8,512]{3,2,1,0:T(8,128)(2,1)S(1)}, u32[]{:S(2)}, u32[]{:S(2)}) collective-permute-start(bf16[3,2,8,512]{3,2,1,0:T(8,128)(2,1)S(1)} %get-tuple-element.149), channel_id=1, source_target_pairs={{0,1},{1,2},{2,3},{4,5},{5,6},{6,7},{8,9},{9,10},{10,11},{12,13},{... | collective-permute-start | bytes 147464 | tf_op jit(solution)/shard_map/ppermute | solution.py:584
  52.1 4.6 %collective-permute-start.4 = (f32[16,512]{1,0:T(8,128)S(1)}, f32[16,512]{1,0:T(8,128)S(1)}, u32[]{:S(2)}, u32[]{:S(2)}) collective-permute-start(f32[16,512]{1,0:T(8,128)S(1)} %add.94), channel_id=1, source_target_pairs={{0,16},{1,17},{2,18},{3,19},{4,20},{5,21},{6,22},{7,23},{8,24},{9,... | collective-permute-start | bytes 98312 | tf_op jit(solution)/shard_map/ppermute | solution.py:559
  56.8 1.8 %collective-permute-done.4 = f32[16,512]{1,0:T(8,128)S(1)} collective-permute-done((f32[16,512]{1,0:T(8,128)S(1)}, f32[16,512]{1,0:T(8,128)S(1)}, u32[]{:S(2)}, u32[]{:S(2)}) %collective-permute-start.4) | collective-permute-done | bytes 32800 | tf_op jit(solution)/shard_map/ppermute | solution.py:559
  58.6 4.9 %shard_map.581 = (bf16[816,512]{1,0:T(8,128)(2,1)S(1)}, f32[816,640]{1,0:T(8,128)S(1)}, bf16[816,512]{1,0:T(8,128)(2,1)S(1)}, bf16[512,768]{1,0:T(8,128)(2,1)S(1...) custom-call(s32[10]{0:T(128)S(1)} %stack.52.ints, bf16[3,256,512]{2,1,0:T(8,128)(2,1)S(1)} %copy-done, ...), custom_call_target="tpu_custom_call" | custom-call | flops 29245440 | bytes 3342336 | tf_op jit(solution)/shard_map/pallas_call | solution.py:625
  63.5 9.7 %shard_map.582 = (bf16[768,1536]{1,0:T(8,128)(2,1)S(1)}, bf16[816,1536]{1,0:T(8,128)(2,1)S(1)}, bf16[16,64,768]{2,1,0:T(8,128)(2,1)S(1)}, bf16[16,64,768]{2,1,0:...) custom-call(s32[10]{0:T(128)S(1)} %stack.52.ints, ...), custom_call_target="tpu_custom_call" | custom-call | flops 5133828096 | bytes 10027008 | tf_op jit(solution)/shard_map/pallas_call | solution.py:639
  74.2 3.0 %collective-permute-done.18 = bf16[16,64,768]{2,1,0:T(8,128)(2,1)S(1)} collective-permute-done((bf16[16,64,768]{2,1,0:T(8,128)(2,1)S(1)}, bf16[16,64,768]{2,1,0:T(8,128)(2,1)S(1)}, u32[]{:S(2)}, u32[]{:S(2)}) %collective-permute-start.18) | collective-permute-done | bytes 1572896 | tf_op jit(solution)/shard_map/ppermute | solution.py:559
  78.7 11.1 %collective-permute-done.19 = bf16[8,64,768]{2,1,0:T(8,128)(2,1)S(1)} collective-permute-done((bf16[8,64,768]{2,1,0:T(8,128)(2,1)S(1)}, bf16[8,64,768]{2,1,0:T(8,128)(2,1)S(1)}, u32[]{:S(2)}, u32[]{:S(2)}) %collective-permute-start.19) | collective-permute-done | bytes 786464 | tf_op jit(solution)/shard_map/ppermute | solution.py:559
  90.0 1.6 %collective-permute-start.20 = (bf16[4,64,768]{2,1,0:T(8,128)(2,1)S(1)}, bf16[4,64,768]{2,1,0:T(8,128)(2,1)S(1)}, u32[]{:S(2)}, u32[]{:S(2)}) collective-permute-start(bf16[4,64,768]{2,1,0:T(8,128)(2,1)S(1)} %get-tuple-element.147), channel_id=1, source_target_pairs={{0,4},{1,3},{2,6},{3,1},{4,0},{5,7},{6,2},{7,5},{8,12},{9,11},{10,... | collective-permute-start | bytes 1179656 | tf_op jit(solution)/shard_map/ppermute | solution.py:559
  91.6 4.0 %shard_map.583 = (f32[3,256,512]{2,1,0:T(8,128)}, f32[8,512]{1,0:T(8,128)S(1)}) custom-call(s32[10]{0:T(128)S(1)} %stack.52.ints, f32[16,512]{1,0:T(8,128)S(1)} %add.95.params, bf16[768,1536]{1,0:T(8,128)(2,1)S(1)} %get-tuple-element.95.act, bf16[512,1536]{1,0:T(8,128)(2,1)S(1)} %get-tuple-element.96.down, bf16[3,256,512]{2,1,0:T(8,128)(2,1)S(1)} %copy-done, ...), custom_call_target="tpu_custom_call" | custom-call | flops 1207959552 | bytes 3342336 | tf_op jit(solution)/shard_map/pallas_call | solution.py:650
  95.5 2.2 %collective-permute-done.20 = bf16[4,64,768]{2,1,0:T(8,128)(2,1)S(1)} collective-permute-done((bf16[4,64,768]{2,1,0:T(8,128)(2,1)S(1)}, bf16[4,64,768]{2,1,0:T(8,128)(2,1)S(1)}, u32[]{:S(2)}, u32[]{:S(2)}) %collective-permute-start.20) | collective-permute-done | bytes 393248 | tf_op jit(solution)/shard_map/ppermute | solution.py:559
  98.7 8.2 %shard_map.584 = (f32[3,256,512]{2,1,0:T(8,128)}, f32[16,512]{1,0:T(8,128)S(1)}) custom-call(s32[10]{0:T(128)S(1)} %stack.52.ints, f32[16,512]{1,0:T(8,128)S(1)} %add.95.params, bf16[3,2,8,512]{3,2,1,0:T(8,128)(2,1)S(1)} %collective-permute-done.5.left, bf16[3,2,8,512]{3,2,1,0:T(8,128)(2,1)S(1)} %collective-permute-done.6.right, ...), custom_call_target="tpu_custom_call" | custom-call | flops 1283457024 | bytes 3342336 | tf_op jit(solution)/shard_map/pallas_call | solution.py:665
  108.1 3.3 %collective-permute-start.14 = (f32[16,512]{1,0:T(8,128)S(1)}, f32[16,512]{1,0:T(8,128)S(1)}, u32[]{:S(2)}, u32[]{:S(2)}) collective-permute-start(f32[16,512]{1,0:T(8,128)S(1)} %add.97), channel_id=1, source_target_pairs={{0,16},{1,17},{2,18},{3,19},{4,20},{5,21},{6,22},{7,23},{8,24},{9,... | collective-permute-start | bytes 98312 | tf_op jit(solution)/shard_map/ppermute | solution.py:559
  111.4 2.4 %collective-permute-done.14 = f32[16,512]{1,0:T(8,128)S(1)} collective-permute-done((f32[16,512]{1,0:T(8,128)S(1)}, f32[16,512]{1,0:T(8,128)S(1)}, u32[]{:S(2)}, u32[]{:S(2)}) %collective-permute-start.14) | collective-permute-done | bytes 32800 | tf_op jit(solution)/shard_map/ppermute | solution.py:559
  114.9 2.8 %collective-permute-done.15 = f32[16,512]{1,0:T(8,128)S(1)} collective-permute-done((f32[16,512]{1,0:T(8,128)S(1)}, f32[16,512]{1,0:T(8,128)S(1)}, u32[]{:S(2)}, u32[]{:S(2)}) %collective-permute-start.15) | collective-permute-done | bytes 32800 | tf_op jit(solution)/shard_map/ppermute | solution.py:559
  117.8 1.5 %collective-permute-start.16 = (f32[16,512]{1,0:T(8,128)S(1)}, f32[16,512]{1,0:T(8,128)S(1)}, u32[]{:S(2)}, u32[]{:S(2)}) collective-permute-start(f32[16,512]{1,0:T(8,128)S(1)} %add.99), channel_id=1, source_target_pairs={{0,4},{1,3},{2,6},{3,1},{4,0},{5,7},{6,2},{7,5},{8,12},{9,11},{10,... | collective-permute-start | bytes 98312 | tf_op jit(solution)/shard_map/ppermute | solution.py:559
  119.3 2.4 %collective-permute-done.16 = f32[16,512]{1,0:T(8,128)S(1)} collective-permute-done((f32[16,512]{1,0:T(8,128)S(1)}, f32[16,512]{1,0:T(8,128)S(1)}, u32[]{:S(2)}, u32[]{:S(2)}) %collective-permute-start.16) | collective-permute-done | bytes 32800 | tf_op jit(solution)/shard_map/ppermute | solution.py:559
  122.3 2.9 %collective-permute-start.22 = (bf16[1,64,768]{2,1,0:T(8,128)(2,1)S(1)}, bf16[1,64,768]{2,1,0:T(8,128)(2,1)S(1)}, u32[]{:S(2)}, u32[]{:S(2)}) collective-permute-start(bf16[1,64,768]{2,1,0:T(8,128)(2,1)S(1)} %get-tuple-element.152), channel_id=1, source_target_pairs={{0,16},{1,9},{2,18},{3,11},{4,20},{5,13},{6,22},{7,15},{8,24},{9,1... | collective-permute-start | bytes 294920 | tf_op jit(solution)/shard_map/ppermute | solution.py:559
  125.7 1.4 %shard_map.585 = (f32[7,16]{1,0:T(8,128)}, f32[7,16]{1,0:T(8,128)}, f32[7,16]{1,0:T(8,128)}, f32[7,16]{1,0:T(8,128)}, f32[1,16]{1,0:T(1,128)}, /*index=5*/f32[1,...) custom-call(s32[3]{0:T(128)S(1)} %pad_add_fusion.ints, ...), custom_call_target="tpu_custom_call" | custom-call | tf_op jit(solution)/shard_map/pallas_call | solution.py:715
  127.1 1.8 %collective-permute-done.22.arrived = bf16[1,64,768]{2,1,0:T(8,128)(2,1)S(1)} collective-permute-done((bf16[1,64,768]{2,1,0:T(8,128)(2,1)S(1)}, bf16[1,64,768]{2,1,0:T(8,128)(2,1)S(1)}, u32[]{:S(2)}, u32[]{:S(2)}) %collective-permute-start.22) | collective-permute-done | bytes 98336 | tf_op jit(solution)/shard_map/ppermute | solution.py:559
  (107 shorter events, 13.6 us)
Async XLA Ops:
  1.6 34.6 %copy-start.8 = (f32[16,7]{0,1:T(8,128)S(1)}, f32[16,7]{0,1:T(8,128)}, u32[]{:S(2)}) copy-start(f32[16,7]{0,1:T(8,128)} %param.33) | copy-start | bytes 1348
  1.6 34.6 %copy-start.12 = (f32[16]{0:T(128)S(1)}, f32[16]{0:T(128)}, u32[]{:S(2)}) copy-start(f32[16]{0:T(128)} %param.34) | copy-start | bytes 196
  1.6 34.6 %copy-start.13 = (f32[16]{0:T(128)S(1)}, f32[16]{0:T(128)}, u32[]{:S(2)}) copy-start(f32[16]{0:T(128)} %param.35) | copy-start | bytes 196
  1.6 34.6 %copy-start.14 = (f32[16]{0:T(128)S(1)}, f32[16]{0:T(128)}, u32[]{:S(2)}) copy-start(f32[16]{0:T(128)} %param.36) | copy-start | bytes 196
  1.6 34.6 %copy-start.15 = (f32[16]{0:T(128)S(1)}, f32[16]{0:T(128)}, u32[]{:S(2)}) copy-start(f32[16]{0:T(128)} %param.40) | copy-start | bytes 196
  1.6 34.6 %copy-start.16 = (f32[16]{0:T(128)S(1)}, f32[16]{0:T(128)}, u32[]{:S(2)}) copy-start(f32[16]{0:T(128)} %param.41) | copy-start | bytes 196
  2.6 45.2 %copy-start = (bf16[3,256,512]{2,1,0:T(8,128)(2,1)S(1)}, bf16[3,256,512]{2,1,0:T(8,128)(2,1)}, u32[]{:S(2)}) copy-start(bf16[3,256,512]{2,1,0:T(8,128)(2,1)} %frames.5) | copy-start | bytes 2359300
  2.6 45.2 %copy-start.1 = (bf16[3,256,512]{2,1,0:T(8,128)(2,1)S(1)}, bf16[3,256,512]{2,1,0:T(8,128)(2,1)}, u32[]{:S(2)}) copy-start(bf16[3,256,512]{2,1,0:T(8,128)(2,1)} %cot.5) | copy-start | bytes 2359300
  2.6 6.7 %collective-permute-start.7 = (bf16[1,64,768]{2,1,0:T(8,128)(2,1)S(1)}, bf16[1,64,768]{2,1,0:T(8,128)(2,1)S(1)}, u32[]{:S(2)}, u32[]{:S(2)}) collective-permute-start(bf16[1,64,768]{2,1,0:T(8,128)(2,1)S(1)} %add_bitcast_fusion), channel_id=1, source_target_pairs={{0,16},{1,9},{2,18},{3,11},{4,20},{5,13},{6,22},{7,15},{8,24},{9,1... | collective-permute-start | bytes 294920 | tf_op jit(solution)/shard_map/ppermute | solution.py:559
  9.4 6.7 %collective-permute-start.8 = (bf16[2,64,768]{2,1,0:T(8,128)(2,1)S(1)}, bf16[2,64,768]{2,1,0:T(8,128)(2,1)S(1)}, u32[]{:S(2)}, u32[]{:S(2)}) collective-permute-start(bf16[2,64,768]{2,1,0:T(8,128)(2,1)S(1)} %pad_maximum_fusion.2), channel_id=1, source_target_pairs={{0,8},{1,17},{2,10},{3,19},{4,12},{5,21},{6,14},{7,23},{8,0},{9,25... | collective-permute-start | bytes 589832 | tf_op jit(solution)/shard_map/ppermute | solution.py:559
  16.2 40.6 %copy-start.29 = (s32[3]{0:T(128)S(1)}, s32[3]{0:T(128)}, u32[]{:S(2)}) copy-start(s32[3]{0:T(128)} %param.32) | copy-start | bytes 40
  16.2 7.8 %collective-permute-start.9 = (bf16[4,64,768]{2,1,0:T(8,128)(2,1)S(1)}, bf16[4,64,768]{2,1,0:T(8,128)(2,1)S(1)}, u32[]{:S(2)}, u32[]{:S(2)}) collective-permute-start(bf16[4,64,768]{2,1,0:T(8,128)(2,1)S(1)} %pad_maximum_fusion.1), channel_id=1, source_target_pairs={{0,4},{1,3},{2,6},{3,1},{4,0},{5,7},{6,2},{7,5},{8,12},{9,11},{10,... | collective-permute-start | bytes 1179656 | tf_op jit(solution)/shard_map/ppermute | solution.py:559
  24.1 12.1 %collective-permute-start.10 = (bf16[8,64,768]{2,1,0:T(8,128)(2,1)S(1)}, bf16[8,64,768]{2,1,0:T(8,128)(2,1)S(1)}, u32[]{:S(2)}, u32[]{:S(2)}) collective-permute-start(bf16[8,64,768]{2,1,0:T(8,128)(2,1)S(1)} %pad_maximum_fusion.refs_0_), channel_id=1, source_target_pairs={{0,2},{1,5},{2,0},{3,7},{4,6},{5,1},{6,4},{7,3},{8,10},{9,13},{10,... | collective-permute-start | bytes 2359304 | tf_op jit(solution)/shard_map/ppermute | solution.py:559
  26.0 37.5 %collective-permute-start.11 = (bf16[8,64,768]{2,1,0:T(8,128)(2,1)S(1)}, bf16[8,64,768]{2,1,0:T(8,128)(2,1)}, u32[]{:S(2)}, u32[]{:S(2)}) collective-permute-start(bf16[8,64,768]{2,1,0:T(8,128)(2,1)S(1)} %pad_maximum_fusion.refs_0_), channel_id=1, source_target_pairs={{0,1},{1,0},{2,3},{3,2},{4,5},{5,4},{6,7},{7,6},{8,9},{9,8},{10,11... | collective-permute-start | bytes 2359304 | tf_op jit(solution)/shard_map/ppermute | solution.py:559
  36.2 27.4 %collective-permute-start.12 = (bf16[8,64,768]{2,1,0:T(8,128)(2,1)S(1)}, bf16[8,64,768]{2,1,0:T(8,128)(2,1)}, u32[]{:S(2)}, u32[]{:S(2)}) collective-permute-start(bf16[8,64,768]{2,1,0:T(8,128)(2,1)S(1)} %collective-permute-done.10.refs_1_), channel_id=1, source_target_pairs={{0,1},{1,0},{2,3},{3,2},{4,5},{5,4},{6,7},{7,6},{8,9},{9,8},{10,11... | collective-permute-start | bytes 2359304 | tf_op jit(solution)/shard_map/ppermute | solution.py:559
  37.1 1.8 %collective-permute-start = (f32[16,512]{1,0:T(8,128)S(1)}, f32[16,512]{1,0:T(8,128)S(1)}, u32[]{:S(2)}, u32[]{:S(2)}) collective-permute-start(f32[16,512]{1,0:T(8,128)S(1)} %dynamic_update_slice.7), channel_id=1, source_target_pairs={{0,1},{1,0},{2,3},{3,2},{4,5},{5,4},{6,7},{7,6},{8,9},{9,8},{10,11... | collective-permute-start | bytes 98312 | tf_op jit(solution)/shard_map/ppermute | solution.py:559
  38.9 3.9 %collective-permute-start.1 = (f32[16,512]{1,0:T(8,128)S(1)}, f32[16,512]{1,0:T(8,128)S(1)}, u32[]{:S(2)}, u32[]{:S(2)}) collective-permute-start(f32[16,512]{1,0:T(8,128)S(1)} %add.91), channel_id=1, source_target_pairs={{0,4},{1,3},{2,6},{3,1},{4,0},{5,7},{6,2},{7,5},{8,12},{9,11},{10,... | collective-permute-start | bytes 98312 | tf_op jit(solution)/shard_map/ppermute | solution.py:559
  42.8 3.9 %collective-permute-start.2 = (f32[16,512]{1,0:T(8,128)S(1)}, f32[16,512]{1,0:T(8,128)S(1)}, u32[]{:S(2)}, u32[]{:S(2)}) collective-permute-start(f32[16,512]{1,0:T(8,128)S(1)} %add.92), channel_id=1, source_target_pairs={{0,2},{1,5},{2,0},{3,7},{4,6},{5,1},{6,4},{7,3},{8,10},{9,13},{10,... | collective-permute-start | bytes 98312 | tf_op jit(solution)/shard_map/ppermute | solution.py:559
  46.7 5.4 %collective-permute-start.3 = (f32[16,512]{1,0:T(8,128)S(1)}, f32[16,512]{1,0:T(8,128)S(1)}, u32[]{:S(2)}, u32[]{:S(2)}) collective-permute-start(f32[16,512]{1,0:T(8,128)S(1)} %add.93), channel_id=1, source_target_pairs={{0,8},{1,9},{2,10},{3,11},{4,12},{5,13},{6,14},{7,15},{8,0},{9,1},... | collective-permute-start | bytes 98312 | tf_op jit(solution)/shard_map/ppermute | solution.py:559
  47.8 10.8 %collective-permute-start.6 = (bf16[3,2,8,512]{3,2,1,0:T(8,128)(2,1)S(1)}, bf16[3,2,8,512]{3,2,1,0:T(8,128)(2,1)S(1)}, u32[]{:S(2)}, u32[]{:S(2)}) collective-permute-start(bf16[3,2,8,512]{3,2,1,0:T(8,128)(2,1)S(1)} %get-tuple-element.148), channel_id=1, source_target_pairs={{1,0},{2,1},{3,2},{5,4},{6,5},{7,6},{9,8},{10,9},{11,10},{13,12},{... | collective-permute-start | bytes 147464 | tf_op jit(solution)/shard_map/ppermute | solution.py:585
  49.1 9.5 %collective-permute-start.5 = (bf16[3,2,8,512]{3,2,1,0:T(8,128)(2,1)S(1)}, bf16[3,2,8,512]{3,2,1,0:T(8,128)(2,1)S(1)}, u32[]{:S(2)}, u32[]{:S(2)}) collective-permute-start(bf16[3,2,8,512]{3,2,1,0:T(8,128)(2,1)S(1)} %get-tuple-element.149), channel_id=1, source_target_pairs={{0,1},{1,2},{2,3},{4,5},{5,6},{6,7},{8,9},{9,10},{10,11},{12,13},{... | collective-permute-start | bytes 147464 | tf_op jit(solution)/shard_map/ppermute | solution.py:584
  52.1 6.5 %collective-permute-start.4 = (f32[16,512]{1,0:T(8,128)S(1)}, f32[16,512]{1,0:T(8,128)S(1)}, u32[]{:S(2)}, u32[]{:S(2)}) collective-permute-start(f32[16,512]{1,0:T(8,128)S(1)} %add.94), channel_id=1, source_target_pairs={{0,16},{1,17},{2,18},{3,19},{4,20},{5,21},{6,22},{7,23},{8,24},{9,... | collective-permute-start | bytes 98312 | tf_op jit(solution)/shard_map/ppermute | solution.py:559
  73.2 4.0 %collective-permute-start.18 = (bf16[16,64,768]{2,1,0:T(8,128)(2,1)S(1)}, bf16[16,64,768]{2,1,0:T(8,128)(2,1)S(1)}, u32[]{:S(2)}, u32[]{:S(2)}) collective-permute-start(bf16[16,64,768]{2,1,0:T(8,128)(2,1)S(1)} %get-tuple-element.123), channel_id=1, source_target_pairs={{0,1},{1,0},{2,3},{3,2},{4,5},{5,4},{6,7},{7,6},{8,9},{9,8},{10,11... | collective-permute-start | bytes 4718600 | tf_op jit(solution)/shard_map/ppermute | solution.py:559
  77.7 12.1 %collective-permute-start.19 = (bf16[8,64,768]{2,1,0:T(8,128)(2,1)S(1)}, bf16[8,64,768]{2,1,0:T(8,128)(2,1)S(1)}, u32[]{:S(2)}, u32[]{:S(2)}) collective-permute-start(bf16[8,64,768]{2,1,0:T(8,128)(2,1)S(1)} %get-tuple-element.145), channel_id=1, source_target_pairs={{0,2},{1,5},{2,0},{3,7},{4,6},{5,1},{6,4},{7,3},{8,10},{9,13},{10,... | collective-permute-start | bytes 2359304 | tf_op jit(solution)/shard_map/ppermute | solution.py:559
  90.0 7.8 %collective-permute-start.20 = (bf16[4,64,768]{2,1,0:T(8,128)(2,1)S(1)}, bf16[4,64,768]{2,1,0:T(8,128)(2,1)S(1)}, u32[]{:S(2)}, u32[]{:S(2)}) collective-permute-start(bf16[4,64,768]{2,1,0:T(8,128)(2,1)S(1)} %get-tuple-element.147), channel_id=1, source_target_pairs={{0,4},{1,3},{2,6},{3,1},{4,0},{5,7},{6,2},{7,5},{8,12},{9,11},{10,... | collective-permute-start | bytes 1179656 | tf_op jit(solution)/shard_map/ppermute | solution.py:559
  97.9 24.3 %collective-permute-start.21 = (bf16[2,64,768]{2,1,0:T(8,128)(2,1)S(1)}, bf16[2,64,768]{2,1,0:T(8,128)(2,1)S(1)}, u32[]{:S(2)}, u32[]{:S(2)}) collective-permute-start(bf16[2,64,768]{2,1,0:T(8,128)(2,1)S(1)} %get-tuple-element.151), channel_id=1, source_target_pairs={{0,8},{1,17},{2,10},{3,19},{4,12},{5,21},{6,14},{7,23},{8,0},{9,25... | collective-permute-start | bytes 589832 | tf_op jit(solution)/shard_map/ppermute | solution.py:559
  106.9 1.2 collective-permute-start.13
  108.1 5.8 %collective-permute-start.14 = (f32[16,512]{1,0:T(8,128)S(1)}, f32[16,512]{1,0:T(8,128)S(1)}, u32[]{:S(2)}, u32[]{:S(2)}) collective-permute-start(f32[16,512]{1,0:T(8,128)S(1)} %add.97), channel_id=1, source_target_pairs={{0,16},{1,17},{2,18},{3,19},{4,20},{5,21},{6,22},{7,23},{8,24},{9,... | collective-permute-start | bytes 98312 | tf_op jit(solution)/shard_map/ppermute | solution.py:559
  113.8 3.9 %collective-permute-start.15 = (f32[16,512]{1,0:T(8,128)S(1)}, f32[16,512]{1,0:T(8,128)S(1)}, u32[]{:S(2)}, u32[]{:S(2)}) collective-permute-start(f32[16,512]{1,0:T(8,128)S(1)} %add.98), channel_id=1, source_target_pairs={{0,2},{1,5},{2,0},{3,7},{4,6},{5,1},{6,4},{7,3},{8,10},{9,13},{10,... | collective-permute-start | bytes 98312 | tf_op jit(solution)/shard_map/ppermute | solution.py:559
  117.8 3.9 %collective-permute-start.16 = (f32[16,512]{1,0:T(8,128)S(1)}, f32[16,512]{1,0:T(8,128)S(1)}, u32[]{:S(2)}, u32[]{:S(2)}) collective-permute-start(f32[16,512]{1,0:T(8,128)S(1)} %add.99), channel_id=1, source_target_pairs={{0,4},{1,3},{2,6},{3,1},{4,0},{5,7},{6,2},{7,5},{8,12},{9,11},{10,... | collective-permute-start | bytes 98312 | tf_op jit(solution)/shard_map/ppermute | solution.py:559
  121.7 3.9 %collective-permute-start.17 = (f32[16,512]{1,0:T(8,128)S(1)}, f32[16,512]{1,0:T(8,128)S(1)}, u32[]{:S(2)}, u32[]{:S(2)}) collective-permute-start(f32[16,512]{1,0:T(8,128)S(1)} %add.100), channel_id=1, source_target_pairs={{0,8},{1,9},{2,10},{3,11},{4,12},{5,13},{6,14},{7,15},{8,0},{9,1},... | collective-permute-start | bytes 98312 | tf_op jit(solution)/shard_map/ppermute | solution.py:559
  122.3 6.6 %collective-permute-start.22 = (bf16[1,64,768]{2,1,0:T(8,128)(2,1)S(1)}, bf16[1,64,768]{2,1,0:T(8,128)(2,1)S(1)}, u32[]{:S(2)}, u32[]{:S(2)}) collective-permute-start(bf16[1,64,768]{2,1,0:T(8,128)(2,1)S(1)} %get-tuple-element.152), channel_id=1, source_target_pairs={{0,16},{1,9},{2,18},{3,11},{4,20},{5,13},{6,22},{7,15},{8,24},{9,1... | collective-permute-start | bytes 294920 | tf_op jit(solution)/shard_map/ppermute | solution.py:559
  (21 other events, 595.8 us)
